TPU v7x, 32 devices: a whole 2x2x4 slice. The times are simulated.
32 devices in a mesh: ens: 8 (over z, x), mesh: 4 (over y, core).
Axes of the slice: x: 2, y: 2, z: 4, core: 2. Of those that a mesh axis runs over, the one named last changes fastest.
Arguments:
- inputs: bfloat16 [8, 1024, 512], P('ens', 'mesh'), may hold values from -6 to 6
- cotangent: bfloat16 [8, 1024, 512], P('ens', 'mesh'), may hold values from -6 to 6
- noise_level: float32 [8], P('ens'), may hold values from 0.02 to 80
- neighbours: int32 [1024, 32], P('mesh'), may hold values from 0 to 1023, as said below
- live_slots: int32 [1024, 32], P('mesh'), may hold values from 0 to 1
- projections: bfloat16 [2, 4, 512, 512], replicated, may hold values from -4 to 4
- film_weights: float32 [2, 32, 1024], replicated, may hold values from -0.5 to 0.5
Outputs:
- grad_input: bfloat16 [8, 1024, 512], P('ens', 'mesh')
- grad_projections: float32 [2, 4, 512, 512], P(None, None, 'ens', 'mesh')
- grad_film: float32 [2, 32, 1024], P(None, None, 'mesh')
Inputs may be any that keep to these rules, and one draw needn't show every extreme that they name: `neighbours`: slot 0 of node i names i and is live. The live slots of a node name distinct nodes within 128 of it; every node at least 128 from both ends of the numbering has a live slot exactly 128 away. Padded slots name the node itself.
All inputs are finite; a program needn't handle non-finite values.
Results may differ from a plain program's by a relative error of at most 0.028.
Values may be sent and summed in bfloat16 or wider, within the bound.
No kernel may reach another device: no remote copies, remote signals or barrier semaphores. Data moves between devices by JAX's collectives and lax.ppermute only.
A program may use at most 64 MiB of HBM per device.

v0:
```python
import math

import jax
import jax.numpy as jnp
from jax import lax
from jax.sharding import PartitionSpec as P

HEADS = 4
NOISE_FREQ = 16
LAYERS = 2


epsilon = 1e-05


def padded(cells, sides, width):
    for axis, dim in sides:
        count = lax.axis_size(axis)
        ends = count - 1
        head = lax.slice_in_dim(cells, 0, width, axis=dim)
        tail = lax.slice_in_dim(cells, cells.shape[dim] - width, cells.shape[dim], axis=dim)
        cells = jnp.concatenate(
            [
                lax.ppermute(tail, axis, [(i, (i + 1) % count) for i in range(ends)]),
                cells,
                lax.ppermute(head, axis, [((i + 1) % count, i) for i in range(ends)]),
            ],
            axis=dim,
        )
    return cells


def from_behind(block, axis, distance):
    devices = range(lax.axis_size(axis))
    route = [(i - distance, i) for i in devices if i - distance in devices]
    return lax.ppermute(block, axis, route)


def noise_features(noise_level):
    frequency = jnp.arange(1, NOISE_FREQ + 1).astype(jnp.float32)
    angles = jnp.log(noise_level)[:, None] * frequency[None, :]
    return jnp.concatenate([jnp.sin(angles), jnp.cos(angles)], axis=1)


def project(left_side, right_side):
    return jnp.dot(left_side, right_side, preferred_element_type=jnp.float32)


def contract_rows(left_side, right_side):
    return lax.dot_general(
        left_side, right_side, (((0,), (0,)), ((), ())), preferred_element_type=jnp.float32
    )


def contract_cols(left_side, right_side):
    return lax.dot_general(
        left_side, right_side, (((1,), (1,)), ((), ())), preferred_element_type=jnp.float32
    )


def normalize(states, film_row, model_width):
    values = states.astype(jnp.float32)
    centre = jnp.mean(values, axis=1, keepdims=True)
    spread = jnp.mean(jnp.square(values - centre), axis=1, keepdims=True)
    inverse = lax.rsqrt(spread + epsilon)
    unit_rows = (values - centre) * inverse
    normed = (unit_rows * (1.0 + film_row[:model_width]) + film_row[model_width:]).astype(
        jnp.bfloat16
    )
    return (unit_rows, inverse, normed)


def dense_attention(query_head, key_head, present, head_size):
    scores = contract_cols(query_head, key_head) / math.sqrt(head_size)
    scores = jnp.where(present, scores, -jnp.inf)
    row_peak = jnp.max(scores, axis=1, keepdims=True)
    weights = jnp.where(present, jnp.exp(scores - row_peak), 0.0)
    return weights / jnp.sum(weights, axis=1, keepdims=True)


def extend_rims(normed, weights, rim_width, model_width):
    joined = jnp.concatenate(
        [
            project(normed, weights[1]).astype(jnp.bfloat16),
            project(normed, weights[2]).astype(jnp.bfloat16),
        ],
        axis=1,
    )
    joined_ext = padded(joined, (("mesh", 0),), rim_width)
    key_ext = joined_ext[:, :model_width]
    value_ext = joined_ext[:, model_width:]
    return (key_ext, value_ext)


def body(inputs, cotangent, noise_level, neighbours, live_slots, projections, film_weights):
    current = inputs[0]
    node_count, model_width = current.shape
    head_size = model_width // HEADS
    rim_width = node_count // 2
    window = node_count + 2 * rim_width
    offset = lax.axis_index("mesh") * node_count - rim_width
    columns = neighbours - offset
    row_ids = jnp.broadcast_to(jnp.arange(node_count, dtype=jnp.int32)[:, None], columns.shape)
    adjacency = (
        jnp.zeros((node_count, window), jnp.float32)
        .at[row_ids, columns]
        .add(live_slots.astype(jnp.float32))
    )
    present = adjacency > 0.5
    embedding = noise_features(noise_level)[0]
    film_rows = [
        jnp.dot(embedding[None, :], film_weights[layer_number], precision=lax.Precision.HIGHEST)[0]
        for layer_number in range(LAYERS)
    ]
    stored = []
    for layer_number in range(LAYERS):
        weights = projections[layer_number]
        unit_rows, inverse, normed = normalize(current, film_rows[layer_number], model_width)
        queries = project(normed, weights[0]).astype(jnp.bfloat16)
        key_ext, value_ext = extend_rims(normed, weights, rim_width, model_width)
        pieces = []
        for head_index in range(HEADS):
            head_cols = slice(head_index * head_size, (head_index + 1) * head_size)
            attention = dense_attention(
                queries[:, head_cols], key_ext[:, head_cols], present, head_size
            )
            pieces.append(project(attention.astype(jnp.bfloat16), value_ext[:, head_cols]))
        attended = jnp.concatenate(pieces, axis=1).astype(jnp.bfloat16)
        stored.append((unit_rows, inverse, normed, queries, key_ext, value_ext, attended))
        current = (current.astype(jnp.float32) + project(attended, weights[3])).astype(jnp.bfloat16)
    upstream = cotangent[0]
    weight_list = [None] * LAYERS
    film_list = [None] * LAYERS
    for layer_number in reversed(range(LAYERS)):
        weights = projections[layer_number]
        film_row = film_rows[layer_number]
        unit_rows, inverse, normed, queries, key_ext, value_ext, attended = stored[layer_number]
        grad_out = contract_rows(attended, upstream)
        grad_attended = contract_cols(upstream, weights[3]).astype(jnp.bfloat16)
        query_parts, key_parts, value_parts = ([], [], [])
        for head_index in range(HEADS):
            head_cols = slice(head_index * head_size, (head_index + 1) * head_size)
            attention = dense_attention(
                queries[:, head_cols], key_ext[:, head_cols], present, head_size
            )
            rounded = attention.astype(jnp.bfloat16)
            grad_head = grad_attended[:, head_cols]
            grad_probs = contract_cols(grad_head, value_ext[:, head_cols])
            grad_scores = (
                attention
                * (grad_probs - jnp.sum(attention * grad_probs, axis=1, keepdims=True))
                / math.sqrt(head_size)
            ).astype(jnp.bfloat16)
            query_parts.append(project(grad_scores, key_ext[:, head_cols]))
            key_parts.append(contract_rows(grad_scores, queries[:, head_cols]))
            value_parts.append(contract_rows(rounded, grad_head))
        grad_queries = jnp.concatenate(query_parts, axis=1).astype(jnp.bfloat16)
        rim_terms = jnp.concatenate(key_parts + value_parts, axis=1)
        from_above = from_behind(rim_terms[:rim_width].astype(jnp.bfloat16), "mesh", -1).astype(
            jnp.float32
        )
        from_below = from_behind(
            rim_terms[rim_width + node_count :].astype(jnp.bfloat16), "mesh", 1
        ).astype(jnp.float32)
        owned_rows = rim_terms[rim_width : rim_width + node_count]
        owned_rows = (
            owned_rows
            + jnp.pad(from_below, ((0, node_count - rim_width), (0, 0)))
            + jnp.pad(from_above, ((node_count - rim_width, 0), (0, 0)))
        )
        grad_keys = owned_rows[:, :model_width].astype(jnp.bfloat16)
        grad_values = owned_rows[:, model_width:].astype(jnp.bfloat16)
        weight_list[layer_number] = jnp.stack(
            [
                contract_rows(normed, grad_queries),
                contract_rows(normed, grad_keys),
                contract_rows(normed, grad_values),
                grad_out,
            ]
        )
        grad_normed = (
            contract_cols(grad_queries, weights[0])
            + contract_cols(grad_keys, weights[1])
            + contract_cols(grad_values, weights[2])
        )
        grad_conditioning = jnp.concatenate(
            [jnp.sum(grad_normed * unit_rows, axis=0), jnp.sum(grad_normed, axis=0)]
        )
        film_list[layer_number] = embedding[:, None] * grad_conditioning[None, :]
        grad_unit = grad_normed * (1.0 + film_row[:model_width])
        centred = (
            grad_unit
            - jnp.mean(grad_unit, axis=1, keepdims=True)
            - unit_rows * jnp.mean(grad_unit * unit_rows, axis=1, keepdims=True)
        )
        upstream = (upstream.astype(jnp.float32) + inverse * centred).astype(jnp.bfloat16)
    weight_grads = jnp.stack(weight_list)
    film_grads = jnp.stack(film_list)
    weight_part = lax.psum_scatter(
        weight_grads.astype(jnp.bfloat16), "ens", scatter_dimension=2, tiled=True
    )
    film_part = lax.psum(film_grads.astype(jnp.bfloat16), "ens")
    weight_out, film_out = (
        lax.psum_scatter(weight_part, "mesh", scatter_dimension=3, tiled=True).astype(jnp.float32),
        lax.psum_scatter(film_part, "mesh", scatter_dimension=2, tiled=True).astype(jnp.float32),
    )
    return (upstream[None], weight_out, film_out)


def solution(mesh):
    placed = (
        P("ens", "mesh", None),
        P("ens", "mesh", None),
        P("ens"),
        P("mesh", None),
        P("mesh", None),
        P(),
        P(),
    )
    return jax.shard_map(
        body,
        mesh=mesh,
        in_specs=placed,
        out_specs=(P("ens", "mesh", None), P(None, None, "ens", "mesh"), P(None, None, "mesh")),
        check_vma=False,
    )
```

profile of v0, /device:TPU:0, one launch (start us, length us, event | category | flops | bytes accessed | tf_op | source)
XLA Modules:
  0.0 294.2 jit_solution(6089208120001934512)
XLA Ops:
  8.0 1.1 convert_reduce_fusion
  9.1 1.2 fusion.37
  10.2 1.1 fusion.115
  11.5 1.6 convolution_convert_fusion.14
  13.1 1.4 convolution_convert_fusion.13
  14.5 2.4 collective-permute-start
  17.0 1.3 collective-permute-start.1
  19.1 56.7 %scatter_custom_fusion = f32[131072]{0:T(1024)S(1)} fusion(s32[8192]{0:T(1024)S(1)} %reshape.328, f32[8192]{0:T(1024)S(1)} %reshape.330, f32[]{:T(128)} %constant.46.clone.1), kind=kCustom, calls=%fused_computation.217 | custom fusion | flops 8192 | bytes 524292
  76.1 1.4 convolution_convert_fusion.15
  79.0 0.7 fusion.75
  83.4 5.1 %collective-permute-start.2 = (bf16[128,1024]{1,0:T(8,128)(2,1)S(1)}, bf16[128,1024]{1,0:T(8,128)(2,1)S(1)}, u32[]{:S(2)}, u32[]{:S(2)}) collective-permute-start(bf16[128,1024]{1,0:T(8,128)(2,1)S(1)} %get-tuple-element.31), channel_id=1, source_target_pairs={{0,1},{1,2},{2,3},{4,5},{5,6},{6,7},{8,9},{9,10},{10,11},{12,13},{... | collective-permute-start | bytes 786440 | tf_op jit(solution)/shard_map/ppermute | solution.py:24
  88.6 1.5 collective-permute-start.3
  90.7 2.5 collective-permute-done.3
  96.1 0.9 multiply_reduce_fusion.9
  101.5 6.7 %collective-permute-start.4 = (bf16[128,1024]{0,1:T(8,128)(2,1)S(1)}, bf16[128,1024]{0,1:T(8,128)(2,1)S(1)}, u32[]{:S(2)}, u32[]{:S(2)}) collective-permute-start(bf16[128,1024]{0,1:T(8,128)(2,1)S(1)} %get-tuple-element.29), channel_id=1, source_target_pairs={{0,1},{1,2},{2,3},{4,5},{5,6},{6,7},{8,9},{9,10},{10,11},{12,13},{... | collective-permute-start | bytes 786440 | tf_op jit(solution)/shard_map/ppermute | solution.py:36
  108.2 1.3 collective-permute-start.5
  110.5 1.1 collective-permute-done.5
  118.9 6.2 %collective-permute-start.6 = (bf16[128,1024]{0,1:T(8,128)(2,1)S(1)}, bf16[128,1024]{0,1:T(8,128)(2,1)S(1)}, u32[]{:S(2)}, u32[]{:S(2)}) collective-permute-start(bf16[128,1024]{0,1:T(8,128)(2,1)S(1)} %get-tuple-element.27), channel_id=1, source_target_pairs={{0,1},{1,2},{2,3},{4,5},{5,6},{6,7},{8,9},{9,10},{10,11},{12,13},{... | collective-permute-start | bytes 786440 | tf_op jit(solution)/shard_map/ppermute | solution.py:36
  125.1 1.5 collective-permute-start.7
  127.8 0.8 collective-permute-done.7
  130.0 2.3 pad_maximum_fusion
  132.4 1.4 fusion.56
  133.8 1.4 convolution_add_fusion.1
  135.2 1.6 fusion.36
  137.7 87.3 %reduce-scatter.6.cloned.1.call-done = bf16[2,4,64,512]{3,2,1,0:T(8,128)(2,1)} async-done(((bf16[2,4,512,512]{3,2,1,0:T(8,128)(2,1)}), bf16[2,4,64,512]{3,2,1,0:T(8,128)(2,1)}) %reduce-scatter.6.cloned.1.call-update) | async-done | bytes 524304 | tf_op jit(solution)/shard_map/reduce_scatter | solution.py:199
  224.9 1.6 copy.13
  226.6 1.4 reshape.338
  228.0 1.0 fusion.93
  229.0 18.3 %reduce-scatter.8.cloned.1.call-done = bf16[2,32,256]{2,1,0:T(8,128)(2,1)} async-done(((bf16[2,32,1024]{2,1,0:T(8,128)(2,1)}), bf16[2,32,256]{2,1,0:T(8,128)(2,1)}) %reduce-scatter.8.cloned.1.call-update) | async-done | bytes 32784 | tf_op jit(solution)/shard_map/reduce_scatter | solution.py:205
  247.3 37.8 %psum.8 = bf16[2,32,256]{2,1,0:T(8,128)(2,1)S(1)} all-reduce(bf16[2,32,256]{2,1,0:T(8,128)(2,1)} %reduce-scatter.8.cloned.1.call-done), channel_id=1, replica_groups=mesh['ens'=8,'mesh'=4] {'ens'}, use_global_device_ids=true, to_apply=%region_39.40 | all-reduce | flops 16384 | bytes 65536 | tf_op jit(solution)/shard_map/psum | solution.py:202
  285.7 1.1 reshape.339
  287.0 0.7 convert_element_type.206
  (148 shorter events, 26.5 us)
Async XLA Ops:
  7.2 5.9 %copy-start = (bf16[1,256,512]{2,1,0:T(8,128)(2,1)S(1)}, bf16[1,256,512]{2,1,0:T(8,128)(2,1)}, u32[]{:S(2)}) copy-start(bf16[1,256,512]{2,1,0:T(8,128)(2,1)} %param.7) | copy-start | bytes 786436
  7.2 217.8 %reduce-scatter.6.cloned.1.call-start = ((), (), s32[]{:S(2)}) async-start(), calls=%async_computation.3 | async-start | bytes 4718592 | tf_op jit(solution)/shard_map/reduce_scatter | solution.py:199
  11.4 6.8 %copy-start.2 = (f32[2,32,1024]{2,1,0:T(8,128)S(1)}, f32[2,32,1024]{2,1,0:T(8,128)}, u32[]{:S(2)}) copy-start(f32[2,32,1024]{2,1,0:T(8,128)} %param.13) | copy-start | bytes 786436
  11.4 7.1 %copy-start.4 = (s32[256,32]{0,1:T(8,128)S(1)}, s32[256,32]{0,1:T(8,128)}, u32[]{:S(2)}) copy-start(s32[256,32]{0,1:T(8,128)} %param.10) | copy-start | bytes 98308
  11.4 7.1 %copy-start.7 = (s32[2]{0:T(128)S(1)}, s32[2]{0:T(128)}, u32[]{:S(2)}) copy-start(s32[2]{0:T(128)} %constant.74) | copy-start | bytes 28
  11.4 7.2 %copy-start.6 = (s32[2]{0:T(128)S(1)}, s32[2]{0:T(128)}, u32[]{:S(2)}) copy-start(s32[2]{0:T(128)} %constant.71) | copy-start | bytes 28
  11.5 7.3 %copy-start.5 = (s32[256,32]{0,1:T(8,128)S(1)}, s32[256,32]{0,1:T(8,128)}, u32[]{:S(2)}) copy-start(s32[256,32]{0,1:T(8,128)} %param.11) | copy-start | bytes 98308
  14.5 63.0 %collective-permute-start = (bf16[128,1024]{1,0:T(8,128)(2,1)S(1)}, bf16[128,1024]{1,0:T(8,128)(2,1)S(1)}, u32[]{:S(2)}, u32[]{:S(2)}) collective-permute-start(bf16[128,1024]{1,0:T(8,128)(2,1)S(1)} %get-tuple-element.33), channel_id=1, source_target_pairs={{0,1},{1,2},{2,3},{4,5},{5,6},{6,7},{8,9},{9,10},{10,11},{12,13},{... | collective-permute-start | bytes 786440 | tf_op jit(solution)/shard_map/ppermute | solution.py:24
  17.0 60.6 %collective-permute-start.1 = (bf16[128,1024]{1,0:T(8,128)(2,1)S(1)}, bf16[128,1024]{1,0:T(8,128)(2,1)S(1)}, u32[]{:S(2)}, u32[]{:S(2)}) collective-permute-start(bf16[128,1024]{1,0:T(8,128)(2,1)S(1)} %get-tuple-element.34), channel_id=1, source_target_pairs={{1,0},{2,1},{3,2},{5,4},{6,5},{7,6},{9,8},{10,9},{11,10},{13,12},{... | collective-permute-start | bytes 786440 | tf_op jit(solution)/shard_map/ppermute | solution.py:26
  79.7 2.2 copy-start.1
  82.5 7.5 %copy-start.3 = (bf16[1,256,512]{2,1,0:T(8,128)(2,1)S(1)}, bf16[1,256,512]{2,1,0:T(8,128)(2,1)}, u32[]{:S(2)}) copy-start(bf16[1,256,512]{2,1,0:T(8,128)(2,1)} %param.8) | copy-start | bytes 786436
  83.4 7.3 %collective-permute-start.2 = (bf16[128,1024]{1,0:T(8,128)(2,1)S(1)}, bf16[128,1024]{1,0:T(8,128)(2,1)S(1)}, u32[]{:S(2)}, u32[]{:S(2)}) collective-permute-start(bf16[128,1024]{1,0:T(8,128)(2,1)S(1)} %get-tuple-element.31), channel_id=1, source_target_pairs={{0,1},{1,2},{2,3},{4,5},{5,6},{6,7},{8,9},{9,10},{10,11},{12,13},{... | collective-permute-start | bytes 786440 | tf_op jit(solution)/shard_map/ppermute | solution.py:24
  88.6 4.7 %collective-permute-start.3 = (bf16[128,1024]{1,0:T(8,128)(2,1)S(1)}, bf16[128,1024]{1,0:T(8,128)(2,1)S(1)}, u32[]{:S(2)}, u32[]{:S(2)}) collective-permute-start(bf16[128,1024]{1,0:T(8,128)(2,1)S(1)} %get-tuple-element.32), channel_id=1, source_target_pairs={{1,0},{2,1},{3,2},{5,4},{6,5},{7,6},{9,8},{10,9},{11,10},{13,12},{... | collective-permute-start | bytes 786440 | tf_op jit(solution)/shard_map/ppermute | solution.py:26
  101.5 9.0 %collective-permute-start.4 = (bf16[128,1024]{0,1:T(8,128)(2,1)S(1)}, bf16[128,1024]{0,1:T(8,128)(2,1)S(1)}, u32[]{:S(2)}, u32[]{:S(2)}) collective-permute-start(bf16[128,1024]{0,1:T(8,128)(2,1)S(1)} %get-tuple-element.29), channel_id=1, source_target_pairs={{0,1},{1,2},{2,3},{4,5},{5,6},{6,7},{8,9},{9,10},{10,11},{12,13},{... | collective-permute-start | bytes 786440 | tf_op jit(solution)/shard_map/ppermute | solution.py:36
  108.2 3.4 %collective-permute-start.5 = (bf16[128,1024]{0,1:T(8,128)(2,1)S(1)}, bf16[128,1024]{0,1:T(8,128)(2,1)S(1)}, u32[]{:S(2)}, u32[]{:S(2)}) collective-permute-start(bf16[128,1024]{0,1:T(8,128)(2,1)S(1)} %get-tuple-element.30), channel_id=1, source_target_pairs={{1,0},{2,1},{3,2},{5,4},{6,5},{7,6},{9,8},{10,9},{11,10},{13,12},{... | collective-permute-start | bytes 786440 | tf_op jit(solution)/shard_map/ppermute | solution.py:36
  118.9 8.8 %collective-permute-start.6 = (bf16[128,1024]{0,1:T(8,128)(2,1)S(1)}, bf16[128,1024]{0,1:T(8,128)(2,1)S(1)}, u32[]{:S(2)}, u32[]{:S(2)}) collective-permute-start(bf16[128,1024]{0,1:T(8,128)(2,1)S(1)} %get-tuple-element.27), channel_id=1, source_target_pairs={{0,1},{1,2},{2,3},{4,5},{5,6},{6,7},{8,9},{9,10},{10,11},{12,13},{... | collective-permute-start | bytes 786440 | tf_op jit(solution)/shard_map/ppermute | solution.py:36
  125.1 3.4 %collective-permute-start.7 = (bf16[128,1024]{0,1:T(8,128)(2,1)S(1)}, bf16[128,1024]{0,1:T(8,128)(2,1)S(1)}, u32[]{:S(2)}, u32[]{:S(2)}) collective-permute-start(bf16[128,1024]{0,1:T(8,128)(2,1)S(1)} %get-tuple-element.28), channel_id=1, source_target_pairs={{1,0},{2,1},{3,2},{5,4},{6,5},{7,6},{9,8},{10,9},{11,10},{13,12},{... | collective-permute-start | bytes 786440 | tf_op jit(solution)/shard_map/ppermute | solution.py:36
  132.3 115.0 %reduce-scatter.8.cloned.1.call-start = ((), (), s32[]{:S(2)}) async-start(), calls=%async_computation.4 | async-start | bytes 163840 | tf_op jit(solution)/shard_map/reduce_scatter | solution.py:205
  137.6 148.1 %reduce-scatter.10.cloned.1.call-start = ((), (), s32[]{:S(2)}) async-start(), calls=%async_computation.5 | async-start | bytes 655360
Sparse Core Ops, SparseCore 0:
  132.4 92.4 reduce-scatter.5
  227.9 19.2 reduce-scatter.7
  249.8 21.6 reduce-scatter.9
where the time goes:
time: 295 us; the launch traced here: 294 us
  waiting for transfers between devices  110 us (37%)
  other arithmetic  69.8 us (24%)
  blocking collectives  37.8 us (13%)
  matrix products  29.4 us (10%)
  starting transfers between devices  26.1 us (9%)
  between operations  15.4 us (5%)
  local copies, waits for them, and re-layouts  5.72 us (2%)
    reduce_scatter x1, waiting for transfers between devices, body(): lax.psum_scatter(weight_grads.astype(jnp.bfloat16), 'ens', scatter_dimens...  87.3 us
    unnamed x4, other arithmetic  56.9 us
    psum x1, blocking collectives, body(): film_part = lax.psum(film_grads.astype(jnp.bfloat16), 'ens')  37.8 us
    reduce_scatter x1, waiting for transfers between devices, body(): lax.psum_scatter(film_part, 'mesh', scatter_dimension=2, tiled=True)  18.3 us
    ppermute x4, starting transfers between devices, from_behind(): return lax.ppermute(block, axis, route)  15.7 us
    dot_general x24, matrix products, contract_cols(): lax.dot_general(left_side, right_side, (((1,), (1,)), ((), ())), preferre...  11.8 us
    dot_general x23, matrix products, project(): return jnp.dot(left_side, right_side, preferred_element_type=jnp.float32)  9.49 us
    ppermute x2, starting transfers between devices, padded(): lax.ppermute(tail, axis, [(i, (i + 1) % count) for i in range(ends)])  7.55 us
  transfers between devices with their start and end apart: 11, of which 5 were waited for; matrix products, arithmetic and copies ran while one was open for 24% of the time, Pallas kernels for 0%

commit v1 on v0

v1 whole, which is shorter than its diff:
```python
import math

import jax
import jax.numpy as jnp
from jax import lax
from jax.experimental import pallas as pl
from jax.experimental.pallas import tpu as pltpu
from jax.sharding import PartitionSpec as P

HEADS = 4
NOISE_FREQ = 16
LAYERS = 2
LANES = 128

epsilon = 1e-05
F32 = jnp.float32
BF16 = jnp.bfloat16
ABSENT = -1e30


def mm(left_side, right_side):
    return jnp.dot(left_side, right_side, preferred_element_type=F32)


def mm_rows(left_side, right_side):
    return lax.dot_general(
        left_side, right_side, (((0,), (0,)), ((), ())), preferred_element_type=F32
    )


def mm_cols(left_side, right_side):
    return lax.dot_general(
        left_side, right_side, (((1,), (1,)), ((), ())), preferred_element_type=F32
    )


def unit_of(states):
    values = states.astype(F32)
    centre = jnp.mean(values, axis=1, keepdims=True)
    centred = values - centre
    inverse = lax.rsqrt(jnp.mean(jnp.square(centred), axis=1, keepdims=True) + epsilon)
    return centred * inverse, inverse


def normed_of(states, film_ref, layer):
    width = states.shape[1]
    unit, _ = unit_of(states)
    scale = film_ref[layer : layer + 1, :width]
    shift = film_ref[layer : layer + 1, width:]
    return (unit * (1.0 + scale) + shift).astype(BF16)


def embedding_of(noise):
    row = lax.broadcasted_iota(jnp.int32, noise.shape, 0)
    wave = row - jnp.where(row >= NOISE_FREQ, NOISE_FREQ, 0) + 1
    angle = jnp.log(noise) * wave.astype(F32)
    return jnp.where(row < NOISE_FREQ, jnp.sin(angle), jnp.cos(angle))


def project_own(normed, w_ref, layer, q_ref, k_ref, v_ref):
    for slot, out_ref in enumerate((q_ref, k_ref, v_ref)):
        out_ref[...] = mm(normed, w_ref[layer, slot]).astype(BF16)


def start_kernel(
    x_ref, near_ref, live_ref, noise_ref, film_w_ref, w_ref,
    film_ref, bias_own_ref, bias_halo_ref, normed_ref, q_ref, k_ref, v_ref,
):
    node_count, slots = near_ref.shape
    rim = node_count // 2
    place = lax.axis_index("mesh")
    parity = lax.rem(place, 2)
    embedding = embedding_of(jnp.full((2 * NOISE_FREQ, 1), noise_ref[0], F32))
    for layer in range(LAYERS):
        film_ref[layer : layer + 1, :] = jnp.sum(
            embedding * film_w_ref[layer], axis=0, keepdims=True
        )
    normed = normed_of(x_ref[...], film_ref, 0)
    normed_ref[...] = normed
    project_own(normed, w_ref, 0, q_ref, k_ref, v_ref)
    column = lax.broadcasted_iota(jnp.int32, (1, node_count), 1)
    low, high = column - node_count, column + rim
    beside = jnp.where(column < rim, high + rim, low)
    behind = jnp.where(column < rim, column - rim, high)
    halo = jnp.where(parity == 0, beside, behind)
    halo = jnp.where(column < rim,
                     jnp.where(parity == 0, column + node_count, column - rim),
                     jnp.where(parity == 0, column - node_count, column + rim))
    step = 32

    def rows(index, carry):
        start = pl.multiple_of(index * step, step)
        near = near_ref[pl.ds(start, step), :] - place * node_count
        near = jnp.where(live_ref[pl.ds(start, step), :] > 0, near, -(1 << 24))
        for ids, out_ref in ((column, bias_own_ref), (halo, bias_halo_ref)):
            bias = jnp.full((step, node_count), ABSENT, F32)
            for slot in range(slots):
                bias = jnp.where(near[:, slot : slot + 1] == ids, 0.0, bias)
            out_ref[pl.ds(start, step), :] = bias
        return carry

    lax.fori_loop(0, node_count // step, rows, 0)


def own_kernel(x_ref, cot_ref, film_ref, w_ref, normed_ref, q_ref, k_ref, v_ref, ga_ref):
    normed = normed_of(x_ref[...], film_ref, 1)
    normed_ref[...] = normed
    project_own(normed, w_ref, 1, q_ref, k_ref, v_ref)
    ga_ref[...] = mm_cols(cot_ref[...], w_ref[1, 3]).astype(BF16)


def project_halo(pair_ref, other_ref, film_ref, w_ref, layer, normed_ref, k_ref, v_ref):
    rim = pair_ref.shape[0]
    normed_ref[:rim, :] = normed_of(pair_ref[...], film_ref, layer)
    normed_ref[rim:, :] = normed_of(other_ref[...], film_ref, layer)
    normed = normed_ref[...]
    k_ref[...] = mm(normed, w_ref[layer, 1]).astype(BF16)
    v_ref[...] = mm(normed, w_ref[layer, 2]).astype(BF16)


def softmax_blocks(query, keys, biases):
    factor = 1.0 / math.sqrt(query.shape[1])
    scores = [mm_cols(query, key) * factor + bias for key, bias in zip(keys, biases)]
    peak = jnp.max(jnp.maximum(*scores), axis=1, keepdims=True)
    weights = [jnp.exp(score - peak) for score in scores]
    total = jnp.sum(weights[0] + weights[1], axis=1, keepdims=True)
    share = 1.0 / total
    return [weight * share for weight in weights]


def heads_of(width):
    head = width // HEADS
    return [slice(index * head, (index + 1) * head) for index in range(HEADS)]


def forward_kernel(
    x_ref, pair_ref, other_ref, film_ref, q_ref, k_ref, v_ref, bias_own_ref, bias_halo_ref, w_ref,
    next_ref, to_pair_ref, to_other_ref, normed_h_ref, k_h_ref, v_h_ref, p_own_ref, p_halo_ref,
    attended_ref,
):
    rim = pair_ref.shape[0]
    parity = lax.rem(lax.axis_index("mesh"), 2)
    project_halo(pair_ref, other_ref, film_ref, w_ref, 0, normed_h_ref, k_h_ref, v_h_ref)
    for index, cols in enumerate(heads_of(x_ref.shape[1])):
        own, halo = softmax_blocks(
            q_ref[:, cols],
            (k_ref[:, cols], k_h_ref[:, cols]),
            (bias_own_ref[...], bias_halo_ref[...]),
        )
        own, halo = own.astype(BF16), halo.astype(BF16)
        p_own_ref[index] = own
        p_halo_ref[index] = halo
        attended_ref[:, cols] = (mm(own, v_ref[:, cols]) + mm(halo, v_h_ref[:, cols])).astype(BF16)
    next_ref[...] = (x_ref[...].astype(F32) + mm(attended_ref[...], w_ref[0, 3])).astype(BF16)
    to_pair_ref[...] = next_ref[pl.ds(pl.multiple_of((1 - parity) * rim, rim), rim), :]
    to_other_ref[...] = next_ref[pl.ds(pl.multiple_of(parity * rim, rim), rim), :]


def head_backward(
    cols, own, halo, own16, halo16, ga_ref, q_ref, k_ref, v_ref, k_h_ref, v_h_ref,
    gq_ref, gk_ref, gv_ref, gk_h_ref, gv_h_ref,
):
    grad = ga_ref[:, cols]
    query = q_ref[:, cols]
    factor = 1.0 / math.sqrt(query.shape[1])
    probs = mm_cols(grad, v_ref[:, cols])
    probs_h = mm_cols(grad, v_h_ref[:, cols])
    middle = jnp.sum(own * probs + halo * probs_h, axis=1, keepdims=True)
    scores = (own * (probs - middle) * factor).astype(BF16)
    scores_h = (halo * (probs_h - middle) * factor).astype(BF16)
    gq_ref[:, cols] = (mm(scores, k_ref[:, cols]) + mm(scores_h, k_h_ref[:, cols])).astype(BF16)
    gk_ref[:, cols] = mm_rows(scores, query).astype(BF16)
    gk_h_ref[:, cols] = mm_rows(scores_h, query).astype(BF16)
    gv_ref[:, cols] = mm_rows(own16, grad).astype(BF16)
    gv_h_ref[:, cols] = mm_rows(halo16, grad).astype(BF16)


def grads_out(
    layer, unit, pair_ref, other_ref, w_ref, gq_ref, gk_ref, gv_ref, gk_h_ref, gv_h_ref,
    gn_ref, to_pair_ref, to_other_ref, cond_ref,
):
    rim, width = pair_ref.shape
    grad_h = mm_cols(gk_h_ref[...], w_ref[layer, 1]) + mm_cols(gv_h_ref[...], w_ref[layer, 2])
    to_pair_ref[...] = grad_h[:rim].astype(BF16)
    to_other_ref[...] = grad_h[rim:].astype(BF16)
    grad = (
        mm_cols(gq_ref[...], w_ref[layer, 0])
        + mm_cols(gk_ref[...], w_ref[layer, 1])
        + mm_cols(gv_ref[...], w_ref[layer, 2])
    )
    gn_ref[...] = grad
    pair, _ = unit_of(pair_ref[...])
    other, _ = unit_of(other_ref[...])

    def over_nodes(term):
        return jnp.sum(term, axis=0, keepdims=True)

    cond_ref[:, :width] = (
        over_nodes(grad * unit) + over_nodes(grad_h[:rim] * pair) + over_nodes(grad_h[rim:] * other)
    )
    cond_ref[:, width:] = over_nodes(grad) + over_nodes(grad_h)


def last_layer_kernel(
    x_ref, pair_ref, other_ref, film_ref, q_ref, k_ref, v_ref, ga_ref, bias_own_ref, bias_halo_ref,
    w_ref,
    normed_h_ref, attended_ref, gq_ref, gk_ref, gv_ref, gk_h_ref, gv_h_ref,
    gn_ref, to_pair_ref, to_other_ref, cond_ref,
    k_h_ref, v_h_ref,
):
    project_halo(pair_ref, other_ref, film_ref, w_ref, 1, normed_h_ref, k_h_ref, v_h_ref)
    for cols in heads_of(x_ref.shape[1]):
        own, halo = softmax_blocks(
            q_ref[:, cols],
            (k_ref[:, cols], k_h_ref[:, cols]),
            (bias_own_ref[...], bias_halo_ref[...]),
        )
        own16, halo16 = own.astype(BF16), halo.astype(BF16)
        attended_ref[:, cols] = (mm(own16, v_ref[:, cols]) + mm(halo16, v_h_ref[:, cols])).astype(BF16)
        head_backward(
            cols, own, halo, own16, halo16, ga_ref, q_ref, k_ref, v_ref, k_h_ref, v_h_ref,
            gq_ref, gk_ref, gv_ref, gk_h_ref, gv_h_ref,
        )
    unit, _ = unit_of(x_ref[...])
    grads_out(
        1, unit, pair_ref, other_ref, w_ref, gq_ref, gk_ref, gv_ref, gk_h_ref, gv_h_ref,
        gn_ref, to_pair_ref, to_other_ref, cond_ref,
    )


def upstream_of(x, up, gn_ref, pair_ref, other_ref, film_ref, layer, total_ref):
    rim, width = pair_ref.shape
    parity = lax.rem(lax.axis_index("mesh"), 2)
    total_ref[...] = gn_ref[...]
    at_pair = pl.ds(pl.multiple_of((1 - parity) * rim, rim), rim)
    at_other = pl.ds(pl.multiple_of(parity * rim, rim), rim)
    total_ref[at_pair, :] += pair_ref[...].astype(F32)
    total_ref[at_other, :] += other_ref[...].astype(F32)
    unit, inverse = unit_of(x)
    grad = total_ref[...] * (1.0 + film_ref[layer : layer + 1, :width])
    centred = (
        grad
        - jnp.mean(grad, axis=1, keepdims=True)
        - unit * jnp.mean(grad * unit, axis=1, keepdims=True)
    )
    return (up.astype(F32) + inverse * centred).astype(BF16)


def first_layer_kernel(
    next_ref, cot_ref, gn2_ref, back_pair_ref, back_other_ref, film_ref,
    x_ref, pair_ref, other_ref, q_ref, k_ref, v_ref, k_h_ref, v_h_ref, p_own_ref, p_halo_ref, w_ref,
    up_ref, gq_ref, gk_ref, gv_ref, gk_h_ref, gv_h_ref, gn_ref, to_pair_ref, to_other_ref, cond_ref,
    total_ref, ga_ref,
):
    up = upstream_of(
        next_ref[...], cot_ref[...], gn2_ref, back_pair_ref, back_other_ref, film_ref, 1, total_ref
    )
    up_ref[...] = up
    ga_ref[...] = mm_cols(up, w_ref[0, 3]).astype(BF16)
    for index, cols in enumerate(heads_of(x_ref.shape[1])):
        own16, halo16 = p_own_ref[index], p_halo_ref[index]
        head_backward(
            cols, own16.astype(F32), halo16.astype(F32), own16, halo16,
            ga_ref, q_ref, k_ref, v_ref, k_h_ref, v_h_ref,
            gq_ref, gk_ref, gv_ref, gk_h_ref, gv_h_ref,
        )
    unit, _ = unit_of(x_ref[...])
    grads_out(
        0, unit, pair_ref, other_ref, w_ref, gq_ref, gk_ref, gv_ref, gk_h_ref, gv_h_ref,
        gn_ref, to_pair_ref, to_other_ref, cond_ref,
    )


def end_kernel(x_ref, up_ref, gn_ref, pair_ref, other_ref, film_ref, out_ref, total_ref):
    out_ref[...] = upstream_of(
        x_ref[...], up_ref[...], gn_ref, pair_ref, other_ref, film_ref, 0, total_ref
    )


def weight_products(
    normed_ref, normed_h_ref, attended_ref, up_ref, gq_ref, gk_ref, gv_ref, gk_h_ref, gv_h_ref, put
):
    put(0, mm_rows(normed_ref[...], gq_ref[...]))
    put(1, mm_rows(normed_ref[...], gk_ref[...]) + mm_rows(normed_h_ref[...], gk_h_ref[...]))
    put(2, mm_rows(normed_ref[...], gv_ref[...]) + mm_rows(normed_h_ref[...], gv_h_ref[...]))
    put(3, mm_rows(attended_ref[...], up_ref[...]))


def plain_weight_kernel(*refs):
    *ins, out_ref = refs

    def put(slot, value):
        out_ref[slot] = value

    weight_products(*ins, put)


def split_weight_kernel(*refs):
    *ins, send_ref, keep_ref, total_ref = refs

    def put(slot, value):
        total_ref[slot] = value

    weight_products(*ins, put)
    _, _, _, deep, _, _ = keep_ref.shape
    rows = keep_ref.shape[4] // 2
    ens, mesh = lax.axis_index("ens"), lax.axis_index("mesh")
    for slot in range(4):
        group, inner = slot // 2, slot % 2
        spot = slice(inner * rows, (inner + 1) * rows)
        for core in range(2):
            for y in range(2):
                col = lax.bitwise_xor(mesh, y * 2 + core)
                cols = pl.ds(pl.multiple_of(col * LANES, LANES), LANES)
                for x in range(2):
                    for z in range(deep):
                        row = lax.bitwise_xor(ens, z * 2 + x)
                        at = pl.ds(pl.multiple_of(row * rows, rows), rows)
                        piece = total_ref[slot, at, cols]
                        first, second = (y, x) if group == 0 else (x, y)
                        if core:
                            send_ref[group, first, second, z, spot, :] = piece.astype(BF16)
                        else:
                            keep_ref[group, first, second, z, spot, :] = piece


def film_kernel(rows_ref, noise_ref, out_ref):
    members = rows_ref.shape[0]
    for layer in range(LAYERS):
        total = jnp.zeros(out_ref.shape[1:], F32)
        for member in range(members):
            noise = jnp.full((2 * NOISE_FREQ, 1), noise_ref[member], F32)
            total += embedding_of(noise) * rows_ref[member, layer : layer + 1, :]
        out_ref[layer] = total


def whole():
    return pl.BlockSpec(memory_space=pltpu.VMEM)


def call(kernel, name, args, outs, scratch=(), flops=0, specs=None):
    moved = sum(a.size * a.dtype.itemsize for a in args)
    moved += sum(math.prod(shape) * jnp.dtype(kind).itemsize for shape, kind in outs)
    return pl.pallas_call(
        kernel,
        name=name,
        out_shape=[jax.ShapeDtypeStruct(shape, kind) for shape, kind in outs],
        in_specs=specs or [whole() for _ in args],
        out_specs=[whole() for _ in outs],
        scratch_shapes=[pltpu.VMEM(shape, kind) for shape, kind in scratch],
        cost_estimate=pl.CostEstimate(flops=flops, bytes_accessed=moved, transcendentals=0),
    )(*args)


def swap(block, axis, bit):
    count = lax.axis_size(axis)
    return lax.ppermute(block, axis, [(i, i ^ bit) for i in range(count)])


def exchange(to_pair, to_other):
    count = lax.axis_size("mesh")
    route = []
    for i in range(1, count - 1, 2):
        route += [(i, i + 1), (i + 1, i)]
    other = lax.ppermute(to_other, "mesh", route)
    return swap(to_pair, "mesh", 1), other


def scattered_core(send):
    return swap(send, "mesh", 1)


def scatter_first(keep, send):
    held = keep + swap(send, "mesh", 1).astype(F32)
    to_y, to_x = held[0, 1].astype(BF16), held[1, 1].astype(BF16)
    return (held[0, 0], held[1, 0]), (swap(to_y, "mesh", 2), swap(to_x, "ens", 1))


def scatter_second(kept, came):
    one = kept[0] + came[0].astype(F32)
    two = kept[1] + came[1].astype(F32)
    to_x, to_y = one[1].astype(BF16), two[1].astype(BF16)
    return (one[0], two[0]), (swap(to_x, "ens", 1), swap(to_y, "mesh", 2))


def scatter_third(kept, came):
    both = jnp.stack([kept[0] + came[0].astype(F32), kept[1] + came[1].astype(F32)])
    total = both[:, 0]
    came = [swap(both[:, z].astype(BF16), "ens", 2 * z) for z in range(1, both.shape[1])]
    for part in came:
        total = total + part.astype(F32)
    return total


def film_sum(conds, noise_level, mesh_count):
    mesh = lax.axis_index("mesh")
    rows = jnp.concatenate(conds, axis=0)
    width = rows.shape[1] // mesh_count
    pieces = rows.reshape(LAYERS, mesh_count, width).transpose(1, 0, 2)
    order = lax.bitwise_xor(jnp.arange(mesh_count), mesh)
    pieces = jnp.take(pieces, order, axis=0)
    bit = 1
    while bit < mesh_count:
        pieces = pieces.reshape(-1, 2, LAYERS, width)
        pieces = pieces[:, 0] + swap(pieces[:, 1], "mesh", bit)
        bit *= 2
    row = jnp.concatenate([pieces[0], jnp.full((1, width), noise_level[0])])[None]
    bit = 1
    while bit < lax.axis_size("ens"):
        row = jnp.concatenate([row, swap(row, "ens", bit)])
        bit *= 2
    noise = row[:, LAYERS, 0]
    return call(
        film_kernel, "film", (row, noise), [((LAYERS, 2 * NOISE_FREQ, width), F32)],
        specs=[whole(), pl.BlockSpec(memory_space=pltpu.SMEM)],
    )[0]


def body(inputs, cotangent, noise_level, neighbours, live_slots, projections, film_weights):
    states, cot = inputs[0], cotangent[0]
    nodes, width = states.shape
    rim = nodes // 2
    mesh_count, ens_count = lax.axis_size("mesh"), lax.axis_size("ens")
    parity = lax.rem(lax.axis_index("mesh"), 2)
    square = 2 * nodes * width * width
    mesh_split = width // mesh_count
    split = mesh_count == 4 and mesh_split % LANES == 0 and ens_count % 2 == 0

    def full(kind=BF16):
        return ((nodes, width), kind)

    rims = [((rim, width), BF16)] * 2
    cond_shape = ((1, 2 * width), F32)
    pair1, other1 = exchange(
        lax.dynamic_slice_in_dim(states, (1 - parity) * rim, rim),
        lax.dynamic_slice_in_dim(states, parity * rim, rim),
    )
    film, bias_own, bias_halo, normed1, q1, k1, v1 = call(
        start_kernel, "start",
        (states, neighbours, live_slots, noise_level, film_weights, projections),
        [((LAYERS, 2 * width), F32), ((nodes, nodes), F32), ((nodes, nodes), F32)] + [full()] * 4,
        flops=3 * square,
        specs=[whole()] * 3 + [pl.BlockSpec(memory_space=pltpu.SMEM)] + [whole()] * 2,
    )
    probs_shape = ((HEADS, nodes, nodes), BF16)
    states2, to_pair, to_other, normed1_h, k1_h, v1_h, p_own, p_halo, attended1 = call(
        forward_kernel, "forward",
        (states, pair1, other1, film, q1, k1, v1, bias_own, bias_halo, projections),
        [full()] + rims + [full()] * 3 + [probs_shape] * 2 + [full()],
        flops=5 * square,
    )
    pair2, other2 = exchange(to_pair, to_other)
    normed2, q2, k2, v2, ga2 = call(
        own_kernel, "own", (states2, cot, film, projections), [full()] * 5, flops=4 * square
    )
    grads = [full()] * 5 + [full(F32)] + rims + [cond_shape]
    normed2_h, attended2, gq2, gk2, gv2, gk2_h, gv2_h, gn2, to_pair, to_other, cond2 = call(
        last_layer_kernel, "last",
        (states2, pair2, other2, film, q2, k2, v2, ga2, bias_own, bias_halo, projections),
        [full()] * 2 + grads,
        scratch=[full()] * 2, flops=14 * square,
    )
    back_pair, back_other = exchange(to_pair, to_other)

    def weight_grads(name, *args):
        if not split:
            return call(
                plain_weight_kernel, name, args, [((4, width, width), F32)], flops=6 * square
            )[0]
        shape = (2, 2, 2, ens_count // 2, 2 * (width // ens_count), LANES)
        return call(
            split_weight_kernel, name, args, [(shape, BF16), (shape, F32)],
            scratch=[((4, width, width), F32)], flops=6 * square,
        )

    weights2 = weight_grads(
        "weights2", normed2, normed2_h, attended2, cot, gq2, gk2, gv2, gk2_h, gv2_h
    )
    up, gq1, gk1, gv1, gk1_h, gv1_h, gn1, to_pair, to_other, cond1 = call(
        first_layer_kernel, "first",
        (states2, cot, gn2, back_pair, back_other, film,
         states, pair1, other1, q1, k1, v1, k1_h, v1_h, p_own, p_halo, projections),
        [full()] + grads,
        scratch=[full(F32), full()], flops=11 * square,
    )
    back_pair, back_other = exchange(to_pair, to_other)
    weights1 = weight_grads(
        "weights1", normed1, normed1_h, attended1, up, gq1, gk1, gv1, gk1_h, gv1_h
    )
    grad_input = call(
        end_kernel, "end", (states, up, gn1, back_pair, back_other, film), [full()],
        scratch=[full(F32)],
    )[0]
    film_out = film_sum((cond1, cond2), noise_level, mesh_count)
    if split:
        outs = []
        for send, keep in (weights1, weights2):
            kept, came = scatter_first(keep, send)
            kept, came = scatter_second(kept, came)
            total = scatter_third(kept, came)
            outs.append(total.reshape(4, width // ens_count, LANES))
        weight_out = jnp.stack(outs)
    else:
        part = jnp.stack([weights1, weights2]).astype(BF16)
        part = lax.psum_scatter(part, "ens", scatter_dimension=2, tiled=True)
        weight_out = lax.psum_scatter(part, "mesh", scatter_dimension=3, tiled=True).astype(F32)
    return (grad_input[None], weight_out, film_out)


def solution(mesh):
    placed = (
        P("ens", "mesh", None),
        P("ens", "mesh", None),
        P("ens"),
        P("mesh", None),
        P("mesh", None),
        P(),
        P(),
    )
    return jax.shard_map(
        body,
        mesh=mesh,
        in_specs=placed,
        out_specs=(P("ens", "mesh", None), P(None, None, "ens", "mesh"), P(None, None, "mesh")),
        check_vma=False,
    )
```

time: 295 us -> 125 us (0.42)
  waiting for transfers between devices: 110 us -> 21.7 us
  other arithmetic: 69.8 us -> 4.08 us
  Pallas kernels: 0 us -> 47.3 us
  blocking collectives: 37.8 us -> 0 us
  matrix products: 29.4 us -> 0 us
  starting transfers between devices: 26.1 us -> 41.6 us
  between operations: 15.4 us -> 1.6 us
    reduce_scatter x2 -> x0, waiting for transfers between devices: 106 us -> none  [the longest x1 87.3 us: body(): lax.psum_scatter(weight_grads.astype(jnp.bfloat16), 'ens', scatter_dimens...]
    unnamed x4 -> x0, other arithmetic: 56.9 us -> none
    pallas_call x0 -> x9, Pallas kernels: none -> 47.3 us  [call(): pl.pallas_call(kernel, name=name, out_shape=[jax.ShapeDtypeStruct(shape,...]
    psum x1 -> x0, blocking collectives: 37.8 us -> none  [body(): film_part = lax.psum(film_grads.astype(jnp.bfloat16), 'ens')]
    dot_general x73 -> x0, matrix products: 29.4 us -> none  [the longest x24 11.8 us: contract_cols(): lax.dot_general(left_side, right_side, (((1,), (1,)), ((), ())), preferre...]
    ppermute x8 -> x29, waiting for transfers between devices: 4.42 us -> 21.7 us  [the longest x25 21.7 us: swap(): return lax.ppermute(block, axis, [(i, i ^ bit) for i in range(count)])]
    ppermute x8 -> x29, starting transfers between devices: 26 us -> 41.6 us  [the longest x25 38.8 us: swap(): return lax.ppermute(block, axis, [(i, i ^ bit) for i in range(count)])]
    reduce_sum x5 -> x0, other arithmetic: 3.88 us -> none  [the longest x2 1.44 us: dense_attention(): return weights / jnp.sum(weights, axis=1, keepdims=True)]
  transfers between devices with their start and end apart: 11 -> 29, of which waited for: 5 -> 12; matrix products, arithmetic and copies ran while one was open for 24% -> 5% of each run, Pallas kernels for 0% -> 19%
where the time goes in v1:
time: 125 us
  Pallas kernels  47.3 us (38%)
  starting transfers between devices  41.6 us (33%)
  waiting for transfers between devices  21.7 us (17%)
  local copies, waits for them, and re-layouts  8.27 us (7%)
  other arithmetic  4.08 us (3%)
  between operations  1.6 us (1%)
    pallas_call x9, Pallas kernels, call(): pl.pallas_call(kernel, name=name, out_shape=[jax.ShapeDtypeStruct(shape,...  47.3 us
    ppermute x25, starting transfers between devices, swap(): return lax.ppermute(block, axis, [(i, i ^ bit) for i in range(count)])  38.8 us
    ppermute x25, waiting for transfers between devices, swap(): return lax.ppermute(block, axis, [(i, i ^ bit) for i in range(count)])  21.7 us
    unnamed x26, local copies, waits for them, and re-layouts  5.84 us
    ppermute x4, starting transfers between devices, exchange(): other = lax.ppermute(to_other, 'mesh', route)  2.81 us
  transfers between devices with their start and end apart: 29, of which 12 were waited for; matrix products, arithmetic and copies ran while one was open for 5% of the time, Pallas kernels for 19%

profile of v1, /device:TPU:0, one launch (start us, length us, event | category | flops | bytes accessed | tf_op | source)
XLA Modules:
  0.0 124.6 jit_solution(15373330164353475506)
XLA Ops:
  6.5 6.2 %start.1 = (f32[2,1024]{1,0:T(2,128)}, f32[256,256]{1,0:T(8,128)}, f32[256,256]{1,0:T(8,128)}, bf16[256,512]{1,0:T(8,128)(2,1)}, bf16[256,512]{1,0:T(8,128)(2,1)...) custom-call(bf16[256,512]{1,0:T(8,128)(2,1)} %bitcast.143, s32[256,32]{1,0:T(8,128)} %copy.18.near_ref, ...), custom_call_target="tpu_custom_call" | custom-call | flops 402653184 | bytes 6365188 | tf_op jit(solution)/shard_map/start/pallas_call | solution.py:344
  13.4 6.4 %forward.1 = (bf16[256,512]{1,0:T(8,128)(2,1)}, bf16[128,512]{1,0:T(8,128)(2,1)}, bf16[128,512]{1,0:T(8,128)(2,1)}, bf16[256,512]{1,0:T(8,128)(2,1)}, bf16[256,5...) custom-call(bf16[256,512]{1,0:T(8,128)(2,1)} %bitcast.144, ...), custom_call_target="tpu_custom_call" | custom-call | flops 671088640 | bytes 8658944 | tf_op jit(solution)/shard_map/forward/pallas_call | solution.py:344
  19.8 3.9 %collective-permute-start.2 = (bf16[128,512]{1,0:T(8,128)(2,1)}, bf16[128,512]{1,0:T(8,128)(2,1)S(1)}, u32[]{:S(2)}, u32[]{:S(2)}) collective-permute-start(bf16[128,512]{1,0:T(8,128)(2,1)} %get-tuple-element.56), channel_id=1, source_target_pairs={{0,1},{1,0},{2,3},{3,2},{4,5},{5,4},{6,7},{7,6},{8,9},{9,8},{10,11... | collective-permute-start | bytes 393224 | tf_op jit(solution)/shard_map/ppermute | solution.py:357
  24.4 4.0 %own.1 = (bf16[256,512]{1,0:T(8,128)(2,1)}, bf16[256,512]{1,0:T(8,128)(2,1)}, bf16[256,512]{1,0:T(8,128)(2,1)}, bf16[256,512]{1,0:T(8,128)(2,1)}, bf16[256,512]{1,0:T(8,128)(2,1)}) custom-call(bf16[256,512]{1,0:T(8,128)(2,1)} %get-tuple-element.55.x_ref.next_ref, bf16[256,512]{1,0:T(8,128)(2,1)} %bitcast.147, f32[2,1024]{1,0:T(2,128)} %get-tuple-element.49.film_ref, ...), custom_call_target="tpu_custom_call" | custom-call | flops 536870912 | bytes 6037504 | tf_op jit(solution)/shard_map/own/pallas_call | solution.py:344
  29.2 8.9 %last.1 = (bf16[256,512]{1,0:T(8,128)(2,1)}, bf16[256,512]{1,0:T(8,128)(2,1)}, bf16[256,512]{1,0:T(8,128)(2,1)}, bf16[256,512]{1,0:T(8,128)(2,1)}, bf16[256,512]...) custom-call(bf16[256,512]{1,0:T(8,128)(2,1)} %get-tuple-element.55.x, ...), custom_call_target="tpu_custom_call" | custom-call | flops 1879048192 | bytes 8925184 | tf_op jit(solution)/shard_map/last/pallas_call | solution.py:344
  38.1 1.7 %collective-permute-start.4 = (bf16[128,512]{1,0:T(8,128)(2,1)}, bf16[128,512]{1,0:T(8,128)(2,1)S(1)}, u32[]{:S(2)}, u32[]{:S(2)}) collective-permute-start(bf16[128,512]{1,0:T(8,128)(2,1)} %get-tuple-element.63), channel_id=1, source_target_pairs={{0,1},{1,0},{2,3},{3,2},{4,5},{5,4},{6,7},{7,6},{8,9},{9,8},{10,11... | collective-permute-start | bytes 393224 | tf_op jit(solution)/shard_map/ppermute | solution.py:357
  41.7 8.0 %first.1 = (bf16[256,512]{1,0:T(8,128)(2,1)}, bf16[256,512]{1,0:T(8,128)(2,1)}, bf16[256,512]{1,0:T(8,128)(2,1)}, bf16[256,512]{1,0:T(8,128)(2,1)}, bf16[256,512...) custom-call(bf16[256,512]{1,0:T(8,128)(2,1)} %get-tuple-element.55.x, ...), custom_call_target="tpu_custom_call" | custom-call | flops 1476395008 | bytes 10760192 | tf_op jit(solution)/shard_map/first/pallas_call | solution.py:344
  51.0 5.3 %collective-permute-start.24 = (f32[2,2,256]{2,1,0:T(2,128)S(1)}, f32[2,2,256]{2,1,0:T(2,128)S(1)}, u32[]{:S(2)}, u32[]{:S(2)}) collective-permute-start(f32[2,2,256]{2,1,0:T(2,128)S(1)} %slice_bitcast_fusion.18), channel_id=1, source_target_pairs={{0,1},{1,0},{2,3},{3,2},{4,5},{5,4},{6,7},{7,6},{8,9},{9,8},{10,11... | collective-permute-start | bytes 12296 | tf_op jit(solution)/shard_map/ppermute | solution.py:357
  56.3 4.5 %weights2.1 = (bf16[2,2,2,4,128,128]{5,4,3,2,1,0:T(8,128)(2,1)}, f32[2,2,2,4,128,128]{5,4,3,2,1,0:T(8,128)}) custom-call(bf16[256,512]{1,0:T(8,128)(2,1)} %get-tuple-element.83.refs_0_, bf16[256,512]{1,0:T(8,128)(2,1)} %get-tuple-element.84.refs_1_, bf16[256,512]{1,0:T(8,128)(2,1)} %get-tuple-element.85.refs_2_, bf16[256,512]{1,0:T(8,128)(2,1)} %bitcast.149, ...), custom_call_target="tpu_custom_call" | custom-call | flops 805306368 | bytes 5505024 | tf_op jit(solution)/shard_map/weights2/pallas_call | solution.py:344
  60.9 1.7 %collective-permute-start.25 = (f32[1,2,256]{2,1,0:T(2,128)S(1)}, f32[1,2,256]{2,1,0:T(2,128)S(1)}, u32[]{:S(2)}, u32[]{:S(2)}) collective-permute-start(f32[1,2,256]{2,1,0:T(2,128)S(1)} %slice_bitcast_fusion.20), channel_id=1, source_target_pairs={{0,2},{1,3},{2,0},{3,1},{4,6},{5,7},{6,4},{7,5},{8,10},{9,11},{10,... | collective-permute-start | bytes 6152 | tf_op jit(solution)/shard_map/ppermute | solution.py:357
  62.6 1.9 %collective-permute-done.25 = f32[1,2,256]{2,1,0:T(2,128)S(1)} collective-permute-done((f32[1,2,256]{2,1,0:T(2,128)S(1)}, f32[1,2,256]{2,1,0:T(2,128)S(1)}, u32[]{:S(2)}, u32[]{:S(2)}) %collective-permute-start.25) | collective-permute-done | bytes 2080 | tf_op jit(solution)/shard_map/ppermute | solution.py:357
  64.5 1.7 %collective-permute-start.26 = (f32[1,3,256]{2,1,0:T(4,128)S(1)}, f32[1,3,256]{2,1,0:T(4,128)S(1)}, u32[]{:S(2)}, u32[]{:S(2)}) collective-permute-start(f32[1,3,256]{2,1,0:T(4,128)S(1)} %pad_bitcast_fusion), channel_id=1, source_target_pairs={{0,4},{4,0},{8,12},{12,8},{16,20},{20,16},{24,28},{28,24},{1,5},{5... | collective-permute-start | bytes 9224 | tf_op jit(solution)/shard_map/ppermute | solution.py:357
  66.2 4.7 %weights1.1 = (bf16[2,2,2,4,128,128]{5,4,3,2,1,0:T(8,128)(2,1)}, f32[2,2,2,4,128,128]{5,4,3,2,1,0:T(8,128)}) custom-call(bf16[256,512]{1,0:T(8,128)(2,1)} %get-tuple-element.73.refs_0_, bf16[256,512]{1,0:T(8,128)(2,1)} %get-tuple-element.74.refs_1_, bf16[256,512]{1,0:T(8,128)(2,1)} %get-tuple-element.75.refs_2_, ...), custom_call_target="tpu_custom_call" | custom-call | flops 805306368 | bytes 5505024 | tf_op jit(solution)/shard_map/weights1/pallas_call | solution.py:344
  71.0 1.6 %collective-permute-start.27 = (f32[2,3,256]{2,1,0:T(4,128)S(1)}, f32[2,3,256]{2,1,0:T(4,128)S(1)}, u32[]{:S(2)}, u32[]{:S(2)}) collective-permute-start(f32[2,3,256]{2,1,0:T(4,128)S(1)} %pad_maximum_fusion.6), channel_id=1, source_target_pairs={{0,8},{4,12},{8,0},{12,4},{16,24},{20,28},{24,16},{28,20},{1,9},{5... | collective-permute-start | bytes 18440 | tf_op jit(solution)/shard_map/ppermute | solution.py:357
  72.6 2.1 %collective-permute-done.27 = f32[2,3,256]{2,1,0:T(4,128)S(1)} collective-permute-done((f32[2,3,256]{2,1,0:T(4,128)S(1)}, f32[2,3,256]{2,1,0:T(4,128)S(1)}, u32[]{:S(2)}, u32[]{:S(2)}) %collective-permute-start.27) | collective-permute-done | bytes 6176 | tf_op jit(solution)/shard_map/ppermute | solution.py:357
  74.7 2.6 %collective-permute-start.28 = (f32[4,3,256]{2,1,0:T(4,128)S(1)}, f32[4,3,256]{2,1,0:T(4,128)S(1)}, u32[]{:S(2)}, u32[]{:S(2)}) collective-permute-start(f32[4,3,256]{2,1,0:T(4,128)S(1)} %pad_maximum_fusion.4), channel_id=1, source_target_pairs={{0,16},{4,20},{8,24},{12,28},{16,0},{20,4},{24,8},{28,12},{1,17},{... | collective-permute-start | bytes 36872 | tf_op jit(solution)/shard_map/ppermute | solution.py:357
  80.0 2.1 %film.1 = f32[2,32,256]{2,1,0:T(8,128)} custom-call(f32[8,3,256]{2,1,0:T(4,128)} %copy-done.4, f32[8]{0:T(128)} %slice_reduce_fusion.noise_ref), custom_call_target="tpu_custom_call" | custom-call | bytes 90144 | tf_op jit(solution)/shard_map/film/pallas_call | solution.py:344
  82.9 2.5 %end.1 = bf16[256,512]{1,0:T(8,128)(2,1)} custom-call(bf16[256,512]{1,0:T(8,128)(2,1)} %bitcast.146, bf16[256,512]{1,0:T(8,128)(2,1)} %get-tuple-element.69.up_ref.refs_3_, f32[256,512]{1,0:T(8,128)} %get-tuple-element.70.gn_ref, bf16[128,512]{1,0:T(8,128)(2,1)} %copy-done.7, bf16[128,512]{1,0:T(8,128)(2,1)} %copy-done.8, f32[2,1024]{1,0:T(2,128)} %get-tuple-element.49.film_ref), custom_call_target="tpu_custom_call" | custom-call | bytes 1581056 | tf_op jit(solution)/shard_map/end/pallas_call | solution.py:344
  86.3 3.2 %collective-permute-start.17 = (bf16[2,4,128,128]{3,2,1,0:T(8,128)(2,1)S(1)}, bf16[2,4,128,128]{3,2,1,0:T(8,128)(2,1)S(1)}, u32[]{:S(2)}, u32[]{:S(2)}) collective-permute-start(bf16[2,4,128,128]{3,2,1,0:T(8,128)(2,1)S(1)} %get-tuple-element.106), channel_id=1, source_target_pairs={{0,2},{1,3},{2,0},{3,1},{4,6},{5,7},{6,4},{7,5},{8,10},{9,11},{10,... | collective-permute-start | bytes 786440 | tf_op jit(solution)/shard_map/ppermute | solution.py:357
  89.5 1.7 %fusion.33 = (bf16[2,2,2,4,128,128]{5,4,3,2,1,0:T(8,128)(2,1)S(1)}, f32[2,2,2,4,128,128]{5,4,3,2,1,0:T(8,128)S(1)}) fusion(f32[2,2,2,4,128,128]{5,4,3,2,1,0:T(8,128)S(1)} %copy-done.1, bf16[2,2,2,4,128,128]{5,4,3,2,1,0:T(8,128)(2,1)} %collective-permute-done.8), kind=kLoop, calls=%fused_computation.82 | loop fusion | flops 1572864 | bytes 6291456 | tf_op jit(solution)/shard_map/convert.13
  91.2 1.6 %collective-permute-start.11 = (bf16[2,4,128,128]{3,2,1,0:T(8,128)(2,1)S(1)}, bf16[2,4,128,128]{3,2,1,0:T(8,128)(2,1)S(1)}, u32[]{:S(2)}, u32[]{:S(2)}) collective-permute-start(bf16[2,4,128,128]{3,2,1,0:T(8,128)(2,1)S(1)} %get-tuple-element.103), channel_id=1, source_target_pairs={{0,4},{4,0},{8,12},{12,8},{16,20},{20,16},{24,28},{28,24},{1,5},{5... | collective-permute-start | bytes 786440 | tf_op jit(solution)/shard_map/ppermute | solution.py:357
  94.0 2.7 %collective-permute-done.17 = bf16[2,4,128,128]{3,2,1,0:T(8,128)(2,1)S(1)} collective-permute-done((bf16[2,4,128,128]{3,2,1,0:T(8,128)(2,1)S(1)}, bf16[2,4,128,128]{3,2,1,0:T(8,128)(2,1)S(1)}, u32[]{:S(2)}, u32[]{:S(2)}) %collective-permute-start.17) | collective-permute-done | bytes 262176 | tf_op jit(solution)/shard_map/ppermute | solution.py:357
  96.8 1.6 %collective-permute-start.18 = (bf16[4,128,128]{2,1,0:T(8,128)(2,1)S(1)}, bf16[4,128,128]{2,1,0:T(8,128)(2,1)S(1)}, u32[]{:S(2)}, u32[]{:S(2)}) collective-permute-start(bf16[4,128,128]{2,1,0:T(8,128)(2,1)S(1)} %fusion.16), channel_id=1, source_target_pairs={{0,4},{4,0},{8,12},{12,8},{16,20},{20,16},{24,28},{28,24},{1,5},{5... | collective-permute-start | bytes 393224 | tf_op jit(solution)/shard_map/ppermute | solution.py:357
  98.4 2.1 %collective-permute-start.20 = (bf16[4,128,128]{2,1,0:T(8,128)(2,1)S(1)}, bf16[4,128,128]{2,1,0:T(8,128)(2,1)S(1)}, u32[]{:S(2)}, u32[]{:S(2)}) collective-permute-start(bf16[4,128,128]{2,1,0:T(8,128)(2,1)S(1)} %fusion.17), channel_id=1, source_target_pairs={{0,2},{1,3},{2,0},{3,1},{4,6},{5,7},{6,4},{7,5},{8,10},{9,11},{10,... | collective-permute-start | bytes 393224 | tf_op jit(solution)/shard_map/ppermute | solution.py:357
  100.5 2.8 %collective-permute-done.18 = bf16[4,128,128]{2,1,0:T(8,128)(2,1)S(1)} collective-permute-done((bf16[4,128,128]{2,1,0:T(8,128)(2,1)S(1)}, bf16[4,128,128]{2,1,0:T(8,128)(2,1)S(1)}, u32[]{:S(2)}, u32[]{:S(2)}) %collective-permute-start.18) | collective-permute-done | bytes 131104 | tf_op jit(solution)/shard_map/ppermute | solution.py:357
  103.3 1.5 %collective-permute-done.20 = bf16[4,128,128]{2,1,0:T(8,128)(2,1)S(1)} collective-permute-done((bf16[4,128,128]{2,1,0:T(8,128)(2,1)S(1)}, bf16[4,128,128]{2,1,0:T(8,128)(2,1)S(1)}, u32[]{:S(2)}, u32[]{:S(2)}) %collective-permute-start.20) | collective-permute-done | bytes 131104 | tf_op jit(solution)/shard_map/ppermute | solution.py:357
  106.4 1.7 %collective-permute-start.22 = (bf16[2,128,128]{2,1,0:T(8,128)(2,1)S(1)}, bf16[2,128,128]{2,1,0:T(8,128)(2,1)S(1)}, u32[]{:S(2)}, u32[]{:S(2)}) collective-permute-start(bf16[2,128,128]{2,1,0:T(8,128)(2,1)S(1)} %get-tuple-element.112), channel_id=1, source_target_pairs={{0,16},{4,20},{8,24},{12,28},{16,0},{20,4},{24,8},{28,12},{1,17},{... | collective-permute-start | bytes 196616 | tf_op jit(solution)/shard_map/ppermute | solution.py:357
  109.6 1.5 %collective-permute-start.10 = (bf16[4,128,128]{2,1,0:T(8,128)(2,1)S(1)}, bf16[4,128,128]{2,1,0:T(8,128)(2,1)S(1)}, u32[]{:S(2)}, u32[]{:S(2)}) collective-permute-start(bf16[4,128,128]{2,1,0:T(8,128)(2,1)S(1)} %fusion.14), channel_id=1, source_target_pairs={{0,4},{4,0},{8,12},{12,8},{16,20},{20,16},{24,28},{28,24},{1,5},{5... | collective-permute-start | bytes 393224 | tf_op jit(solution)/shard_map/ppermute | solution.py:357
  111.5 3.1 %collective-permute-done.10 = bf16[4,128,128]{2,1,0:T(8,128)(2,1)S(1)} collective-permute-done((bf16[4,128,128]{2,1,0:T(8,128)(2,1)S(1)}, bf16[4,128,128]{2,1,0:T(8,128)(2,1)S(1)}, u32[]{:S(2)}, u32[]{:S(2)}) %collective-permute-start.10) | collective-permute-done | bytes 131104 | tf_op jit(solution)/shard_map/ppermute | solution.py:357
  114.7 1.5 %collective-permute-done.12 = bf16[4,128,128]{2,1,0:T(8,128)(2,1)S(1)} collective-permute-done((bf16[4,128,128]{2,1,0:T(8,128)(2,1)S(1)}, bf16[4,128,128]{2,1,0:T(8,128)(2,1)S(1)}, u32[]{:S(2)}, u32[]{:S(2)}) %collective-permute-start.12) | collective-permute-done | bytes 131104 | tf_op jit(solution)/shard_map/ppermute | solution.py:357
  118.5 2.2 %collective-permute-start.13 = (bf16[2,128,128]{2,1,0:T(8,128)(2,1)S(1)}, bf16[2,128,128]{2,1,0:T(8,128)(2,1)S(1)}, u32[]{:S(2)}, u32[]{:S(2)}) collective-permute-start(bf16[2,128,128]{2,1,0:T(8,128)(2,1)S(1)} %get-tuple-element.107), channel_id=1, source_target_pairs={{0,8},{4,12},{8,0},{12,4},{16,24},{20,28},{24,16},{28,20},{1,9},{5... | collective-permute-start | bytes 196616 | tf_op jit(solution)/shard_map/ppermute | solution.py:357
  120.8 1.7 %collective-permute-done.15 = bf16[2,128,128]{2,1,0:T(8,128)(2,1)S(1)} collective-permute-done((bf16[2,128,128]{2,1,0:T(8,128)(2,1)S(1)}, bf16[2,128,128]{2,1,0:T(8,128)(2,1)S(1)}, u32[]{:S(2)}, u32[]{:S(2)}) %collective-permute-start.15) | collective-permute-done | bytes 65568 | tf_op jit(solution)/shard_map/ppermute | solution.py:357
  (98 shorter events, 24.2 us)
Async XLA Ops:
  1.6 11.1 %collective-permute-start = (bf16[128,512]{1,0:T(8,128)(2,1)S(1)}, bf16[128,512]{1,0:T(8,128)(2,1)S(1)}, u32[]{:S(2)}, u32[]{:S(2)}) collective-permute-start(bf16[128,512]{1,0:T(8,128)(2,1)S(1)} %get-tuple-element.114), channel_id=1, source_target_pairs={{0,1},{1,0},{2,3},{3,2},{4,5},{5,4},{6,7},{7,6},{8,9},{9,8},{10,11... | collective-permute-start | bytes 393224 | tf_op jit(solution)/shard_map/ppermute | solution.py:357
  2.2 10.5 %collective-permute-start.1 = (bf16[128,512]{1,0:T(8,128)(2,1)S(1)}, bf16[128,512]{1,0:T(8,128)(2,1)S(1)}, u32[]{:S(2)}, u32[]{:S(2)}) collective-permute-start(bf16[128,512]{1,0:T(8,128)(2,1)S(1)} %get-tuple-element.113), channel_id=1, source_target_pairs={{1,2},{2,1},{5,6},{6,5},{9,10},{10,9},{13,14},{14,13},{17,18},{18,... | collective-permute-start | bytes 393224 | tf_op jit(solution)/shard_map/ppermute | solution.py:365
  19.8 8.6 %collective-permute-start.2 = (bf16[128,512]{1,0:T(8,128)(2,1)}, bf16[128,512]{1,0:T(8,128)(2,1)S(1)}, u32[]{:S(2)}, u32[]{:S(2)}) collective-permute-start(bf16[128,512]{1,0:T(8,128)(2,1)} %get-tuple-element.56), channel_id=1, source_target_pairs={{0,1},{1,0},{2,3},{3,2},{4,5},{5,4},{6,7},{7,6},{8,9},{9,8},{10,11... | collective-permute-start | bytes 393224 | tf_op jit(solution)/shard_map/ppermute | solution.py:357
  23.8 4.7 %collective-permute-start.3 = (bf16[128,512]{1,0:T(8,128)(2,1)}, bf16[128,512]{1,0:T(8,128)(2,1)S(1)}, u32[]{:S(2)}, u32[]{:S(2)}) collective-permute-start(bf16[128,512]{1,0:T(8,128)(2,1)} %get-tuple-element.57), channel_id=1, source_target_pairs={{1,2},{2,1},{5,6},{6,5},{9,10},{10,9},{13,14},{14,13},{17,18},{18,... | collective-permute-start | bytes 393224 | tf_op jit(solution)/shard_map/ppermute | solution.py:365
  38.1 2.9 %collective-permute-start.4 = (bf16[128,512]{1,0:T(8,128)(2,1)}, bf16[128,512]{1,0:T(8,128)(2,1)S(1)}, u32[]{:S(2)}, u32[]{:S(2)}) collective-permute-start(bf16[128,512]{1,0:T(8,128)(2,1)} %get-tuple-element.63), channel_id=1, source_target_pairs={{0,1},{1,0},{2,3},{3,2},{4,5},{5,4},{6,7},{7,6},{8,9},{9,8},{10,11... | collective-permute-start | bytes 393224 | tf_op jit(solution)/shard_map/ppermute | solution.py:357
  39.8 1.2 collective-permute-start.5
  41.7 8.0 %copy-start.9 = (f32[1,1024]{1,0:T(1,128)S(1)}, f32[1,1024]{1,0:T(1,128)}, u32[]{:S(2)}) copy-start(f32[1,1024]{1,0:T(1,128)} %get-tuple-element.94) | copy-start | bytes 12292
  51.0 9.8 %collective-permute-start.24 = (f32[2,2,256]{2,1,0:T(2,128)S(1)}, f32[2,2,256]{2,1,0:T(2,128)S(1)}, u32[]{:S(2)}, u32[]{:S(2)}) collective-permute-start(f32[2,2,256]{2,1,0:T(2,128)S(1)} %slice_bitcast_fusion.18), channel_id=1, source_target_pairs={{0,1},{1,0},{2,3},{3,2},{4,5},{5,4},{6,7},{7,6},{8,9},{9,8},{10,11... | collective-permute-start | bytes 12296 | tf_op jit(solution)/shard_map/ppermute | solution.py:357
  60.8 24.5 %collective-permute-start.16 = (bf16[2,2,2,4,128,128]{5,4,3,2,1,0:T(8,128)(2,1)}, bf16[2,2,2,4,128,128]{5,4,3,2,1,0:T(8,128)(2,1)S(1)}, u32[]{:S(2)}, u32[]{:S(2)}) collective-permute-start(bf16[2,2,2,4,128,128]{5,4,3,2,1,0:T(8,128)(2,1)} %get-tuple-element.92), channel_id=1, source_target_pairs={{0,1},{1,0},{2,3},{3,2},{4,5},{5,4},{6,7},{7,6},{8,9},{9,8},{10,11... | collective-permute-start | bytes 3145736 | tf_op jit(solution)/shard_map/ppermute | solution.py:357
  60.9 3.7 %collective-permute-start.25 = (f32[1,2,256]{2,1,0:T(2,128)S(1)}, f32[1,2,256]{2,1,0:T(2,128)S(1)}, u32[]{:S(2)}, u32[]{:S(2)}) collective-permute-start(f32[1,2,256]{2,1,0:T(2,128)S(1)} %slice_bitcast_fusion.20), channel_id=1, source_target_pairs={{0,2},{1,3},{2,0},{3,1},{4,6},{5,7},{6,4},{7,5},{8,10},{9,11},{10,... | collective-permute-start | bytes 6152 | tf_op jit(solution)/shard_map/ppermute | solution.py:357
  64.5 6.4 %collective-permute-start.26 = (f32[1,3,256]{2,1,0:T(4,128)S(1)}, f32[1,3,256]{2,1,0:T(4,128)S(1)}, u32[]{:S(2)}, u32[]{:S(2)}) collective-permute-start(f32[1,3,256]{2,1,0:T(4,128)S(1)} %pad_bitcast_fusion), channel_id=1, source_target_pairs={{0,4},{4,0},{8,12},{12,8},{16,20},{20,16},{24,28},{28,24},{1,5},{5... | collective-permute-start | bytes 9224 | tf_op jit(solution)/shard_map/ppermute | solution.py:357
  66.2 19.1 %copy-start = (f32[2,2,2,4,128,128]{5,4,3,2,1,0:T(8,128)S(1)}, f32[2,2,2,4,128,128]{5,4,3,2,1,0:T(8,128)}, u32[]{:S(2)}) copy-start(f32[2,2,2,4,128,128]{5,4,3,2,1,0:T(8,128)} %get-tuple-element.91) | copy-start | bytes 6291460
  70.9 18.6 %collective-permute-start.8 = (bf16[2,2,2,4,128,128]{5,4,3,2,1,0:T(8,128)(2,1)}, bf16[2,2,2,4,128,128]{5,4,3,2,1,0:T(8,128)(2,1)}, u32[]{:S(2)}, u32[]{:S(2)}) collective-permute-start(bf16[2,2,2,4,128,128]{5,4,3,2,1,0:T(8,128)(2,1)} %get-tuple-element.82), channel_id=1, source_target_pairs={{0,1},{1,0},{2,3},{3,2},{4,5},{5,4},{6,7},{7,6},{8,9},{9,8},{10,11... | collective-permute-start | bytes 3145736 | tf_op jit(solution)/shard_map/ppermute | solution.py:357
  71.0 3.7 %collective-permute-start.27 = (f32[2,3,256]{2,1,0:T(4,128)S(1)}, f32[2,3,256]{2,1,0:T(4,128)S(1)}, u32[]{:S(2)}, u32[]{:S(2)}) collective-permute-start(f32[2,3,256]{2,1,0:T(4,128)S(1)} %pad_maximum_fusion.6), channel_id=1, source_target_pairs={{0,8},{4,12},{8,0},{12,4},{16,24},{20,28},{24,16},{28,20},{1,9},{5... | collective-permute-start | bytes 18440 | tf_op jit(solution)/shard_map/ppermute | solution.py:357
  74.7 4.6 %collective-permute-start.28 = (f32[4,3,256]{2,1,0:T(4,128)S(1)}, f32[4,3,256]{2,1,0:T(4,128)S(1)}, u32[]{:S(2)}, u32[]{:S(2)}) collective-permute-start(f32[4,3,256]{2,1,0:T(4,128)S(1)} %pad_maximum_fusion.4), channel_id=1, source_target_pairs={{0,16},{4,20},{8,24},{12,28},{16,0},{20,4},{24,8},{28,12},{1,17},{... | collective-permute-start | bytes 36872 | tf_op jit(solution)/shard_map/ppermute | solution.py:357
  77.3 4.9 %collective-permute-start.6 = (bf16[128,512]{1,0:T(8,128)(2,1)}, bf16[128,512]{1,0:T(8,128)(2,1)S(1)}, u32[]{:S(2)}, u32[]{:S(2)}) collective-permute-start(bf16[128,512]{1,0:T(8,128)(2,1)} %get-tuple-element.71), channel_id=1, source_target_pairs={{0,1},{1,0},{2,3},{3,2},{4,5},{5,4},{6,7},{7,6},{8,9},{9,8},{10,11... | collective-permute-start | bytes 393224 | tf_op jit(solution)/shard_map/ppermute | solution.py:357
  77.3 4.9 %collective-permute-start.7 = (bf16[128,512]{1,0:T(8,128)(2,1)}, bf16[128,512]{1,0:T(8,128)(2,1)S(1)}, u32[]{:S(2)}, u32[]{:S(2)}) collective-permute-start(bf16[128,512]{1,0:T(8,128)(2,1)} %get-tuple-element.72), channel_id=1, source_target_pairs={{1,2},{2,1},{5,6},{6,5},{9,10},{10,9},{13,14},{14,13},{17,18},{18,... | collective-permute-start | bytes 393224 | tf_op jit(solution)/shard_map/ppermute | solution.py:365
  85.4 4.2 %copy-start.1 = (f32[2,2,2,4,128,128]{5,4,3,2,1,0:T(8,128)S(1)}, f32[2,2,2,4,128,128]{5,4,3,2,1,0:T(8,128)}, u32[]{:S(2)}) copy-start(f32[2,2,2,4,128,128]{5,4,3,2,1,0:T(8,128)} %get-tuple-element.81) | copy-start | bytes 6291460
  85.8 8.1 %collective-permute-start.19 = (bf16[2,4,128,128]{3,2,1,0:T(8,128)(2,1)S(1)}, bf16[2,4,128,128]{3,2,1,0:T(8,128)(2,1)S(1)}, u32[]{:S(2)}, u32[]{:S(2)}) collective-permute-start(bf16[2,4,128,128]{3,2,1,0:T(8,128)(2,1)S(1)} %get-tuple-element.105), channel_id=1, source_target_pairs={{0,4},{4,0},{8,12},{12,8},{16,20},{20,16},{24,28},{28,24},{1,5},{5... | collective-permute-start | bytes 786440 | tf_op jit(solution)/shard_map/ppermute | solution.py:357
  86.3 10.4 %collective-permute-start.17 = (bf16[2,4,128,128]{3,2,1,0:T(8,128)(2,1)S(1)}, bf16[2,4,128,128]{3,2,1,0:T(8,128)(2,1)S(1)}, u32[]{:S(2)}, u32[]{:S(2)}) collective-permute-start(bf16[2,4,128,128]{3,2,1,0:T(8,128)(2,1)S(1)} %get-tuple-element.106), channel_id=1, source_target_pairs={{0,2},{1,3},{2,0},{3,1},{4,6},{5,7},{6,4},{7,5},{8,10},{9,11},{10,... | collective-permute-start | bytes 786440 | tf_op jit(solution)/shard_map/ppermute | solution.py:357
  91.2 18.2 %collective-permute-start.11 = (bf16[2,4,128,128]{3,2,1,0:T(8,128)(2,1)S(1)}, bf16[2,4,128,128]{3,2,1,0:T(8,128)(2,1)S(1)}, u32[]{:S(2)}, u32[]{:S(2)}) collective-permute-start(bf16[2,4,128,128]{3,2,1,0:T(8,128)(2,1)S(1)} %get-tuple-element.103), channel_id=1, source_target_pairs={{0,4},{4,0},{8,12},{12,8},{16,20},{20,16},{24,28},{28,24},{1,5},{5... | collective-permute-start | bytes 786440 | tf_op jit(solution)/shard_map/ppermute | solution.py:357
  92.8 16.6 %collective-permute-start.9 = (bf16[2,4,128,128]{3,2,1,0:T(8,128)(2,1)S(1)}, bf16[2,4,128,128]{3,2,1,0:T(8,128)(2,1)S(1)}, u32[]{:S(2)}, u32[]{:S(2)}) collective-permute-start(bf16[2,4,128,128]{3,2,1,0:T(8,128)(2,1)S(1)} %get-tuple-element.104), channel_id=1, source_target_pairs={{0,2},{1,3},{2,0},{3,1},{4,6},{5,7},{6,4},{7,5},{8,10},{9,11},{10,... | collective-permute-start | bytes 786440 | tf_op jit(solution)/shard_map/ppermute | solution.py:357
  96.8 6.5 %collective-permute-start.18 = (bf16[4,128,128]{2,1,0:T(8,128)(2,1)S(1)}, bf16[4,128,128]{2,1,0:T(8,128)(2,1)S(1)}, u32[]{:S(2)}, u32[]{:S(2)}) collective-permute-start(bf16[4,128,128]{2,1,0:T(8,128)(2,1)S(1)} %fusion.16), channel_id=1, source_target_pairs={{0,4},{4,0},{8,12},{12,8},{16,20},{20,16},{24,28},{28,24},{1,5},{5... | collective-permute-start | bytes 393224 | tf_op jit(solution)/shard_map/ppermute | solution.py:357
  98.4 6.5 %collective-permute-start.20 = (bf16[4,128,128]{2,1,0:T(8,128)(2,1)S(1)}, bf16[4,128,128]{2,1,0:T(8,128)(2,1)S(1)}, u32[]{:S(2)}, u32[]{:S(2)}) collective-permute-start(bf16[4,128,128]{2,1,0:T(8,128)(2,1)S(1)} %fusion.17), channel_id=1, source_target_pairs={{0,2},{1,3},{2,0},{3,1},{4,6},{5,7},{6,4},{7,5},{8,10},{9,11},{10,... | collective-permute-start | bytes 393224 | tf_op jit(solution)/shard_map/ppermute | solution.py:357
  105.0 13.5 %collective-permute-start.23 = (bf16[2,128,128]{2,1,0:T(8,128)(2,1)S(1)}, bf16[2,128,128]{2,1,0:T(8,128)(2,1)S(1)}, u32[]{:S(2)}, u32[]{:S(2)}) collective-permute-start(bf16[2,128,128]{2,1,0:T(8,128)(2,1)S(1)} %get-tuple-element.111), channel_id=1, source_target_pairs={{0,24},{4,28},{8,16},{12,20},{16,8},{20,12},{24,0},{28,4},{1,25},{... | collective-permute-start | bytes 196616 | tf_op jit(solution)/shard_map/ppermute | solution.py:357
  106.4 14.4 %collective-permute-start.22 = (bf16[2,128,128]{2,1,0:T(8,128)(2,1)S(1)}, bf16[2,128,128]{2,1,0:T(8,128)(2,1)S(1)}, u32[]{:S(2)}, u32[]{:S(2)}) collective-permute-start(bf16[2,128,128]{2,1,0:T(8,128)(2,1)S(1)} %get-tuple-element.112), channel_id=1, source_target_pairs={{0,16},{4,20},{8,24},{12,28},{16,0},{20,4},{24,8},{28,12},{1,17},{... | collective-permute-start | bytes 196616 | tf_op jit(solution)/shard_map/ppermute | solution.py:357
  108.1 12.7 %collective-permute-start.21 = (bf16[2,128,128]{2,1,0:T(8,128)(2,1)S(1)}, bf16[2,128,128]{2,1,0:T(8,128)(2,1)S(1)}, u32[]{:S(2)}, u32[]{:S(2)}) collective-permute-start(bf16[2,128,128]{2,1,0:T(8,128)(2,1)S(1)} %get-tuple-element.110), channel_id=1, source_target_pairs={{0,8},{4,12},{8,0},{12,4},{16,24},{20,28},{24,16},{28,20},{1,9},{5... | collective-permute-start | bytes 196616 | tf_op jit(solution)/shard_map/ppermute | solution.py:357
  109.6 5.0 %collective-permute-start.10 = (bf16[4,128,128]{2,1,0:T(8,128)(2,1)S(1)}, bf16[4,128,128]{2,1,0:T(8,128)(2,1)S(1)}, u32[]{:S(2)}, u32[]{:S(2)}) collective-permute-start(bf16[4,128,128]{2,1,0:T(8,128)(2,1)S(1)} %fusion.14), channel_id=1, source_target_pairs={{0,4},{4,0},{8,12},{12,8},{16,20},{20,16},{24,28},{28,24},{1,5},{5... | collective-permute-start | bytes 393224 | tf_op jit(solution)/shard_map/ppermute | solution.py:357
  111.2 5.0 %collective-permute-start.12 = (bf16[4,128,128]{2,1,0:T(8,128)(2,1)S(1)}, bf16[4,128,128]{2,1,0:T(8,128)(2,1)S(1)}, u32[]{:S(2)}, u32[]{:S(2)}) collective-permute-start(bf16[4,128,128]{2,1,0:T(8,128)(2,1)S(1)} %fusion.15), channel_id=1, source_target_pairs={{0,2},{1,3},{2,0},{3,1},{4,6},{5,7},{6,4},{7,5},{8,10},{9,11},{10,... | collective-permute-start | bytes 393224 | tf_op jit(solution)/shard_map/ppermute | solution.py:357
  116.3 6.2 %collective-permute-start.15 = (bf16[2,128,128]{2,1,0:T(8,128)(2,1)S(1)}, bf16[2,128,128]{2,1,0:T(8,128)(2,1)S(1)}, u32[]{:S(2)}, u32[]{:S(2)}) collective-permute-start(bf16[2,128,128]{2,1,0:T(8,128)(2,1)S(1)} %get-tuple-element.108), channel_id=1, source_target_pairs={{0,24},{4,28},{8,16},{12,20},{16,8},{20,12},{24,0},{28,4},{1,25},{... | collective-permute-start | bytes 196616 | tf_op jit(solution)/shard_map/ppermute | solution.py:357
  117.7 6.1 %collective-permute-start.14 = (bf16[2,128,128]{2,1,0:T(8,128)(2,1)S(1)}, bf16[2,128,128]{2,1,0:T(8,128)(2,1)S(1)}, u32[]{:S(2)}, u32[]{:S(2)}) collective-permute-start(bf16[2,128,128]{2,1,0:T(8,128)(2,1)S(1)} %get-tuple-element.109), channel_id=1, source_target_pairs={{0,16},{4,20},{8,24},{12,28},{16,0},{20,4},{24,8},{28,12},{1,17},{... | collective-permute-start | bytes 196616 | tf_op jit(solution)/shard_map/ppermute | solution.py:357
  118.5 5.3 %collective-permute-start.13 = (bf16[2,128,128]{2,1,0:T(8,128)(2,1)S(1)}, bf16[2,128,128]{2,1,0:T(8,128)(2,1)S(1)}, u32[]{:S(2)}, u32[]{:S(2)}) collective-permute-start(bf16[2,128,128]{2,1,0:T(8,128)(2,1)S(1)} %get-tuple-element.107), channel_id=1, source_target_pairs={{0,8},{4,12},{8,0},{12,4},{16,24},{20,28},{24,16},{28,20},{1,9},{5... | collective-permute-start | bytes 196616 | tf_op jit(solution)/shard_map/ppermute | solution.py:357
  (9 other events, 6.1 us)

commit v2 on v1

--- a/solution.py
+++ b/solution.py
@@ -1,3 +1,4 @@
+import functools
 import math
 
 import jax
@@ -7,6 +8,7 @@
 from jax.experimental.pallas import tpu as pltpu
 from jax.sharding import PartitionSpec as P
 
+
 HEADS = 4
 NOISE_FREQ = 16
 LAYERS = 2
@@ -63,35 +65,39 @@
 
 
 def start_kernel(
-    x_ref, near_ref, live_ref, noise_ref, film_w_ref, w_ref,
-    film_ref, bias_own_ref, bias_halo_ref, normed_ref, q_ref, k_ref, v_ref,
-):
-    node_count, slots = near_ref.shape
+    x_hbm, near_hbm, live_hbm, noise_ref, film_w_hbm, w_hbm,
+    film_ref, bias_own_ref, bias_halo_ref, normed_ref, q_ref, k_ref, v_ref, w_ref,
+    x_ref, near_ref, live_ref, film_w_ref, near_t_ref, sems,
+):
+    copies = [
+        pltpu.make_async_copy(near_hbm, near_ref, sems.at[0]),
+        pltpu.make_async_copy(live_hbm, live_ref, sems.at[1]),
+        pltpu.make_async_copy(x_hbm, x_ref, sems.at[2]),
+        pltpu.make_async_copy(film_w_hbm, film_w_ref, sems.at[3]),
+        pltpu.make_async_copy(w_hbm, w_ref, sems.at[4]),
+    ]
+    for copy in copies:
+        copy.start()
+    slots, node_count = near_ref.shape
     rim = node_count // 2
     place = lax.axis_index("mesh")
     parity = lax.rem(place, 2)
     embedding = embedding_of(jnp.full((2 * NOISE_FREQ, 1), noise_ref[0], F32))
-    for layer in range(LAYERS):
-        film_ref[layer : layer + 1, :] = jnp.sum(
-            embedding * film_w_ref[layer], axis=0, keepdims=True
-        )
-    normed = normed_of(x_ref[...], film_ref, 0)
-    normed_ref[...] = normed
-    project_own(normed, w_ref, 0, q_ref, k_ref, v_ref)
     column = lax.broadcasted_iota(jnp.int32, (1, node_count), 1)
-    low, high = column - node_count, column + rim
-    beside = jnp.where(column < rim, high + rim, low)
-    behind = jnp.where(column < rim, column - rim, high)
-    halo = jnp.where(parity == 0, beside, behind)
-    halo = jnp.where(column < rim,
-                     jnp.where(parity == 0, column + node_count, column - rim),
-                     jnp.where(parity == 0, column - node_count, column + rim))
+    halo = jnp.where(
+        column < rim,
+        jnp.where(parity == 0, column + node_count, column - rim),
+        jnp.where(parity == 0, column - node_count, column + rim),
+    )
+    copies[0].wait()
+    copies[1].wait()
+    near = jnp.where(live_ref[...] > 0, near_ref[...] - place * node_count, -(1 << 24))
+    near_t_ref[...] = near.T
     step = 32
 
     def rows(index, carry):
         start = pl.multiple_of(index * step, step)
-        near = near_ref[pl.ds(start, step), :] - place * node_count
-        near = jnp.where(live_ref[pl.ds(start, step), :] > 0, near, -(1 << 24))
+        near = near_t_ref[pl.ds(start, step), :]
         for ids, out_ref in ((column, bias_own_ref), (halo, bias_halo_ref)):
             bias = jnp.full((step, node_count), ABSENT, F32)
             for slot in range(slots):
@@ -100,6 +106,16 @@
         return carry
 
     lax.fori_loop(0, node_count // step, rows, 0)
+    copies[2].wait()
+    copies[3].wait()
+    for layer in range(LAYERS):
+        film_ref[layer : layer + 1, :] = jnp.sum(
+            embedding * film_w_ref[layer], axis=0, keepdims=True
+        )
+    normed = normed_of(x_ref[...], film_ref, 0)
+    normed_ref[...] = normed
+    copies[4].wait()
+    project_own(normed, w_ref, 0, q_ref, k_ref, v_ref)
 
 
 def own_kernel(x_ref, cot_ref, film_ref, w_ref, normed_ref, q_ref, k_ref, v_ref, ga_ref):
@@ -228,13 +244,19 @@
     )
 
 
-def upstream_of(x, up, gn_ref, pair_ref, other_ref, film_ref, layer, total_ref):
-    rim, width = pair_ref.shape
+def upstream_of(base, x, up, gn_ref, pair_ref, other_ref, film_ref, layer, total_ref):
+    rim, width = other_ref.shape
     parity = lax.rem(lax.axis_index("mesh"), 2)
     total_ref[...] = gn_ref[...]
     at_pair = pl.ds(pl.multiple_of((1 - parity) * rim, rim), rim)
     at_other = pl.ds(pl.multiple_of(parity * rim, rim), rim)
-    total_ref[at_pair, :] += pair_ref[...].astype(F32)
+    if base is None:
+        total_ref[at_pair, :] += pair_ref[...].astype(F32)
+    else:
+        for block in range(width // LANES):
+            start = base + block * rim
+            cols = slice(block * LANES, (block + 1) * LANES)
+            total_ref[at_pair, cols] += pair_ref[start : start + rim, :].astype(F32)
     total_ref[at_other, :] += other_ref[...].astype(F32)
     unit, inverse = unit_of(x)
     grad = total_ref[...] * (1.0 + film_ref[layer : layer + 1, :width])
@@ -247,13 +269,14 @@
 
 
 def first_layer_kernel(
-    next_ref, cot_ref, gn2_ref, back_pair_ref, back_other_ref, film_ref,
+    base, next_ref, cot_ref, gn2_ref, back_pair_ref, back_other_ref, film_ref,
     x_ref, pair_ref, other_ref, q_ref, k_ref, v_ref, k_h_ref, v_h_ref, p_own_ref, p_halo_ref, w_ref,
     up_ref, gq_ref, gk_ref, gv_ref, gk_h_ref, gv_h_ref, gn_ref, to_pair_ref, to_other_ref, cond_ref,
     total_ref, ga_ref,
 ):
     up = upstream_of(
-        next_ref[...], cot_ref[...], gn2_ref, back_pair_ref, back_other_ref, film_ref, 1, total_ref
+        base, next_ref[...], cot_ref[...], gn2_ref, back_pair_ref, back_other_ref, film_ref, 1,
+        total_ref,
     )
     up_ref[...] = up
     ga_ref[...] = mm_cols(up, w_ref[0, 3]).astype(BF16)
@@ -271,9 +294,9 @@
     )
 
 
-def end_kernel(x_ref, up_ref, gn_ref, pair_ref, other_ref, film_ref, out_ref, total_ref):
+def end_kernel(base, x_ref, up_ref, gn_ref, pair_ref, other_ref, film_ref, out_ref, total_ref):
     out_ref[...] = upstream_of(
-        x_ref[...], up_ref[...], gn_ref, pair_ref, other_ref, film_ref, 0, total_ref
+        base, x_ref[...], up_ref[...], gn_ref, pair_ref, other_ref, film_ref, 0, total_ref
     )
 
 
@@ -295,42 +318,210 @@
     weight_products(*ins, put)
 
 
-def split_weight_kernel(*refs):
-    *ins, send_ref, keep_ref, total_ref = refs
+def put_pair(value, out_ref):
+    high = value.astype(BF16)
+    rows = value.shape[0]
+    out_ref[:rows, :] = high
+    out_ref[rows:, :] = (value - high.astype(F32)).astype(BF16)
+
+
+def get_pair(in_ref):
+    rows = in_ref.shape[0] // 2
+    return in_ref[:rows, :].astype(F32) + in_ref[rows:, :].astype(F32)
+
+
+def get_noise(in_ref, start):
+    parts = [in_ref[start + row : start + row + 1, :].astype(F32) for row in range(3)]
+    return (parts[0] + parts[1]) + parts[2]
+
+
+def put_noise(value, out_ref, start):
+    for row in range(3):
+        part = value.astype(BF16)
+        out_ref[start + row : start + row + 1, :] = part
+        value = value - part.astype(F32)
+
+
+def split_weight_kernel(plan, layer, *refs):
+    *ins, to_pair_ref, cond_ref, other_cond_ref, send_ref, keep_ref, film_ref, total_ref = refs
 
     def put(slot, value):
         total_ref[slot] = value
 
     weight_products(*ins, put)
-    _, _, _, deep, _, _ = keep_ref.shape
-    rows = keep_ref.shape[4] // 2
+    rows = plan.rows // 2
     ens, mesh = lax.axis_index("ens"), lax.axis_index("mesh")
     for slot in range(4):
         group, inner = slot // 2, slot % 2
-        spot = slice(inner * rows, (inner + 1) * rows)
         for core in range(2):
             for y in range(2):
                 col = lax.bitwise_xor(mesh, y * 2 + core)
                 cols = pl.ds(pl.multiple_of(col * LANES, LANES), LANES)
                 for x in range(2):
-                    for z in range(deep):
+                    for z in range(plan.deep):
                         row = lax.bitwise_xor(ens, z * 2 + x)
                         at = pl.ds(pl.multiple_of(row * rows, rows), rows)
                         piece = total_ref[slot, at, cols]
                         first, second = (y, x) if group == 0 else (x, y)
+                        start = plan.at(group, first, second, z) + inner * rows
                         if core:
-                            send_ref[group, first, second, z, spot, :] = piece.astype(BF16)
+                            send_ref[start : start + rows, :] = piece.astype(BF16)
                         else:
-                            keep_ref[group, first, second, z, spot, :] = piece
-
-
-def film_kernel(rows_ref, noise_ref, out_ref):
-    members = rows_ref.shape[0]
+                            keep_ref[start : start + rows, :] = piece
+    rim, width = to_pair_ref.shape
+    for block in range(width // LANES):
+        start = plan.weights + block * rim
+        send_ref[start : start + rim, :] = to_pair_ref[:, block * LANES : (block + 1) * LANES]
+    if layer:
+        return
+    half = plan.film_rows // LAYERS
+    for core in range(2):
+        for y in range(2):
+            col = lax.bitwise_xor(mesh, y * 2 + core) * (half * LANES)
+            rows = []
+            for ref in (cond_ref, other_cond_ref):
+                for part in range(half):
+                    start = pl.multiple_of(col + part * LANES, LANES)
+                    rows.append(ref[:, pl.ds(start, LANES)])
+            for index, row in enumerate(rows):
+                film_ref[y, core, index : index + 1, :] = row
+    for y in range(2):
+        start = plan.weights + plan.halo + y * plan.film
+        put_pair(film_ref[y, 1], send_ref.at[start : start + 2 * plan.film_rows, :])
+
+
+def stage_one(plan, keep_ref, came_ref, y_ref, x_ref, kept_ref):
+    size = plan.weights // 4
+    for group, out_ref in ((0, y_ref), (1, x_ref)):
+        start = 2 * group * size
+        kept_ref[group * size : (group + 1) * size, :] = keep_ref[
+            start : start + size, :
+        ] + came_ref[start : start + size, :].astype(F32)
+        start += size
+        out_ref[:size, :] = (
+            keep_ref[start : start + size, :] + came_ref[start : start + size, :].astype(F32)
+        ).astype(BF16)
+
+
+def stage_two(plan, kept_ref, y_ref, x_ref, y_base, x_base, to_x_ref, to_y_ref, next_ref):
+    size = plan.weights // 8
+    for group, in_ref, base, out_ref in ((0, y_ref, y_base, to_x_ref), (1, x_ref, x_base, to_y_ref)):
+        start = 2 * group * size
+        next_ref[group * size : (group + 1) * size, :] = kept_ref[
+            start : start + size, :
+        ] + in_ref[base : base + size, :].astype(F32)
+        out_ref[...] = (
+            kept_ref[start + size : start + 2 * size, :]
+            + in_ref[base + size : base + 2 * size, :].astype(F32)
+        ).astype(BF16)
+
+
+def stage_three(plan, kept_ref, x_ref, y_ref, x_base, y_base, z_refs, last_ref):
+    rows = plan.rows
+    for group, in_ref, base in ((0, x_ref, x_base), (1, y_ref, y_base)):
+        for z in range(plan.deep):
+            start = (group * plan.deep + z) * rows
+            value = kept_ref[start : start + rows, :] + in_ref[
+                base + z * rows : base + (z + 1) * rows, :
+            ].astype(F32)
+            if z:
+                z_refs[z - 1][group * rows : (group + 1) * rows, :] = value.astype(BF16)
+            else:
+                last_ref[group * rows : (group + 1) * rows, :] = value
+
+
+def start_scatter_kernel(plan, keep_ref, came_ref, y_ref, x_ref, kept_ref):
+    stage_one(plan, keep_ref, came_ref, y_ref, x_ref, kept_ref)
+
+
+def slot_a_kernel(
+    plan, keep1_ref, film1_ref, came1_ref, kept2_ref, y2_ref, x2_ref,
+    y_ref, x_ref, kept1_ref, next2_ref, film_ref,
+):
+    size, small = plan.weights // 4, plan.weights // 8
+    stage_one(plan, keep1_ref, came1_ref, y_ref, x_ref, kept1_ref)
+    stage_two(
+        plan, kept2_ref, y2_ref, x2_ref, 0, 0,
+        x_ref.at[size : size + small, :], y_ref.at[size : size + small, :], next2_ref,
+    )
+    start, end = plan.weights + plan.halo, 2 * plan.film_rows
+    film_ref[...] = film1_ref[0, 0] + get_pair(came1_ref.at[start : start + end, :])
+    start += plan.film
+    put_pair(
+        film1_ref[1, 0] + get_pair(came1_ref.at[start : start + end, :]),
+        y_ref.at[size + small : size + small + end, :],
+    )
+
+
+def slot_b_kernel(
+    plan, kept1_ref, kept2_ref, film_ref, y_ref, x_ref, noise_ref, *outs,
+):
+    to_x_ref, to_y_ref, next1_ref, last2_ref, *z_refs = outs
+    size, small = plan.weights // 4, plan.weights // 8
+    stage_two(
+        plan, kept1_ref, y_ref, x_ref, 0, 0, to_x_ref.at[:small, :], to_y_ref.at[:small, :], next1_ref
+    )
+    stage_three(plan, kept2_ref, x_ref, y_ref, size, size, z_refs, last2_ref)
+    end = 2 * plan.film_rows
+    start = size + small
+    total = film_ref[...] + get_pair(y_ref.at[start : start + end, :])
+    put_pair(total, to_x_ref.at[small : small + end, :])
+    put_noise(jnp.full((1, LANES), noise_ref[0], F32), to_x_ref, small + end)
+
+
+def slot_c_kernel(plan, kept1_ref, x_ref, y_ref, mine_ref, *outs):
+    last1_ref, *z_refs = outs
+    stage_three(plan, kept1_ref, x_ref, y_ref, 0, 0, z_refs, last1_ref)
+    small, end = plan.weights // 8, 2 * plan.rows
+    for z_ref in z_refs:
+        z_ref[end : end + plan.film, :] = mine_ref[small : small + plan.film, :]
+        z_ref[end + plan.film :, :] = x_ref[small : small + plan.film, :]
+
+
+def finish_kernel(plan, last1_ref, last2_ref, mine_ref, x_ref, *refs):
+    count = plan.deep - 1
+    z1_refs, z2_refs, (out_ref, film_ref) = refs[:count], refs[count : 2 * count], refs[2 * count :]
+    for layer, (last_ref, z_refs) in enumerate(((last1_ref, z1_refs), (last2_ref, z2_refs))):
+        rows = plan.rows // 2
+        for slot in range(4):
+            at = slice(slot * rows, (slot + 1) * rows)
+            total = last_ref[at, :]
+            for z_ref in z_refs:
+                total = total + z_ref[at, :].astype(F32)
+            out_ref[layer, slot] = total
+    small, end = plan.weights // 8, 2 * plan.rows
+    packs = [ref.at[small : small + plan.film, :] for ref in (mine_ref, x_ref)]
+    for z_ref in z1_refs:
+        packs += [z_ref.at[end + i * plan.film : end + (i + 1) * plan.film, :] for i in range(2)]
+    lane = lax.broadcasted_iota(jnp.int32, (1, LANES), 1)
+    noise = jnp.ones((1, LANES), F32)
+    pair = 2 * plan.film_rows
+    for member, pack in enumerate(packs):
+        noise = jnp.where(lane == member, get_noise(pack, pair), noise)
+    embedding = embedding_of(jnp.broadcast_to(noise, (2 * NOISE_FREQ, LANES)))
+    members = [get_pair(pack.at[:pair, :]) for pack in packs]
+    half = plan.film_rows // LAYERS
     for layer in range(LAYERS):
-        total = jnp.zeros(out_ref.shape[1:], F32)
+        for part in range(half):
+            row = layer * half + part
+            total = jnp.zeros((2 * NOISE_FREQ, LANES), F32)
+            for member, value in enumerate(members):
+                total += embedding[:, member : member + 1] * value[row : row + 1, :]
+            film_ref[layer, :, part * LANES : (part + 1) * LANES] = total
+
+
+def film_kernel(rows_ref, out_ref):
+    members, _, columns = rows_ref.shape
+    rows = rows_ref[...]
+    lane = lax.broadcasted_iota(jnp.int32, (1, LANES), 1)
+    noise = jnp.ones((1, LANES), F32)
+    for member in range(members):
+        noise = jnp.where(lane == member, rows[member, LAYERS:, :1], noise)
+    embedding = embedding_of(jnp.broadcast_to(noise, (2 * NOISE_FREQ, LANES)))
+    for layer in range(LAYERS):
+        total = jnp.zeros((2 * NOISE_FREQ, columns), F32)
         for member in range(members):
-            noise = jnp.full((2 * NOISE_FREQ, 1), noise_ref[member], F32)
-            total += embedding_of(noise) * rows_ref[member, layer : layer + 1, :]
+            total += embedding[:, member : member + 1] * rows[member, layer : layer + 1, :]
         out_ref[layer] = total
 
 
@@ -338,16 +529,20 @@
     return pl.BlockSpec(memory_space=pltpu.VMEM)
 
 
-def call(kernel, name, args, outs, scratch=(), flops=0, specs=None):
+def apart():
+    return pl.BlockSpec(memory_space=pltpu.HBM)
+
+
+def call(kernel, args, outs, scratch=(), flops=0, specs=None, limit=10 << 20, sems=()):
     moved = sum(a.size * a.dtype.itemsize for a in args)
     moved += sum(math.prod(shape) * jnp.dtype(kind).itemsize for shape, kind in outs)
     return pl.pallas_call(
         kernel,
-        name=name,
         out_shape=[jax.ShapeDtypeStruct(shape, kind) for shape, kind in outs],
         in_specs=specs or [whole() for _ in args],
         out_specs=[whole() for _ in outs],
-        scratch_shapes=[pltpu.VMEM(shape, kind) for shape, kind in scratch],
+        scratch_shapes=[pltpu.VMEM(shape, kind) for shape, kind in scratch] + list(sems),
+        compiler_params=pltpu.CompilerParams(vmem_limit_bytes=limit),
         cost_estimate=pl.CostEstimate(flops=flops, bytes_accessed=moved, transcendentals=0),
     )(*args)
 
@@ -357,63 +552,59 @@
     return lax.ppermute(block, axis, [(i, i ^ bit) for i in range(count)])
 
 
-def exchange(to_pair, to_other):
+def exchange_other(to_other):
     count = lax.axis_size("mesh")
     route = []
     for i in range(1, count - 1, 2):
         route += [(i, i + 1), (i + 1, i)]
-    other = lax.ppermute(to_other, "mesh", route)
+    return lax.ppermute(to_other, "mesh", route)
+
+
+def exchange(to_pair, to_other):
+    other = exchange_other(to_other)
     return swap(to_pair, "mesh", 1), other
 
 
-def scattered_core(send):
-    return swap(send, "mesh", 1)
-
-
-def scatter_first(keep, send):
-    held = keep + swap(send, "mesh", 1).astype(F32)
-    to_y, to_x = held[0, 1].astype(BF16), held[1, 1].astype(BF16)
-    return (held[0, 0], held[1, 0]), (swap(to_y, "mesh", 2), swap(to_x, "ens", 1))
-
-
-def scatter_second(kept, came):
-    one = kept[0] + came[0].astype(F32)
-    two = kept[1] + came[1].astype(F32)
-    to_x, to_y = one[1].astype(BF16), two[1].astype(BF16)
-    return (one[0], two[0]), (swap(to_x, "ens", 1), swap(to_y, "mesh", 2))
-
-
-def scatter_third(kept, came):
-    both = jnp.stack([kept[0] + came[0].astype(F32), kept[1] + came[1].astype(F32)])
-    total = both[:, 0]
-    came = [swap(both[:, z].astype(BF16), "ens", 2 * z) for z in range(1, both.shape[1])]
-    for part in came:
-        total = total + part.astype(F32)
-    return total
-
-
-def film_sum(conds, noise_level, mesh_count):
+class Plan:
+    def __init__(self, width, rim, ens_count, mesh_count):
+        self.deep = ens_count // 2
+        self.rows = 2 * width // ens_count
+        self.weights = 8 * self.deep * self.rows
+        self.halo = rim * width // LANES
+        self.film_rows = LAYERS * (2 * width // mesh_count) // LANES
+        self.film = 16 * pl.cdiv(2 * self.film_rows + 3, 16)
+
+    def at(self, group, first, second, z):
+        return (((group * 2 + first) * 2 + second) * self.deep + z) * self.rows
+
+
+def film_pieces(conds, noise_level, mesh_count):
     mesh = lax.axis_index("mesh")
     rows = jnp.concatenate(conds, axis=0)
     width = rows.shape[1] // mesh_count
     pieces = rows.reshape(LAYERS, mesh_count, width).transpose(1, 0, 2)
-    order = lax.bitwise_xor(jnp.arange(mesh_count), mesh)
-    pieces = jnp.take(pieces, order, axis=0)
-    bit = 1
-    while bit < mesh_count:
-        pieces = pieces.reshape(-1, 2, LAYERS, width)
-        pieces = pieces[:, 0] + swap(pieces[:, 1], "mesh", bit)
-        bit *= 2
-    row = jnp.concatenate([pieces[0], jnp.full((1, width), noise_level[0])])[None]
-    bit = 1
-    while bit < lax.axis_size("ens"):
-        row = jnp.concatenate([row, swap(row, "ens", bit)])
-        bit *= 2
-    noise = row[:, LAYERS, 0]
-    return call(
-        film_kernel, "film", (row, noise), [((LAYERS, 2 * NOISE_FREQ, width), F32)],
-        specs=[whole(), pl.BlockSpec(memory_space=pltpu.SMEM)],
-    )[0]
+    pieces = jnp.take(pieces, lax.bitwise_xor(jnp.arange(mesh_count), mesh), axis=0)
+    noise = jnp.where(jnp.arange(mesh_count) == 0, noise_level[0], 0.0)
+    noise = jnp.broadcast_to(noise[:, None, None], (mesh_count, 1, width))
+    return jnp.concatenate([pieces, noise], axis=1)
+
+
+def film_mesh_step(pieces, bit):
+    pieces = pieces.reshape(-1, 2, *pieces.shape[1:])
+    return pieces[:, 0] + swap(pieces[:, 1], "mesh", bit)
+
+
+def film_ens_step(rows, bit):
+    return jnp.concatenate([rows, swap(rows, "ens", bit)])
+
+
+def film_end(rows):
+    shape = (LAYERS, 2 * NOISE_FREQ, rows.shape[2])
+    return call(film_kernel, (rows,), [(shape, F32)])[0]
+
+
+def bits_of(count):
+    return [1 << index for index in range(count.bit_length() - 1)]
 
 
 def body(inputs, cotangent, noise_level, neighbours, live_slots, projections, film_weights):
@@ -435,72 +626,124 @@
         lax.dynamic_slice_in_dim(states, (1 - parity) * rim, rim),
         lax.dynamic_slice_in_dim(states, parity * rim, rim),
     )
-    film, bias_own, bias_halo, normed1, q1, k1, v1 = call(
-        start_kernel, "start",
-        (states, neighbours, live_slots, noise_level, film_weights, projections),
-        [((LAYERS, 2 * width), F32), ((nodes, nodes), F32), ((nodes, nodes), F32)] + [full()] * 4,
-        flops=3 * square,
-        specs=[whole()] * 3 + [pl.BlockSpec(memory_space=pltpu.SMEM)] + [whole()] * 2,
+    slots = neighbours.shape[1]
+    film, bias_own, bias_halo, normed1, q1, k1, v1, projections = call(
+        start_kernel,
+        (*(pltpu.with_memory_space_constraint(a, pltpu.HBM)
+           for a in (states, neighbours.T, live_slots.T)), noise_level,
+         *(pltpu.with_memory_space_constraint(a, pltpu.HBM)
+           for a in (film_weights, projections))),
+        [((LAYERS, 2 * width), F32), ((nodes, nodes), F32), ((nodes, nodes), F32)] + [full()] * 4
+        + [(projections.shape, BF16)],
+        scratch=[full(), ((slots, nodes), jnp.int32), ((slots, nodes), jnp.int32),
+                 (film_weights.shape, F32), (neighbours.shape, jnp.int32)],
+        sems=[pltpu.SemaphoreType.DMA((5,))], flops=3 * square,
+        specs=[apart()] * 3 + [pl.BlockSpec(memory_space=pltpu.SMEM)] + [apart()] * 2,
     )
     probs_shape = ((HEADS, nodes, nodes), BF16)
     states2, to_pair, to_other, normed1_h, k1_h, v1_h, p_own, p_halo, attended1 = call(
-        forward_kernel, "forward",
+        forward_kernel,
         (states, pair1, other1, film, q1, k1, v1, bias_own, bias_halo, projections),
         [full()] + rims + [full()] * 3 + [probs_shape] * 2 + [full()],
         flops=5 * square,
     )
     pair2, other2 = exchange(to_pair, to_other)
     normed2, q2, k2, v2, ga2 = call(
-        own_kernel, "own", (states2, cot, film, projections), [full()] * 5, flops=4 * square
+        own_kernel, (states2, cot, film, projections), [full()] * 5, flops=4 * square
     )
     grads = [full()] * 5 + [full(F32)] + rims + [cond_shape]
     normed2_h, attended2, gq2, gk2, gv2, gk2_h, gv2_h, gn2, to_pair, to_other, cond2 = call(
-        last_layer_kernel, "last",
+        last_layer_kernel,
         (states2, pair2, other2, film, q2, k2, v2, ga2, bias_own, bias_halo, projections),
         [full()] * 2 + grads,
         scratch=[full()] * 2, flops=14 * square,
     )
-    back_pair, back_other = exchange(to_pair, to_other)
-
-    def weight_grads(name, *args):
+    plan = Plan(width, rim, ens_count, mesh_count) if split else None
+    base = plan.weights if split else None
+    sums = plan.weights if split else 0
+
+    def block(rows, kind=BF16):
+        return ((rows, LANES), kind)
+
+    def weight_grads(layer, to_pair, conds, *args):
         if not split:
-            return call(
-                plain_weight_kernel, name, args, [((4, width, width), F32)], flops=6 * square
-            )[0]
-        shape = (2, 2, 2, ens_count // 2, 2 * (width // ens_count), LANES)
+            out = call(plain_weight_kernel, args, [((4, width, width), F32)], flops=6 * square)
+            return out[0], None, None
+        film_shape = (2, 2, plan.film_rows, LANES)
         return call(
-            split_weight_kernel, name, args, [(shape, BF16), (shape, F32)],
+            functools.partial(split_weight_kernel, plan, layer), args + (to_pair,) + conds,
+            [block(sums + plan.halo + 2 * plan.film), block(sums, F32), (film_shape, F32)],
             scratch=[((4, width, width), F32)], flops=6 * square,
         )
 
-    weights2 = weight_grads(
-        "weights2", normed2, normed2_h, attended2, cot, gq2, gk2, gv2, gk2_h, gv2_h
-    )
+    back_other = exchange_other(to_other)
+    weights2, keep2, _ = weight_grads(
+        1, to_pair, (cond2, cond2),
+        normed2, normed2_h, attended2, cot, gq2, gk2, gv2, gk2_h, gv2_h,
+    )
+    if split:
+        back_pair = swap(weights2, "mesh", 1)
+        to_y, to_x, kept2 = call(
+            functools.partial(start_scatter_kernel, plan), (keep2, back_pair),
+            [block(sums // 4)] * 2 + [block(sums // 2, F32)],
+        )
+        y2, x2 = swap(to_y, "mesh", 2), swap(to_x, "ens", 1)
+    else:
+        back_pair = swap(to_pair, "mesh", 1)
     up, gq1, gk1, gv1, gk1_h, gv1_h, gn1, to_pair, to_other, cond1 = call(
-        first_layer_kernel, "first",
+        functools.partial(first_layer_kernel, base),
         (states2, cot, gn2, back_pair, back_other, film,
          states, pair1, other1, q1, k1, v1, k1_h, v1_h, p_own, p_halo, projections),
         [full()] + grads,
         scratch=[full(F32), full()], flops=11 * square,
     )
-    back_pair, back_other = exchange(to_pair, to_other)
-    weights1 = weight_grads(
-        "weights1", normed1, normed1_h, attended1, up, gq1, gk1, gv1, gk1_h, gv1_h
-    )
+    back_other = exchange_other(to_other)
+    weights1, keep1, rows1 = weight_grads(
+        0, to_pair, (cond1, cond2),
+        normed1, normed1_h, attended1, up, gq1, gk1, gv1, gk1_h, gv1_h,
+    )
+    back_pair = swap(weights1 if split else to_pair, "mesh", 1)
     grad_input = call(
-        end_kernel, "end", (states, up, gn1, back_pair, back_other, film), [full()],
+        functools.partial(end_kernel, base),
+        (states, up, gn1, back_pair, back_other, film), [full()],
         scratch=[full(F32)],
     )[0]
-    film_out = film_sum((cond1, cond2), noise_level, mesh_count)
     if split:
-        outs = []
-        for send, keep in (weights1, weights2):
-            kept, came = scatter_first(keep, send)
-            kept, came = scatter_second(kept, came)
-            total = scatter_third(kept, came)
-            outs.append(total.reshape(4, width // ens_count, LANES))
-        weight_out = jnp.stack(outs)
+        to_y, to_x, kept1, kept2, film_mine = call(
+            functools.partial(slot_a_kernel, plan),
+            (keep1, rows1, back_pair, kept2, y2, x2),
+            [block(sums // 4 + sums // 8 + plan.film), block(sums // 4 + sums // 8),
+             block(sums // 2, F32), block(sums // 4, F32), block(plan.film_rows, F32)],
+        )
+        came_y, came_x = swap(to_y, "mesh", 2), swap(to_x, "ens", 1)
+        others = range(1, plan.deep)
+        to_x, to_y, kept1, last2, *to_z = call(
+            functools.partial(slot_b_kernel, plan),
+            (kept1, kept2, film_mine, came_y, came_x, noise_level),
+            [block(sums // 8 + plan.film), block(sums // 8), block(sums // 4, F32),
+             block(2 * plan.rows, F32)] + [block(2 * plan.rows) for _ in others],
+            specs=[whole()] * 5 + [pl.BlockSpec(memory_space=pltpu.SMEM)],
+        )
+        came_x, came_y = swap(to_x, "ens", 1), swap(to_y, "mesh", 2)
+        came_z2 = [swap(to_z[z - 1], "ens", 2 * z) for z in others]
+        last1, *to_z = call(
+            functools.partial(slot_c_kernel, plan), (kept1, came_x, came_y, to_x),
+            [block(2 * plan.rows, F32)] + [block(2 * plan.rows + 2 * plan.film) for _ in others],
+        )
+        came_z1 = [swap(to_z[z - 1], "ens", 2 * z) for z in others]
+        weight_out, film_out = call(
+            functools.partial(finish_kernel, plan),
+            (last1, last2, to_x, came_x, *came_z1, *came_z2),
+            [((LAYERS, 4, width // ens_count, LANES), F32),
+             ((LAYERS, 2 * NOISE_FREQ, 2 * width // mesh_count), F32)],
+        )
     else:
+        film_rows = film_pieces((cond1, cond2), noise_level, mesh_count)
+        for bit in bits_of(mesh_count):
+            film_rows = film_mesh_step(film_rows, bit)
+        for bit in bits_of(ens_count):
+            film_rows = film_ens_step(film_rows, bit)
+        film_out = film_end(film_rows)
         part = jnp.stack([weights1, weights2]).astype(BF16)
         part = lax.psum_scatter(part, "ens", scatter_dimension=2, tiled=True)
         weight_out = lax.psum_scatter(part, "mesh", scatter_dimension=3, tiled=True).astype(F32)

time: 125 us -> 84 us (0.67)
  Pallas kernels: 47.3 us -> 23.1 us
  starting transfers between devices: 41.6 us -> 33.5 us
  local copies, waits for them, and re-layouts: 8.27 us -> 1 us
  other arithmetic: 4.08 us -> 0 us
  waiting for transfers between devices: 21.7 us -> 24.7 us
    pallas_call x9 -> x13, Pallas kernels: 47.3 us -> 23.1 us  [call(): pl.pallas_call(kernel, out_shape=[jax.ShapeDtypeStruct(shape, kind) for s...]
    ppermute x25 -> x16, starting transfers between devices: 38.8 us -> 30.7 us  [swap(): return lax.ppermute(block, axis, [(i, i ^ bit) for i in range(count)])]
    unnamed x26 -> x4, local copies, waits for them, and re-layouts: 5.84 us -> 0.01 us
    ppermute x25 -> x16, waiting for transfers between devices: 21.7 us -> 24.7 us  [swap(): return lax.ppermute(block, axis, [(i, i ^ bit) for i in range(count)])]
    another operation x9 -> x0, other arithmetic: 2.97 us -> none
  transfers between devices with their start and end apart: 29 -> 20, of which waited for: 12 -> 6; matrix products, arithmetic and copies ran while one was open for 5% -> 0% of each run, Pallas kernels for 19% -> 8%
where the time goes in v2:
time: 84 us; the launch traced here: 83.8 us
  starting transfers between devices  33.5 us (40%)
  waiting for transfers between devices  24.7 us (29%)
  Pallas kernels  23.1 us (28%)
  between operations  1.47 us (2%)
  local copies, waits for them, and re-layouts  1 us (1%)
    ppermute x16, starting transfers between devices, swap(): return lax.ppermute(block, axis, [(i, i ^ bit) for i in range(count)])  30.7 us
    ppermute x16, waiting for transfers between devices, swap(): return lax.ppermute(block, axis, [(i, i ^ bit) for i in range(count)])  24.7 us
    pallas_call x13, Pallas kernels, call(): pl.pallas_call(kernel, out_shape=[jax.ShapeDtypeStruct(shape, kind) for s...  23.1 us
    ppermute x4, starting transfers between devices, exchange_other(): return lax.ppermute(to_other, 'mesh', route)  2.81 us
  transfers between devices with their start and end apart: 20, of which 6 were waited for; matrix products, arithmetic and copies ran while one was open for 0% of the time, Pallas kernels for 8%

profile of v2, /device:TPU:0, one launch (start us, length us, event | category | flops | bytes accessed | tf_op | source)
XLA Modules:
  0.0 83.8 jit_solution(17506081210548557890)
XLA Ops:
  0.6 1.0 %dynamic-slice_bitcast_fusion = (bf16[128,512]{1,0:T(8,128)(2,1)S(1)}, bf16[128,512]{1,0:T(8,128)(2,1)S(1)}) fusion(bf16[1,256,512]{2,1,0:T(8,128)(2,1)} %param.7, s32[]{:T(128)S(6)} %select_n.7, s32[]{:T(128)S(6)} %select_n.6), kind=kLoop, calls=%fused_computation | loop fusion | bytes 524296 | tf_op jit(solution)/shard_map/dynamic_slice | solution.py:627
  2.2 0.7 collective-permute-start.1
  3.5 3.9 %shard_map.94 = (f32[2,1024]{1,0:T(2,128)S(1)}, f32[256,256]{1,0:T(8,128)S(1)}, f32[256,256]{1,0:T(8,128)S(1)}, bf16[256,512]{1,0:T(8,128)(2,1)S(1)}, bf16[256,5...) custom-call(bf16[256,512]{1,0:T(8,128)(2,1)} %bitcast.9, ...), custom_call_target="tpu_custom_call" | custom-call | flops 402653184 | bytes 10559492 | tf_op jit(solution)/shard_map/pallas_call | solution.py:539
  7.4 2.6 %shard_map.95 = (bf16[256,512]{1,0:T(8,128)(2,1)S(1)}, bf16[128,512]{1,0:T(8,128)(2,1)S(1)}, bf16[128,512]{1,0:T(8,128)(2,1)S(1)}, bf16[256,512]{1,0:T(8,128)(2,...) custom-call(bf16[256,512]{1,0:T(8,128)(2,1)S(1)} %bitcast.10, ...), custom_call_target="tpu_custom_call" | custom-call | flops 671088640 | bytes 8658944 | tf_op jit(solution)/shard_map/pallas_call | solution.py:539
  10.0 3.9 %collective-permute-start.2 = (bf16[128,512]{1,0:T(8,128)(2,1)S(1)}, bf16[128,512]{1,0:T(8,128)(2,1)S(1)}, u32[]{:S(2)}, u32[]{:S(2)}) collective-permute-start(bf16[128,512]{1,0:T(8,128)(2,1)S(1)} %get-tuple-element.80), channel_id=1, source_target_pairs={{0,1},{1,0},{2,3},{3,2},{4,5},{5,4},{6,7},{7,6},{8,9},{9,8},{10,11... | collective-permute-start | bytes 393224 | tf_op jit(solution)/shard_map/ppermute | solution.py:552
  14.0 0.7 collective-permute-start.3
  14.6 0.9 %shard_map.96 = (bf16[256,512]{1,0:T(8,128)(2,1)S(1)}, bf16[256,512]{1,0:T(8,128)(2,1)S(1)}, bf16[256,512]{1,0:T(8,128)(2,1)S(1)}, bf16[256,512]{1,0:T(8,128)(2,1)S(1)}, bf16[256,512]{1,0:T(8,128)(2,1)S(1)}) custom-call(bf16[256,512]{1,0:T(8,128)(2,1)S(1)} %get-tuple-element.79.x_ref.next_ref, bf16[256,512]{1,0:T(8,128)(2,1)S(1)} %bitcast.13, ...), custom_call_target="tpu_custom_call" | custom-call | flops 536870912 | bytes 6037504 | tf_op jit(solution)/shard_map/pallas_call | solution.py:539
  15.6 5.3 %shard_map.97 = (bf16[256,512]{1,0:T(8,128)(2,1)S(1)}, bf16[256,512]{1,0:T(8,128)(2,1)S(1)}, bf16[256,512]{1,0:T(8,128)(2,1)S(1)}, bf16[256,512]{1,0:T(8,128)(2,...) custom-call(bf16[256,512]{1,0:T(8,128)(2,1)S(1)} %get-tuple-element., ...), custom_call_target="tpu_custom_call" | custom-call | flops 1879048192 | bytes 8925184 | tf_op jit(solution)/shard_map/pallas_call | solution.py:539
  20.9 2.2 %shard_map.98 = (bf16[4640,128]{1,0:T(8,128)(2,1)S(1)}, f32[4096,128]{1,0:T(8,128)S(1)}, f32[2,2,4,128]{3,2,1,0:T(4,128)}) custom-call(bf16[256,512]{1,0:T(8,128)(2,1)S(1)} %get-tuple-element.87.refs_0_, bf16[256,512]{1,0:T(8,128)(2,1)S(1)} %get-tuple-element.88.refs_1_, bf16[256,512]{1,0:T(8,128)(2,1)S(1)} %get-tuple-element.89.refs_2_, ...), custom_call_target="tpu_custom_call" | custom-call | flops 805306368 | bytes 5791744 | tf_op jit(solution)/shard_map/pallas_call | solution.py:539
  23.1 4.6 %collective-permute-start.4 = (bf16[4640,128]{1,0:T(8,128)(2,1)S(1)}, bf16[4640,128]{1,0:T(8,128)(2,1)S(1)}, u32[]{:S(2)}, u32[]{:S(2)}) collective-permute-start(bf16[4640,128]{1,0:T(8,128)(2,1)S(1)} %get-tuple-element.97), channel_id=1, source_target_pairs={{0,1},{1,0},{2,3},{3,2},{4,5},{5,4},{6,7},{7,6},{8,9},{9,8},{10,11... | collective-permute-start | bytes 3563528 | tf_op jit(solution)/shard_map/ppermute | solution.py:552
  27.7 0.8 collective-permute-start.5
  28.5 1.6 %collective-permute-done.4.back_pair_ref.came_ref = bf16[4640,128]{1,0:T(8,128)(2,1)S(1)} collective-permute-done((bf16[4640,128]{1,0:T(8,128)(2,1)S(1)}, bf16[4640,128]{1,0:T(8,128)(2,1)S(1)}, u32[]{:S(2)}, u32[]{:S(2)}) %collective-permute-start.4) | collective-permute-done | bytes 1187872 | tf_op jit(solution)/shard_map/ppermute | solution.py:552
  30.2 3.7 %shard_map.99 = (bf16[256,512]{1,0:T(8,128)(2,1)S(1)}, bf16[256,512]{1,0:T(8,128)(2,1)S(1)}, bf16[256,512]{1,0:T(8,128)(2,1)S(1)}, bf16[256,512]{1,0:T(8,128)(2,...) custom-call(bf16[256,512]{1,0:T(8,128)(2,1)S(1)} %get-tuple-element., ...), custom_call_target="tpu_custom_call" | custom-call | flops 1476395008 | bytes 11816960 | tf_op jit(solution)/shard_map/pallas_call | solution.py:539
  33.9 1.6 %shard_map.100 = (bf16[4640,128]{1,0:T(8,128)(2,1)S(1)}, f32[4096,128]{1,0:T(8,128)S(1)}, f32[2,2,4,128]{3,2,1,0:T(4,128)S(1)}) custom-call(bf16[256,512]{1,0:T(8,128)(2,1)S(1)} %get-tuple-element.105.refs_0_, bf16[256,512]{1,0:T(8,128)(2,1)S(1)} %get-tuple-element.106.refs_1_, bf16[256,512]{1,0:T(8,128)(2,1)S(1)} %get-tuple-element.107.refs_2_, ...), custom_call_target="tpu_custom_call" | custom-call | flops 805306368 | bytes 5791744 | tf_op jit(solution)/shard_map/pallas_call | solution.py:539
  35.5 3.9 %collective-permute-start.6 = (bf16[4640,128]{1,0:T(8,128)(2,1)S(1)}, bf16[4640,128]{1,0:T(8,128)(2,1)S(1)}, u32[]{:S(2)}, u32[]{:S(2)}) collective-permute-start(bf16[4640,128]{1,0:T(8,128)(2,1)S(1)} %get-tuple-element.115), channel_id=1, source_target_pairs={{0,1},{1,0},{2,3},{3,2},{4,5},{5,4},{6,7},{7,6},{8,9},{9,8},{10,11... | collective-permute-start | bytes 3563528 | tf_op jit(solution)/shard_map/ppermute | solution.py:552
  39.7 2.0 %collective-permute-start.9 = (bf16[1024,128]{1,0:T(8,128)(2,1)S(1)}, bf16[1024,128]{1,0:T(8,128)(2,1)S(1)}, u32[]{:S(2)}, u32[]{:S(2)}) collective-permute-start(bf16[1024,128]{1,0:T(8,128)(2,1)S(1)} %get-tuple-element.122), channel_id=1, source_target_pairs={{0,4},{4,0},{8,12},{12,8},{16,20},{20,16},{24,28},{28,24},{1,5},{5... | collective-permute-start | bytes 786440 | tf_op jit(solution)/shard_map/ppermute | solution.py:552
  41.7 6.2 %collective-permute-done.8.y2_ref = bf16[1024,128]{1,0:T(8,128)(2,1)S(1)} collective-permute-done((bf16[1024,128]{1,0:T(8,128)(2,1)S(1)}, bf16[1024,128]{1,0:T(8,128)(2,1)S(1)}, u32[]{:S(2)}, u32[]{:S(2)}) %collective-permute-start.8) | collective-permute-done | bytes 262176 | tf_op jit(solution)/shard_map/ppermute | solution.py:552
  48.7 1.3 %collective-permute-start.10 = (bf16[1552,128]{1,0:T(8,128)(2,1)S(1)}, bf16[1552,128]{1,0:T(8,128)(2,1)S(1)}, u32[]{:S(2)}, u32[]{:S(2)}) collective-permute-start(bf16[1552,128]{1,0:T(8,128)(2,1)S(1)} %get-tuple-element.126), channel_id=1, source_target_pairs={{0,2},{1,3},{2,0},{3,1},{4,6},{5,7},{6,4},{7,5},{8,10},{9,11},{10,... | collective-permute-start | bytes 1191944 | tf_op jit(solution)/shard_map/ppermute | solution.py:552
  50.1 1.5 %collective-permute-start.11 = (bf16[1536,128]{1,0:T(8,128)(2,1)S(1)}, bf16[1536,128]{1,0:T(8,128)(2,1)S(1)}, u32[]{:S(2)}, u32[]{:S(2)}) collective-permute-start(bf16[1536,128]{1,0:T(8,128)(2,1)S(1)} %get-tuple-element.127), channel_id=1, source_target_pairs={{0,4},{4,0},{8,12},{12,8},{16,20},{20,16},{24,28},{28,24},{1,5},{5... | collective-permute-start | bytes 1179656 | tf_op jit(solution)/shard_map/ppermute | solution.py:552
  51.6 8.1 %collective-permute-done.11.x_ref = bf16[1536,128]{1,0:T(8,128)(2,1)S(1)} collective-permute-done((bf16[1536,128]{1,0:T(8,128)(2,1)S(1)}, bf16[1536,128]{1,0:T(8,128)(2,1)S(1)}, u32[]{:S(2)}, u32[]{:S(2)}) %collective-permute-start.11) | collective-permute-done | bytes 393248 | tf_op jit(solution)/shard_map/ppermute | solution.py:552
  59.9 1.6 %collective-permute-start.12 = (bf16[528,128]{1,0:T(8,128)(2,1)S(1)}, bf16[528,128]{1,0:T(8,128)(2,1)S(1)}, u32[]{:S(2)}, u32[]{:S(2)}) collective-permute-start(bf16[528,128]{1,0:T(8,128)(2,1)S(1)} %get-tuple-element.129.mine_ref), channel_id=1, source_target_pairs={{0,4},{4,0},{8,12},{12,8},{16,20},{20,16},{24,28},{28,24},{1,5},{5... | collective-permute-start | bytes 405512 | tf_op jit(solution)/shard_map/ppermute | solution.py:552
  61.5 1.5 %collective-permute-start.13 = (bf16[512,128]{1,0:T(8,128)(2,1)S(1)}, bf16[512,128]{1,0:T(8,128)(2,1)S(1)}, u32[]{:S(2)}, u32[]{:S(2)}) collective-permute-start(bf16[512,128]{1,0:T(8,128)(2,1)S(1)} %get-tuple-element.130), channel_id=1, source_target_pairs={{0,2},{1,3},{2,0},{3,1},{4,6},{5,7},{6,4},{7,5},{8,10},{9,11},{10,... | collective-permute-start | bytes 393224 | tf_op jit(solution)/shard_map/ppermute | solution.py:552
  62.9 0.7 collective-permute-start.7
  63.6 1.6 %collective-permute-start.17 = (bf16[256,128]{1,0:T(8,128)(2,1)S(1)}, bf16[256,128]{1,0:T(8,128)(2,1)S(1)}, u32[]{:S(2)}, u32[]{:S(2)}) collective-permute-start(bf16[256,128]{1,0:T(8,128)(2,1)S(1)} %get-tuple-element.136), channel_id=1, source_target_pairs={{0,8},{4,12},{8,0},{12,4},{16,24},{20,28},{24,16},{28,20},{1,9},{5... | collective-permute-start | bytes 196616 | tf_op jit(solution)/shard_map/ppermute | solution.py:552
  65.2 1.2 %collective-permute-done.13.y_ref = bf16[512,128]{1,0:T(8,128)(2,1)S(1)} collective-permute-done((bf16[512,128]{1,0:T(8,128)(2,1)S(1)}, bf16[512,128]{1,0:T(8,128)(2,1)S(1)}, u32[]{:S(2)}, u32[]{:S(2)}) %collective-permute-start.13) | collective-permute-done | bytes 131104 | tf_op jit(solution)/shard_map/ppermute | solution.py:552
  66.5 1.6 %collective-permute-start.14 = (bf16[288,128]{1,0:T(8,128)(2,1)S(1)}, bf16[288,128]{1,0:T(8,128)(2,1)S(1)}, u32[]{:S(2)}, u32[]{:S(2)}) collective-permute-start(bf16[288,128]{1,0:T(8,128)(2,1)S(1)} %get-tuple-element.133), channel_id=1, source_target_pairs={{0,8},{4,12},{8,0},{12,4},{16,24},{20,28},{24,16},{28,20},{1,9},{5... | collective-permute-start | bytes 221192 | tf_op jit(solution)/shard_map/ppermute | solution.py:552
  68.1 2.6 %collective-permute-start.15 = (bf16[288,128]{1,0:T(8,128)(2,1)S(1)}, bf16[288,128]{1,0:T(8,128)(2,1)S(1)}, u32[]{:S(2)}, u32[]{:S(2)}) collective-permute-start(bf16[288,128]{1,0:T(8,128)(2,1)S(1)} %get-tuple-element.134), channel_id=1, source_target_pairs={{0,16},{4,20},{8,24},{12,28},{16,0},{20,4},{24,8},{28,12},{1,17},{... | collective-permute-start | bytes 221192 | tf_op jit(solution)/shard_map/ppermute | solution.py:552
  70.9 1.7 %collective-permute-start.18 = (bf16[256,128]{1,0:T(8,128)(2,1)S(1)}, bf16[256,128]{1,0:T(8,128)(2,1)S(1)}, u32[]{:S(2)}, u32[]{:S(2)}) collective-permute-start(bf16[256,128]{1,0:T(8,128)(2,1)S(1)} %get-tuple-element.137), channel_id=1, source_target_pairs={{0,16},{4,20},{8,24},{12,28},{16,0},{20,4},{24,8},{28,12},{1,17},{... | collective-permute-start | bytes 196616 | tf_op jit(solution)/shard_map/ppermute | solution.py:552
  72.6 2.0 %collective-permute-start.19 = (bf16[256,128]{1,0:T(8,128)(2,1)S(1)}, bf16[256,128]{1,0:T(8,128)(2,1)S(1)}, u32[]{:S(2)}, u32[]{:S(2)}) collective-permute-start(bf16[256,128]{1,0:T(8,128)(2,1)S(1)} %get-tuple-element.138), channel_id=1, source_target_pairs={{0,24},{4,28},{8,16},{12,20},{16,8},{20,12},{24,0},{28,4},{1,25},{... | collective-permute-start | bytes 196616 | tf_op jit(solution)/shard_map/ppermute | solution.py:552
  74.6 1.2 %shard_map.101 = bf16[256,512]{1,0:T(8,128)(2,1)} custom-call(bf16[256,512]{1,0:T(8,128)(2,1)S(1)} %bitcast.12, bf16[256,512]{1,0:T(8,128)(2,1)S(1)} %get-tuple-element.103.refs_3_.up_ref, f32[256,512]{1,0:T(8,128)S(1)} %get-tuple-element.104.gn_ref, bf16[4640,128]{1,0:T(8,128)(2,1)S(1)} %collective-permute-done.6.pair_ref.came1_ref, ...), custom_call_target="tpu_custom_call" | custom-call | bytes 2637824 | tf_op jit(solution)/shard_map/pallas_call | solution.py:539
  75.8 7.0 %collective-permute-done.18.refs_4_ = bf16[256,128]{1,0:T(8,128)(2,1)S(1)} collective-permute-done((bf16[256,128]{1,0:T(8,128)(2,1)S(1)}, bf16[256,128]{1,0:T(8,128)(2,1)S(1)}, u32[]{:S(2)}, u32[]{:S(2)}) %collective-permute-start.18) | collective-permute-done | bytes 65568 | tf_op jit(solution)/shard_map/ppermute | solution.py:552
  82.8 0.9 %shard_map.106 = (f32[2,4,64,128]{3,2,1,0:T(8,128)}, f32[2,32,256]{2,1,0:T(8,128)}) custom-call(f32[256,128]{1,0:T(8,128)S(1)} %get-tuple-element.131.last1_ref, f32[256,128]{1,0:T(8,128)S(1)} %get-tuple-element.132.last2_ref, bf16[528,128]{1,0:T(8,128)(2,1)S(1)} %get-tuple-element.129.mine_ref, bf16[528,128]{1,0:T(8,128)(2,1)S(1)} %collective-permute-done.12.x_ref, ...), custom_call_target="tpu_custom_call" | custom-call | bytes 1277952 | tf_op jit(solution)/shard_map/pallas_call | solution.py:539
  (26 shorter events, 2.2 us)
Async XLA Ops:
  1.6 5.7 %collective-permute-start = (bf16[128,512]{1,0:T(8,128)(2,1)S(1)}, bf16[128,512]{1,0:T(8,128)(2,1)S(1)}, u32[]{:S(2)}, u32[]{:S(2)}) collective-permute-start(bf16[128,512]{1,0:T(8,128)(2,1)S(1)} %get-tuple-element.142), channel_id=1, source_target_pairs={{0,1},{1,0},{2,3},{3,2},{4,5},{5,4},{6,7},{7,6},{8,9},{9,8},{10,11... | collective-permute-start | bytes 393224 | tf_op jit(solution)/shard_map/ppermute | solution.py:552
  2.2 5.2 %collective-permute-start.1 = (bf16[128,512]{1,0:T(8,128)(2,1)S(1)}, bf16[128,512]{1,0:T(8,128)(2,1)S(1)}, u32[]{:S(2)}, u32[]{:S(2)}) collective-permute-start(bf16[128,512]{1,0:T(8,128)(2,1)S(1)} %get-tuple-element.141), channel_id=1, source_target_pairs={{1,2},{2,1},{5,6},{6,5},{9,10},{10,9},{13,14},{14,13},{17,18},{18,... | collective-permute-start | bytes 393224 | tf_op jit(solution)/shard_map/ppermute | solution.py:560
  3.5 3.9 %copy-start = (bf16[1,256,512]{2,1,0:T(8,128)(2,1)S(1)}, bf16[1,256,512]{2,1,0:T(8,128)(2,1)}, u32[]{:S(2)}) copy-start(bf16[1,256,512]{2,1,0:T(8,128)(2,1)} %param.7) | copy-start | bytes 786436
  7.4 7.2 %copy-start.1 = (bf16[1,256,512]{2,1,0:T(8,128)(2,1)S(1)}, bf16[1,256,512]{2,1,0:T(8,128)(2,1)}, u32[]{:S(2)}) copy-start(bf16[1,256,512]{2,1,0:T(8,128)(2,1)} %param.8) | copy-start | bytes 786436
  10.0 5.6 %collective-permute-start.2 = (bf16[128,512]{1,0:T(8,128)(2,1)S(1)}, bf16[128,512]{1,0:T(8,128)(2,1)S(1)}, u32[]{:S(2)}, u32[]{:S(2)}) collective-permute-start(bf16[128,512]{1,0:T(8,128)(2,1)S(1)} %get-tuple-element.80), channel_id=1, source_target_pairs={{0,1},{1,0},{2,3},{3,2},{4,5},{5,4},{6,7},{7,6},{8,9},{9,8},{10,11... | collective-permute-start | bytes 393224 | tf_op jit(solution)/shard_map/ppermute | solution.py:552
  14.0 1.6 %collective-permute-start.3 = (bf16[128,512]{1,0:T(8,128)(2,1)S(1)}, bf16[128,512]{1,0:T(8,128)(2,1)S(1)}, u32[]{:S(2)}, u32[]{:S(2)}) collective-permute-start(bf16[128,512]{1,0:T(8,128)(2,1)S(1)} %get-tuple-element.81), channel_id=1, source_target_pairs={{1,2},{2,1},{5,6},{6,5},{9,10},{10,9},{13,14},{14,13},{17,18},{18,... | collective-permute-start | bytes 393224 | tf_op jit(solution)/shard_map/ppermute | solution.py:560
  23.1 7.1 %collective-permute-start.4 = (bf16[4640,128]{1,0:T(8,128)(2,1)S(1)}, bf16[4640,128]{1,0:T(8,128)(2,1)S(1)}, u32[]{:S(2)}, u32[]{:S(2)}) collective-permute-start(bf16[4640,128]{1,0:T(8,128)(2,1)S(1)} %get-tuple-element.97), channel_id=1, source_target_pairs={{0,1},{1,0},{2,3},{3,2},{4,5},{5,4},{6,7},{7,6},{8,9},{9,8},{10,11... | collective-permute-start | bytes 3563528 | tf_op jit(solution)/shard_map/ppermute | solution.py:552
  27.7 0.8 %collective-permute-start.5 = (bf16[128,512]{1,0:T(8,128)(2,1)S(1)}, bf16[128,512]{1,0:T(8,128)(2,1)S(1)}, u32[]{:S(2)}, u32[]{:S(2)}) collective-permute-start(bf16[128,512]{1,0:T(8,128)(2,1)S(1)} %get-tuple-element.98), channel_id=1, source_target_pairs={{1,2},{2,1},{5,6},{6,5},{9,10},{10,9},{13,14},{14,13},{17,18},{18,... | collective-permute-start | bytes 393224 | tf_op jit(solution)/shard_map/ppermute | solution.py:560
  35.5 12.9 %collective-permute-start.6 = (bf16[4640,128]{1,0:T(8,128)(2,1)S(1)}, bf16[4640,128]{1,0:T(8,128)(2,1)S(1)}, u32[]{:S(2)}, u32[]{:S(2)}) collective-permute-start(bf16[4640,128]{1,0:T(8,128)(2,1)S(1)} %get-tuple-element.115), channel_id=1, source_target_pairs={{0,1},{1,0},{2,3},{3,2},{4,5},{5,4},{6,7},{7,6},{8,9},{9,8},{10,11... | collective-permute-start | bytes 3563528 | tf_op jit(solution)/shard_map/ppermute | solution.py:552
  39.6 8.3 %collective-permute-start.8 = (bf16[1024,128]{1,0:T(8,128)(2,1)S(1)}, bf16[1024,128]{1,0:T(8,128)(2,1)S(1)}, u32[]{:S(2)}, u32[]{:S(2)}) collective-permute-start(bf16[1024,128]{1,0:T(8,128)(2,1)S(1)} %get-tuple-element.121), channel_id=1, source_target_pairs={{0,2},{1,3},{2,0},{3,1},{4,6},{5,7},{6,4},{7,5},{8,10},{9,11},{10,... | collective-permute-start | bytes 786440 | tf_op jit(solution)/shard_map/ppermute | solution.py:552
  39.7 8.7 %collective-permute-start.9 = (bf16[1024,128]{1,0:T(8,128)(2,1)S(1)}, bf16[1024,128]{1,0:T(8,128)(2,1)S(1)}, u32[]{:S(2)}, u32[]{:S(2)}) collective-permute-start(bf16[1024,128]{1,0:T(8,128)(2,1)S(1)} %get-tuple-element.122), channel_id=1, source_target_pairs={{0,4},{4,0},{8,12},{12,8},{16,20},{20,16},{24,28},{28,24},{1,5},{5... | collective-permute-start | bytes 786440 | tf_op jit(solution)/shard_map/ppermute | solution.py:552
  48.7 11.0 %collective-permute-start.10 = (bf16[1552,128]{1,0:T(8,128)(2,1)S(1)}, bf16[1552,128]{1,0:T(8,128)(2,1)S(1)}, u32[]{:S(2)}, u32[]{:S(2)}) collective-permute-start(bf16[1552,128]{1,0:T(8,128)(2,1)S(1)} %get-tuple-element.126), channel_id=1, source_target_pairs={{0,2},{1,3},{2,0},{3,1},{4,6},{5,7},{6,4},{7,5},{8,10},{9,11},{10,... | collective-permute-start | bytes 1191944 | tf_op jit(solution)/shard_map/ppermute | solution.py:552
  50.1 9.6 %collective-permute-start.11 = (bf16[1536,128]{1,0:T(8,128)(2,1)S(1)}, bf16[1536,128]{1,0:T(8,128)(2,1)S(1)}, u32[]{:S(2)}, u32[]{:S(2)}) collective-permute-start(bf16[1536,128]{1,0:T(8,128)(2,1)S(1)} %get-tuple-element.127), channel_id=1, source_target_pairs={{0,4},{4,0},{8,12},{12,8},{16,20},{20,16},{24,28},{28,24},{1,5},{5... | collective-permute-start | bytes 1179656 | tf_op jit(solution)/shard_map/ppermute | solution.py:552
  59.9 6.6 %collective-permute-start.12 = (bf16[528,128]{1,0:T(8,128)(2,1)S(1)}, bf16[528,128]{1,0:T(8,128)(2,1)S(1)}, u32[]{:S(2)}, u32[]{:S(2)}) collective-permute-start(bf16[528,128]{1,0:T(8,128)(2,1)S(1)} %get-tuple-element.129.mine_ref), channel_id=1, source_target_pairs={{0,4},{4,0},{8,12},{12,8},{16,20},{20,16},{24,28},{28,24},{1,5},{5... | collective-permute-start | bytes 405512 | tf_op jit(solution)/shard_map/ppermute | solution.py:552
  61.5 5.0 %collective-permute-start.13 = (bf16[512,128]{1,0:T(8,128)(2,1)S(1)}, bf16[512,128]{1,0:T(8,128)(2,1)S(1)}, u32[]{:S(2)}, u32[]{:S(2)}) collective-permute-start(bf16[512,128]{1,0:T(8,128)(2,1)S(1)} %get-tuple-element.130), channel_id=1, source_target_pairs={{0,2},{1,3},{2,0},{3,1},{4,6},{5,7},{6,4},{7,5},{8,10},{9,11},{10,... | collective-permute-start | bytes 393224 | tf_op jit(solution)/shard_map/ppermute | solution.py:552
  62.9 8.0 %collective-permute-start.7 = (bf16[128,512]{1,0:T(8,128)(2,1)S(1)}, bf16[128,512]{1,0:T(8,128)(2,1)S(1)}, u32[]{:S(2)}, u32[]{:S(2)}) collective-permute-start(bf16[128,512]{1,0:T(8,128)(2,1)S(1)} %get-tuple-element.116), channel_id=1, source_target_pairs={{1,2},{2,1},{5,6},{6,5},{9,10},{10,9},{13,14},{14,13},{17,18},{18,... | collective-permute-start | bytes 393224 | tf_op jit(solution)/shard_map/ppermute | solution.py:560
  63.6 9.0 %collective-permute-start.17 = (bf16[256,128]{1,0:T(8,128)(2,1)S(1)}, bf16[256,128]{1,0:T(8,128)(2,1)S(1)}, u32[]{:S(2)}, u32[]{:S(2)}) collective-permute-start(bf16[256,128]{1,0:T(8,128)(2,1)S(1)} %get-tuple-element.136), channel_id=1, source_target_pairs={{0,8},{4,12},{8,0},{12,4},{16,24},{20,28},{24,16},{28,20},{1,9},{5... | collective-permute-start | bytes 196616 | tf_op jit(solution)/shard_map/ppermute | solution.py:552
  66.5 16.3 %collective-permute-start.14 = (bf16[288,128]{1,0:T(8,128)(2,1)S(1)}, bf16[288,128]{1,0:T(8,128)(2,1)S(1)}, u32[]{:S(2)}, u32[]{:S(2)}) collective-permute-start(bf16[288,128]{1,0:T(8,128)(2,1)S(1)} %get-tuple-element.133), channel_id=1, source_target_pairs={{0,8},{4,12},{8,0},{12,4},{16,24},{20,28},{24,16},{28,20},{1,9},{5... | collective-permute-start | bytes 221192 | tf_op jit(solution)/shard_map/ppermute | solution.py:552
  68.1 14.7 %collective-permute-start.15 = (bf16[288,128]{1,0:T(8,128)(2,1)S(1)}, bf16[288,128]{1,0:T(8,128)(2,1)S(1)}, u32[]{:S(2)}, u32[]{:S(2)}) collective-permute-start(bf16[288,128]{1,0:T(8,128)(2,1)S(1)} %get-tuple-element.134), channel_id=1, source_target_pairs={{0,16},{4,20},{8,24},{12,28},{16,0},{20,4},{24,8},{28,12},{1,17},{... | collective-permute-start | bytes 221192 | tf_op jit(solution)/shard_map/ppermute | solution.py:552
  70.7 12.1 %collective-permute-start.16 = (bf16[288,128]{1,0:T(8,128)(2,1)S(1)}, bf16[288,128]{1,0:T(8,128)(2,1)S(1)}, u32[]{:S(2)}, u32[]{:S(2)}) collective-permute-start(bf16[288,128]{1,0:T(8,128)(2,1)S(1)} %get-tuple-element.135), channel_id=1, source_target_pairs={{0,24},{4,28},{8,16},{12,20},{16,8},{20,12},{24,0},{28,4},{1,25},{... | collective-permute-start | bytes 221192 | tf_op jit(solution)/shard_map/ppermute | solution.py:552
  70.9 11.9 %collective-permute-start.18 = (bf16[256,128]{1,0:T(8,128)(2,1)S(1)}, bf16[256,128]{1,0:T(8,128)(2,1)S(1)}, u32[]{:S(2)}, u32[]{:S(2)}) collective-permute-start(bf16[256,128]{1,0:T(8,128)(2,1)S(1)} %get-tuple-element.137), channel_id=1, source_target_pairs={{0,16},{4,20},{8,24},{12,28},{16,0},{20,4},{24,8},{28,12},{1,17},{... | collective-permute-start | bytes 196616 | tf_op jit(solution)/shard_map/ppermute | solution.py:552
  72.6 10.2 %collective-permute-start.19 = (bf16[256,128]{1,0:T(8,128)(2,1)S(1)}, bf16[256,128]{1,0:T(8,128)(2,1)S(1)}, u32[]{:S(2)}, u32[]{:S(2)}) collective-permute-start(bf16[256,128]{1,0:T(8,128)(2,1)S(1)} %get-tuple-element.138), channel_id=1, source_target_pairs={{0,24},{4,28},{8,16},{12,20},{16,8},{20,12},{24,0},{28,4},{1,25},{... | collective-permute-start | bytes 196616 | tf_op jit(solution)/shard_map/ppermute | solution.py:552

commit v3 on v2

v3 whole, which is shorter than its diff:
```python
import functools
import math

import jax
import jax.numpy as jnp
from jax import lax
from jax.experimental import pallas as pl
from jax.experimental.pallas import tpu as pltpu
from jax.sharding import PartitionSpec as P


HEADS = 4
NOISE_FREQ = 16
LAYERS = 2
LANES = 128

epsilon = 1e-05
F32 = jnp.float32
BF16 = jnp.bfloat16
ABSENT = -1e30


def mm(left_side, right_side):
    return jnp.dot(left_side, right_side, preferred_element_type=F32)


def mm_rows(left_side, right_side):
    return lax.dot_general(
        left_side, right_side, (((0,), (0,)), ((), ())), preferred_element_type=F32
    )


def mm_cols(left_side, right_side):
    return lax.dot_general(
        left_side, right_side, (((1,), (1,)), ((), ())), preferred_element_type=F32
    )


def unit_of(states):
    values = states.astype(F32)
    centre = jnp.mean(values, axis=1, keepdims=True)
    centred = values - centre
    inverse = lax.rsqrt(jnp.mean(jnp.square(centred), axis=1, keepdims=True) + epsilon)
    return centred * inverse, inverse


def normed_of(states, film_ref, layer):
    width = states.shape[1]
    unit, _ = unit_of(states)
    scale = film_ref[layer : layer + 1, :width]
    shift = film_ref[layer : layer + 1, width:]
    return (unit * (1.0 + scale) + shift).astype(BF16)


def embedding_of(noise):
    row = lax.broadcasted_iota(jnp.int32, noise.shape, 0)
    wave = row - jnp.where(row >= NOISE_FREQ, NOISE_FREQ, 0) + 1
    angle = jnp.log(noise) * wave.astype(F32)
    return jnp.where(row < NOISE_FREQ, jnp.sin(angle), jnp.cos(angle))


def project_own(normed, w_ref, layer):
    return [mm(normed, w_ref[layer, slot]).astype(BF16) for slot in range(3)]


def put_all(refs, values):
    for ref, value in zip(refs, values, strict=True):
        ref[...] = value


def side_by_side(parts):
    return jnp.concatenate(parts, axis=1)


def halves(parity, rim):
    return parity * rim, (1 - parity) * rim


def half_rows(ref, parity, half):
    rim = ref.shape[0] // 2
    return pl.ds(pl.multiple_of(halves(parity, rim)[half], rim), rim)


def start_kernel(
    x_o_ref, x_p_ref, near_hbm, live_hbm, noise_ref, film_w_hbm, w_hbm,
    film_ref, bias_o_ref, bias_p_ref, normed_ref, q_ref, k_ref, v_ref, w_ref,
    near_ref, live_ref, film_w_ref, near_t_ref, sems,
):
    copies = [
        pltpu.make_async_copy(near_hbm, near_ref, sems.at[0]),
        pltpu.make_async_copy(live_hbm, live_ref, sems.at[1]),
        pltpu.make_async_copy(film_w_hbm, film_w_ref, sems.at[2]),
        pltpu.make_async_copy(w_hbm.at[0], w_ref.at[0], sems.at[3]),
        pltpu.make_async_copy(w_hbm.at[1:], w_ref.at[1:], sems.at[4]),
    ]
    for copy in copies:
        copy.start()
    slots, node_count = near_ref.shape
    rim = node_count // 2
    place = lax.axis_index("mesh")
    parity = lax.rem(place, 2)
    embedding = embedding_of(jnp.full((2 * NOISE_FREQ, 1), noise_ref[0], F32))
    copies[2].wait()
    for layer in range(LAYERS):
        film_ref[layer : layer + 1, :] = jnp.sum(
            embedding * film_w_ref[layer], axis=0, keepdims=True
        )
    normed_ref[:rim, :] = normed_of(x_o_ref[...], film_ref, 0)
    normed_ref[rim:, :] = normed_of(x_p_ref[...], film_ref, 0)
    copies[0].wait()
    copies[1].wait()
    near_ref[...] = jnp.where(
        live_ref[...] > 0, near_ref[...] - place * node_count, -(1 << 24)
    )
    column = lax.broadcasted_iota(jnp.int32, (1, 3 * rim), 1)
    side_o, side_p = halves(parity, rim)
    own = jnp.where(column < rim, column + side_o, column - rim + side_p)
    halo_o = column - 2 * rim + jnp.where(parity == 0, -rim, node_count)
    halo_p = column - 2 * rim + jnp.where(parity == 0, node_count, -rim)
    ids_o = jnp.where(column < node_count, own, halo_o)
    ids_p = jnp.where(column < node_count, own, halo_p)
    step = 32
    for side, ids, out_ref in ((side_o, ids_o, bias_o_ref), (side_p, ids_p, bias_p_ref)):
        near_t_ref[...] = near_ref[:, pl.ds(pl.multiple_of(side, rim), rim)].T

        def rows(index, carry, ids=ids, out_ref=out_ref):
            start = pl.multiple_of(index * step, step)
            near = near_t_ref[pl.ds(start, step), :]
            bias = jnp.full((step, 3 * rim), ABSENT, F32)
            for slot in range(slots):
                bias = jnp.where(near[:, slot : slot + 1] == ids, 0.0, bias)
            out_ref[pl.ds(start, step), :] = bias
            return carry

        lax.fori_loop(0, rim // step, rows, 0)
    copies[3].wait()
    put_all((q_ref, k_ref, v_ref), project_own(normed_ref[...], w_ref, 0))
    copies[4].wait()


def own_kernel(
    x_o_ref, x_p_ref, cot_ref, film_ref, w_ref, normed_ref, q_ref, k_ref, v_ref, ga_ref, cot2_ref
):
    parity = lax.rem(lax.axis_index("mesh"), 2)
    cot = jnp.concatenate([cot_ref[half_rows(cot_ref, parity, half), :] for half in range(2)])
    normed = normed_of(stacked(x_o_ref, x_p_ref), film_ref, 1)
    projected = project_own(normed, w_ref, 1)
    grad = mm_cols(cot, w_ref[1, 3]).astype(BF16)
    put_all((normed_ref, q_ref, k_ref, v_ref, ga_ref, cot2_ref), (normed, *projected, grad, cot))


def project_halo(halo_ref, film_ref, w_ref, layer):
    normed = normed_of(halo_ref[...], film_ref, layer)
    key = mm(normed, w_ref[layer, 1]).astype(BF16)
    value = mm(normed, w_ref[layer, 2]).astype(BF16)
    return normed, key, value


def weigh(scores, scores_h, bias, head):
    factor = 1.0 / math.sqrt(head)
    split = scores.shape[1]
    scores = scores * factor + bias[:, :split]
    scores_h = scores_h * factor + bias[:, split:]
    peak = jnp.maximum(
        jnp.max(scores, axis=1, keepdims=True), jnp.max(scores_h, axis=1, keepdims=True)
    )
    own, halo = jnp.exp(scores - peak), jnp.exp(scores_h - peak)
    total = jnp.sum(own, axis=1, keepdims=True) + jnp.sum(halo, axis=1, keepdims=True)
    return own, halo, 1.0 / total


def heads_of(width):
    head = width // HEADS
    return [slice(index * head, (index + 1) * head) for index in range(HEADS)]


def forward_kernel(
    half, x_ref, halo_ref, film_ref, q_ref, k_ref, v_ref, bias_ref, w_ref,
    next_ref, normed_h_ref, k_h_ref, v_h_ref, p_own_ref, p_halo_ref, attended_ref,
):
    rim, width = x_ref.shape
    rows = slice(half * rim, (half + 1) * rim)
    query, key, value, bias = q_ref[rows, :], k_ref[...], v_ref[...], bias_ref[...]
    heads = heads_of(width)
    scores = [mm_cols(query[:, cols], key[:, cols]) for cols in heads]
    normed, key_h, value_h = project_halo(halo_ref, film_ref, w_ref, 0)
    scores_h = [mm_cols(query[:, cols], key_h[:, cols]) for cols in heads]
    shares, parts = [], []
    for index, cols in enumerate(heads):
        own, halo, share = weigh(scores[index], scores_h[index], bias, width // HEADS)
        own, halo = (own * share).astype(BF16), (halo * share).astype(BF16)
        shares.append((own, halo))
        parts.append((mm(own, value[:, cols]) + mm(halo, value_h[:, cols])).astype(BF16))
    attended = side_by_side(parts)
    states = (x_ref[...].astype(F32) + mm(attended, w_ref[0, 3])).astype(BF16)
    put_all(
        (next_ref, normed_h_ref, k_h_ref, v_h_ref, attended_ref),
        (states, normed, key_h, value_h, attended),
    )
    for index, (own, halo) in enumerate(shares):
        p_own_ref[index] = own
        p_halo_ref[index] = halo


def head_backward(own, halo, own16, halo16, probs, probs_h, share, grad, query, key, key_h):
    middle = jnp.sum(own * probs, axis=1, keepdims=True) + jnp.sum(
        halo * probs_h, axis=1, keepdims=True
    )
    factor = 1.0 / math.sqrt(query.shape[1])
    if share is not None:
        middle, factor = middle * share, share * factor
    scores = (own * ((probs - middle) * factor)).astype(BF16)
    scores_h = (halo * ((probs_h - middle) * factor)).astype(BF16)
    return (
        (mm(scores, key) + mm(scores_h, key_h)).astype(BF16),
        mm_rows(scores, query),
        mm_rows(own16, grad),
        mm_rows(scores_h, query).astype(BF16),
        mm_rows(halo16, grad).astype(BF16),
    )


def joined(parts, before, kind):
    gq, gk, gv, gk_h, gv_h = [side_by_side(part) for part in zip(*parts, strict=True)]
    if before:
        gk, gv = gk + before[0][...], gv + before[1][...]
    return gq, gk.astype(kind), gv.astype(kind), gk_h, gv_h


def last_layer_kernel(half, halo_ref, film_ref, q_ref, k_ref, v_ref, ga_ref, bias_ref, w_ref, *refs):
    before = refs[:2] if half == 0 else ()
    normed_h_ref, attended_ref, *outs = refs[len(before) :]
    rim, width = halo_ref.shape
    rows = slice(half * rim, (half + 1) * rim)
    query, key, value, bias = q_ref[rows, :], k_ref[...], v_ref[...], bias_ref[...]
    grad = ga_ref[rows, :]
    heads = heads_of(width)
    scores = [mm_cols(query[:, cols], key[:, cols]) for cols in heads]
    probs = [mm_cols(grad[:, cols], value[:, cols]) for cols in heads]
    normed, key_h, value_h = project_halo(halo_ref, film_ref, w_ref, 1)
    scores_h = [mm_cols(query[:, cols], key_h[:, cols]) for cols in heads]
    probs_h = [mm_cols(grad[:, cols], value_h[:, cols]) for cols in heads]
    attended, parts = [], []
    for index, cols in enumerate(heads):
        own, halo, share = weigh(scores[index], scores_h[index], bias, width // HEADS)
        own16, halo16 = (own * share).astype(BF16), (halo * share).astype(BF16)
        attended.append((mm(own16, value[:, cols]) + mm(halo16, value_h[:, cols])).astype(BF16))
        parts.append(
            head_backward(
                own, halo, own16, halo16, probs[index], probs_h[index], share,
                grad[:, cols], query[:, cols], key[:, cols], key_h[:, cols],
            )
        )
    results = joined(parts, before, outs[1].dtype)
    if half == 0:
        results += (halo_grads(w_ref, 1, *results[3:]).astype(BF16),)
    put_all((normed_h_ref, attended_ref, *outs), (normed, side_by_side(attended), *results))


def halo_grads(w_ref, layer, gk_h, gv_h):
    return mm_cols(gk_h, w_ref[layer, 1]) + mm_cols(gv_h, w_ref[layer, 2])


def grads_kernel(
    plan, layer, x_o_ref, x_p_ref, halo_o_ref, halo_p_ref, gq_o_ref, gq_p_ref, gk_ref, gv_ref,
    gk_h_ref, gv_h_ref, to_other_ref, w_ref, cond2_ref, gn_ref, to_pair_ref, cond_ref, *film_refs,
):
    rim, width = x_o_ref.shape
    grad_p = halo_grads(w_ref, layer, gk_h_ref[...], gv_h_ref[...])
    grad_own = mm_cols(gk_ref[...], w_ref[layer, 1]) + mm_cols(gv_ref[...], w_ref[layer, 2])
    grads = [to_other_ref[...].astype(F32), grad_p]
    for half, gq_ref in enumerate((gq_o_ref, gq_p_ref)):
        rows = slice(half * rim, (half + 1) * rim)
        grads.append(mm_cols(gq_ref[...], w_ref[layer, 0]) + grad_own[rows])
    scaled = jnp.zeros((1, width), F32)
    plain = jnp.zeros((1, width), F32)
    for grad, ref in zip(grads, (halo_o_ref, halo_p_ref, x_o_ref, x_p_ref)):
        scaled += jnp.sum(grad * unit_of(ref[...])[0], axis=0, keepdims=True)
        plain += jnp.sum(grad, axis=0, keepdims=True)
    to_pair_ref[...] = grad_p.astype(BF16)
    gn_ref[:rim, :], gn_ref[rim:, :] = grads[2:]
    cond_ref[:, :width] = scaled
    cond_ref[:, width:] = plain
    if not film_refs:
        return
    keep_ref, send_ref, scratch_ref = film_refs
    part_rows = plan.film_rows // LAYERS
    mesh = lax.axis_index("mesh")
    for core in range(2):
        for y in range(2):
            col = lax.bitwise_xor(mesh, y * 2 + core) * (part_rows * LANES)
            for layer_index, ref in enumerate((cond_ref, cond2_ref)):
                for part in range(part_rows):
                    start = pl.multiple_of(col + part * LANES, LANES)
                    row = layer_index * part_rows + part
                    out_ref = scratch_ref if core else keep_ref
                    out_ref[y, row : row + 1, :] = ref[:, pl.ds(start, LANES)]
    for y in range(2):
        put_pair(
            scratch_ref[y], send_ref.at[y * plan.film : y * plan.film + 2 * plan.film_rows, :]
        )


def upstream_of(states, up, grad, film_ref, layer):
    width = states.shape[1]
    unit, inverse = unit_of(states)
    grad = grad * (1.0 + film_ref[layer : layer + 1, :width])
    centred = (
        grad
        - jnp.mean(grad, axis=1, keepdims=True)
        - unit * jnp.mean(grad * unit, axis=1, keepdims=True)
    )
    return (up.astype(F32) + inverse * centred).astype(BF16)


def first_layer_kernel(
    half, next_ref, cot_ref, gn2_ref, back_ref, film_ref, q_ref, k_ref, v_ref, k_h_ref, v_h_ref,
    p_own_ref, p_halo_ref, w_ref, *refs,
):
    before = refs[:2] if half == 0 else ()
    up_ref, *outs = refs[len(before) :]
    rim, width = next_ref.shape
    rows = slice(half * rim, (half + 1) * rim)
    total = gn2_ref[rows, :] + back_ref[...].astype(F32)
    up = upstream_of(next_ref[...], cot_ref[rows, :], total, film_ref, 1)
    grad = mm_cols(up, w_ref[0, 3]).astype(BF16)
    query, key, value = q_ref[rows, :], k_ref[...], v_ref[...]
    key_h, value_h = k_h_ref[...], v_h_ref[...]
    heads = heads_of(width)
    probs = [mm_cols(grad[:, cols], value[:, cols]) for cols in heads]
    probs_h = [mm_cols(grad[:, cols], value_h[:, cols]) for cols in heads]
    parts = []
    for index, cols in enumerate(heads):
        own16, halo16 = p_own_ref[index], p_halo_ref[index]
        parts.append(
            head_backward(
                own16.astype(F32), halo16.astype(F32), own16, halo16, probs[index], probs_h[index],
                None, grad[:, cols], query[:, cols], key[:, cols], key_h[:, cols],
            )
        )
    results = joined(parts, before, outs[1].dtype)
    if half == 0:
        results += (halo_grads(w_ref, 0, *results[3:]).astype(BF16),)
    put_all((up_ref, *outs), (up, *results))


def end_kernel(
    x_o_ref, x_p_ref, up_o_ref, up_p_ref, gn_ref, back_o_ref, back_p_ref, film_ref, out_ref
):
    parity = lax.rem(lax.axis_index("mesh"), 2)
    rim = x_o_ref.shape[0]
    total = gn_ref[...] + stacked(back_o_ref, back_p_ref).astype(F32)
    grad = upstream_of(stacked(x_o_ref, x_p_ref), stacked(up_o_ref, up_p_ref), total, film_ref, 0)
    for half in range(2):
        out_ref[half_rows(out_ref, parity, half), :] = grad[half * rim : (half + 1) * rim]


def stacked(*refs):
    return jnp.concatenate([ref[...] for ref in refs], axis=0)


def weight_products(
    normed_ref, normed_o_ref, normed_p_ref, attended_o_ref, attended_p_ref, up_o_ref, up_p_ref,
    gq_o_ref, gq_p_ref, gk_ref, gk_o_ref, gk_p_ref, gv_ref, gv_o_ref, gv_p_ref, put,
):
    put(3, mm_rows(stacked(attended_o_ref, attended_p_ref), stacked(up_o_ref, up_p_ref)))
    put(0, mm_rows(normed_ref[...], stacked(gq_o_ref, gq_p_ref)))
    normed = stacked(normed_ref, normed_o_ref, normed_p_ref)
    put(1, mm_rows(normed, stacked(gk_ref, gk_o_ref, gk_p_ref)))
    put(2, mm_rows(normed, stacked(gv_ref, gv_o_ref, gv_p_ref)))


def plain_weight_kernel(*refs):
    *ins, out_ref = refs

    def put(slot, value):
        out_ref[slot] = value

    weight_products(*ins, put)


def put_pair(value, out_ref):
    high = value.astype(BF16)
    rows = value.shape[0]
    out_ref[:rows, :] = high
    out_ref[rows:, :] = (value - high.astype(F32)).astype(BF16)


def get_pair(in_ref):
    rows = in_ref.shape[0] // 2
    return in_ref[:rows, :].astype(F32) + in_ref[rows:, :].astype(F32)


def get_noise(in_ref, start):
    parts = [in_ref[start + row : start + row + 1, :].astype(F32) for row in range(3)]
    return (parts[0] + parts[1]) + parts[2]


def put_noise(value, out_ref, start):
    for row in range(3):
        part = value.astype(BF16)
        out_ref[start + row : start + row + 1, :] = part
        value = value - part.astype(F32)


def split_weight_kernel(plan, *refs):
    *ins, send_ref, keep_ref, total_ref = refs

    def put(slot, value):
        total_ref[slot] = value

    weight_products(*ins, put)
    rows = plan.rows // 2
    ens, mesh = lax.axis_index("ens"), lax.axis_index("mesh")
    for slot in range(4):
        group, inner = slot // 2, slot % 2
        for core in range(2):
            for y in range(2):
                col = lax.bitwise_xor(mesh, y * 2 + core)
                cols = pl.ds(pl.multiple_of(col * LANES, LANES), LANES)
                for x in range(2):
                    for z in range(plan.deep):
                        row = lax.bitwise_xor(ens, z * 2 + x)
                        at = pl.ds(pl.multiple_of(row * rows, rows), rows)
                        piece = total_ref[slot, at, cols]
                        first, second = (y, x) if group == 0 else (x, y)
                        start = plan.at(group, first, second, z) + inner * rows
                        if core:
                            send_ref[start : start + rows, :] = piece.astype(BF16)
                        else:
                            keep_ref[start : start + rows, :] = piece


def stage_one(plan, keep_ref, came_ref, y_ref, x_ref, kept_ref):
    size = plan.weights // 4
    for group, out_ref in ((0, y_ref), (1, x_ref)):
        start = 2 * group * size
        kept_ref[group * size : (group + 1) * size, :] = keep_ref[
            start : start + size, :
        ] + came_ref[start : start + size, :].astype(F32)
        start += size
        out_ref[:size, :] = (
            keep_ref[start : start + size, :] + came_ref[start : start + size, :].astype(F32)
        ).astype(BF16)


def stage_two(plan, kept_ref, y_ref, x_ref, y_base, x_base, to_x_ref, to_y_ref, next_ref):
    size = plan.weights // 8
    for group, in_ref, base, out_ref in ((0, y_ref, y_base, to_x_ref), (1, x_ref, x_base, to_y_ref)):
        start = 2 * group * size
        next_ref[group * size : (group + 1) * size, :] = kept_ref[
            start : start + size, :
        ] + in_ref[base : base + size, :].astype(F32)
        out_ref[...] = (
            kept_ref[start + size : start + 2 * size, :]
            + in_ref[base + size : base + 2 * size, :].astype(F32)
        ).astype(BF16)


def stage_three(plan, kept_ref, x_ref, y_ref, x_base, y_base, z_refs, last_ref):
    rows = plan.rows
    for group, in_ref, base in ((0, x_ref, x_base), (1, y_ref, y_base)):
        for z in range(plan.deep):
            start = (group * plan.deep + z) * rows
            value = kept_ref[start : start + rows, :] + in_ref[
                base + z * rows : base + (z + 1) * rows, :
            ].astype(F32)
            if z:
                z_refs[z - 1][group * rows : (group + 1) * rows, :] = value.astype(BF16)
            else:
                last_ref[group * rows : (group + 1) * rows, :] = value


def start_scatter_kernel(plan, keep_ref, came_ref, y_ref, x_ref, kept_ref):
    stage_one(plan, keep_ref, came_ref, y_ref, x_ref, kept_ref)


def slot_a_kernel(
    plan, keep1_ref, film1_ref, came1_ref, film_came_ref, kept2_ref, y2_ref, x2_ref,
    y_ref, x_ref, kept1_ref, next2_ref, film_ref,
):
    size, small = plan.weights // 4, plan.weights // 8
    stage_one(plan, keep1_ref, came1_ref, y_ref, x_ref, kept1_ref)
    stage_two(
        plan, kept2_ref, y2_ref, x2_ref, 0, 0,
        x_ref.at[size : size + small, :], y_ref.at[size : size + small, :], next2_ref,
    )
    end = 2 * plan.film_rows
    film_ref[...] = film1_ref[0] + get_pair(film_came_ref.at[:end, :])
    put_pair(
        film1_ref[1] + get_pair(film_came_ref.at[plan.film : plan.film + end, :]),
        y_ref.at[size + small : size + small + end, :],
    )


def slot_b_kernel(
    plan, kept1_ref, kept2_ref, film_ref, y_ref, x_ref, noise_ref, *outs,
):
    to_x_ref, to_y_ref, next1_ref, last2_ref, *z_refs = outs
    size, small = plan.weights // 4, plan.weights // 8
    stage_two(
        plan, kept1_ref, y_ref, x_ref, 0, 0, to_x_ref.at[:small, :], to_y_ref.at[:small, :], next1_ref
    )
    stage_three(plan, kept2_ref, x_ref, y_ref, size, size, z_refs, last2_ref)
    end = 2 * plan.film_rows
    start = size + small
    total = film_ref[...] + get_pair(y_ref.at[start : start + end, :])
    put_pair(total, to_x_ref.at[small : small + end, :])
    put_noise(jnp.full((1, LANES), noise_ref[0], F32), to_x_ref, small + end)


def slot_c_kernel(plan, kept1_ref, x_ref, y_ref, mine_ref, *outs):
    last1_ref, *z_refs = outs
    stage_three(plan, kept1_ref, x_ref, y_ref, 0, 0, z_refs, last1_ref)
    small, end = plan.weights // 8, 2 * plan.rows
    for z_ref in z_refs:
        z_ref[end : end + plan.film, :] = mine_ref[small : small + plan.film, :]
        z_ref[end + plan.film :, :] = x_ref[small : small + plan.film, :]


def finish_kernel(plan, last1_ref, last2_ref, mine_ref, x_ref, *refs):
    count = plan.deep - 1
    z1_refs, z2_refs, (out_ref, film_ref) = refs[:count], refs[count : 2 * count], refs[2 * count :]
    for layer, (last_ref, z_refs) in enumerate(((last1_ref, z1_refs), (last2_ref, z2_refs))):
        rows = plan.rows // 2
        for slot in range(4):
            at = slice(slot * rows, (slot + 1) * rows)
            total = last_ref[at, :]
            for z_ref in z_refs:
                total = total + z_ref[at, :].astype(F32)
            out_ref[layer, slot] = total
    small, end = plan.weights // 8, 2 * plan.rows
    packs = [ref.at[small : small + plan.film, :] for ref in (mine_ref, x_ref)]
    for z_ref in z1_refs:
        packs += [z_ref.at[end + i * plan.film : end + (i + 1) * plan.film, :] for i in range(2)]
    lane = lax.broadcasted_iota(jnp.int32, (1, LANES), 1)
    noise = jnp.ones((1, LANES), F32)
    pair = 2 * plan.film_rows
    for member, pack in enumerate(packs):
        noise = jnp.where(lane == member, get_noise(pack, pair), noise)
    embedding = embedding_of(jnp.broadcast_to(noise, (2 * NOISE_FREQ, LANES)))
    members = [get_pair(pack.at[:pair, :]) for pack in packs]
    half = plan.film_rows // LAYERS
    for layer in range(LAYERS):
        for part in range(half):
            row = layer * half + part
            total = jnp.zeros((2 * NOISE_FREQ, LANES), F32)
            for member, value in enumerate(members):
                total += embedding[:, member : member + 1] * value[row : row + 1, :]
            film_ref[layer, :, part * LANES : (part + 1) * LANES] = total


def film_kernel(rows_ref, out_ref):
    members, _, columns = rows_ref.shape
    rows = rows_ref[...]
    lane = lax.broadcasted_iota(jnp.int32, (1, LANES), 1)
    noise = jnp.ones((1, LANES), F32)
    for member in range(members):
        noise = jnp.where(lane == member, rows[member, LAYERS:, :1], noise)
    embedding = embedding_of(jnp.broadcast_to(noise, (2 * NOISE_FREQ, LANES)))
    for layer in range(LAYERS):
        total = jnp.zeros((2 * NOISE_FREQ, columns), F32)
        for member in range(members):
            total += embedding[:, member : member + 1] * rows[member, layer : layer + 1, :]
        out_ref[layer] = total


def whole():
    return pl.BlockSpec(memory_space=pltpu.VMEM)


def apart():
    return pl.BlockSpec(memory_space=pltpu.HBM)


def call(kernel, args, outs, scratch=(), flops=0, specs=None, limit=10 << 20, sems=()):
    moved = sum(a.size * a.dtype.itemsize for a in args)
    moved += sum(math.prod(shape) * jnp.dtype(kind).itemsize for shape, kind in outs)
    return pl.pallas_call(
        kernel,
        out_shape=[jax.ShapeDtypeStruct(shape, kind) for shape, kind in outs],
        in_specs=specs or [whole() for _ in args],
        out_specs=[whole() for _ in outs],
        scratch_shapes=[pltpu.VMEM(shape, kind) for shape, kind in scratch] + list(sems),
        compiler_params=pltpu.CompilerParams(vmem_limit_bytes=limit),
        cost_estimate=pl.CostEstimate(flops=flops, bytes_accessed=moved, transcendentals=0),
    )(*args)


def swap(block, axis, bit):
    count = lax.axis_size(axis)
    return lax.ppermute(block, axis, [(i, i ^ bit) for i in range(count)])


def exchange_other(to_other):
    count = lax.axis_size("mesh")
    route = []
    for i in range(1, count - 1, 2):
        route += [(i, i + 1), (i + 1, i)]
    return lax.ppermute(to_other, "mesh", route)


def exchange(to_pair, to_other):
    other = exchange_other(to_other)
    return swap(to_pair, "mesh", 1), other


class Plan:
    def __init__(self, width, ens_count, mesh_count):
        self.deep = ens_count // 2
        self.rows = 2 * width // ens_count
        self.weights = 8 * self.deep * self.rows
        self.film_rows = LAYERS * (2 * width // mesh_count) // LANES
        self.film = 16 * pl.cdiv(2 * self.film_rows + 3, 16)

    def at(self, group, first, second, z):
        return (((group * 2 + first) * 2 + second) * self.deep + z) * self.rows


def film_pieces(conds, noise_level, mesh_count):
    mesh = lax.axis_index("mesh")
    rows = jnp.concatenate(conds, axis=0)
    width = rows.shape[1] // mesh_count
    pieces = rows.reshape(LAYERS, mesh_count, width).transpose(1, 0, 2)
    pieces = jnp.take(pieces, lax.bitwise_xor(jnp.arange(mesh_count), mesh), axis=0)
    noise = jnp.where(jnp.arange(mesh_count) == 0, noise_level[0], 0.0)
    noise = jnp.broadcast_to(noise[:, None, None], (mesh_count, 1, width))
    return jnp.concatenate([pieces, noise], axis=1)


def film_mesh_step(pieces, bit):
    pieces = pieces.reshape(-1, 2, *pieces.shape[1:])
    return pieces[:, 0] + swap(pieces[:, 1], "mesh", bit)


def film_ens_step(rows, bit):
    return jnp.concatenate([rows, swap(rows, "ens", bit)])


def film_end(rows):
    shape = (LAYERS, 2 * NOISE_FREQ, rows.shape[2])
    return call(film_kernel, (rows,), [(shape, F32)])[0]


def bits_of(count):
    return [1 << index for index in range(count.bit_length() - 1)]


def bind(kernel, *settings):
    return functools.partial(kernel, *settings)


def body(inputs, cotangent, noise_level, neighbours, live_slots, projections, film_weights):
    states, cot = inputs[0], cotangent[0]
    nodes, width = states.shape
    rim = nodes // 2
    mesh_count, ens_count = lax.axis_size("mesh"), lax.axis_size("ens")
    side_o, side_p = halves(lax.rem(lax.axis_index("mesh"), 2), rim)
    square = 2 * nodes * width * width
    split = mesh_count == 4 and width % (mesh_count * LANES) == 0 and ens_count % 2 == 0
    plan = Plan(width, ens_count, mesh_count) if split else None

    def full(kind=BF16):
        return ((nodes, width), kind)

    def part(kind=BF16):
        return ((rim, width), kind)

    def block(rows, kind=BF16):
        return ((rows, LANES), kind)

    def hbm(value):
        return pltpu.with_memory_space_constraint(value, pltpu.HBM)

    smem = pl.BlockSpec(memory_space=pltpu.SMEM)
    cond_shape = ((1, 2 * width), F32)
    x_o = lax.dynamic_slice_in_dim(states, side_o, rim)
    x_p = lax.dynamic_slice_in_dim(states, side_p, rim)
    halo_p, halo_o = exchange(x_p, x_o)
    slots = neighbours.shape[1]
    film, bias_o, bias_p, normed1, q1, k1, v1, projections = call(
        start_kernel,
        (x_o, x_p, hbm(neighbours.T), hbm(live_slots.T), noise_level, hbm(film_weights),
         hbm(projections)),
        [((LAYERS, 2 * width), F32)] + [((rim, 3 * rim), F32)] * 2 + [full()] * 4
        + [(projections.shape, BF16)],
        scratch=[((slots, nodes), jnp.int32), ((slots, nodes), jnp.int32),
                 (film_weights.shape, F32), ((rim, slots), jnp.int32)],
        sems=[pltpu.SemaphoreType.DMA((5,))], flops=3 * square,
        specs=[whole()] * 2 + [apart()] * 2 + [smem] + [apart()] * 2,
    )
    probs_shapes = [((HEADS, rim, nodes), BF16), ((HEADS, rim, rim), BF16)]

    def forward(half, x, halo, bias):
        return call(
            bind(forward_kernel, half), (x, halo, film, q1, k1, v1, bias, projections),
            [part()] * 4 + probs_shapes + [part()], flops=2 * square,
        )

    next_o, normed1_o, k1_o, v1_o, own_o, over_o, attended1_o = forward(0, x_o, halo_o, bias_o)
    halo2_o = exchange_other(next_o)
    next_p, normed1_p, k1_p, v1_p, own_p, over_p, attended1_p = forward(1, x_p, halo_p, bias_p)
    halo2_p = swap(next_p, "mesh", 1)
    normed2, q2, k2, v2, ga2, cot2 = call(
        own_kernel, (next_o, next_p, cot, film, projections), [full()] * 6, flops=4 * square
    )

    def last(half, halo, bias, parts):
        grads = [part(), full(F32), full(F32)] if half else [part(), full(), full()]
        return call(
            bind(last_layer_kernel, half),
            (halo, film, q2, k2, v2, ga2, bias, projections, *parts),
            [part()] * 2 + grads + [part()] * (2 if half else 3),
            flops=4 * square,
        )

    normed2_p, attended2_p, gq2_p, *parts, gk2_p, gv2_p = last(1, halo2_p, bias_p, ())
    normed2_o, attended2_o, gq2_o, gk2, gv2, gk2_o, gv2_o, to_other = last(
        0, halo2_o, bias_o, parts
    )
    back_o = exchange_other(to_other)
    gn2, to_pair, cond2 = call(
        bind(grads_kernel, None, 1),
        (next_o, next_p, halo2_o, halo2_p, gq2_o, gq2_p, gk2, gv2, gk2_p, gv2_p, to_other,
         projections, film),
        [full(F32), part(), cond_shape], flops=4 * square,
    )
    back_p = swap(to_pair, "mesh", 1)

    def weight_grads(*args):
        if not split:
            return call(plain_weight_kernel, args, [((4, width, width), F32)], flops=6 * square)
        return call(
            bind(split_weight_kernel, plan), args,
            [block(plan.weights), block(plan.weights, F32)],
            scratch=[((4, width, width), F32)], flops=6 * square,
        )

    weights2 = weight_grads(
        normed2, normed2_o, normed2_p, attended2_o, attended2_p, cot2[:rim], cot2[rim:],
        gq2_o, gq2_p, gk2, gk2_o, gk2_p, gv2, gv2_o, gv2_p,
    )
    if split:
        sums = plan.weights
        came = swap(weights2[0], "mesh", 1)
        to_y, to_x, kept2 = call(
            bind(start_scatter_kernel, plan), (weights2[1], came),
            [block(sums // 4)] * 2 + [block(sums // 2, F32)],
        )
        y2, x2 = swap(to_y, "mesh", 2), swap(to_x, "ens", 1)

    def first(half, nxt, back, k_h, v_h, own, over, parts):
        grads = [part(), full(F32), full(F32)] if half else [part(), full(), full()]
        return call(
            bind(first_layer_kernel, half),
            (nxt, cot2, gn2, back, film, q1, k1, v1, k_h, v_h, own, over, projections, *parts),
            [part()] + grads + [part()] * (2 if half else 3),
            flops=4 * square,
        )

    up_p, gq1_p, *parts, gk1_p, gv1_p = first(1, next_p, back_p, k1_p, v1_p, own_p, over_p, ())
    up_o, gq1_o, gk1, gv1, gk1_o, gv1_o, to_other = first(
        0, next_o, back_o, k1_o, v1_o, own_o, over_o, parts
    )
    weights1 = weight_grads(
        normed1, normed1_o, normed1_p, attended1_o, attended1_p, up_o, up_p,
        gq1_o, gq1_p, gk1, gk1_o, gk1_p, gv1, gv1_o, gv1_p,
    )
    film_shapes = []
    if split:
        came = swap(weights1[0], "mesh", 1)
        film_shapes = [((2, plan.film_rows, LANES), F32), block(2 * plan.film)]
    back_o = exchange_other(to_other)
    gn1, to_pair, cond1, *film_parts = call(
        bind(grads_kernel, plan, 0),
        (x_o, x_p, halo_o, halo_p, gq1_o, gq1_p, gk1, gv1, gk1_p, gv1_p, to_other,
         projections, cond2),
        [full(F32), part(), cond_shape] + film_shapes,
        scratch=film_shapes[:1], flops=4 * square,
    )
    back_p = swap(to_pair, "mesh", 1)
    grad_input = call(end_kernel, (x_o, x_p, up_o, up_p, gn1, back_o, back_p, film), [full()])[0]
    if split:
        film_came = swap(film_parts[1], "mesh", 1)
        to_y, to_x, kept1, kept2, film_mine = call(
            bind(slot_a_kernel, plan),
            (weights1[1], film_parts[0], came, film_came, kept2, y2, x2),
            [block(sums // 4 + sums // 8 + plan.film), block(sums // 4 + sums // 8),
             block(sums // 2, F32), block(sums // 4, F32), block(plan.film_rows, F32)],
        )
        came_y, came_x = swap(to_y, "mesh", 2), swap(to_x, "ens", 1)
        others = range(1, plan.deep)
        to_x, to_y, kept1, last2, *to_z = call(
            bind(slot_b_kernel, plan),
            (kept1, kept2, film_mine, came_y, came_x, noise_level),
            [block(sums // 8 + plan.film), block(sums // 8), block(sums // 4, F32),
             block(2 * plan.rows, F32)] + [block(2 * plan.rows) for _ in others],
            specs=[whole()] * 5 + [smem],
        )
        came_x, came_y = swap(to_x, "ens", 1), swap(to_y, "mesh", 2)
        came_z2 = [swap(to_z[z - 1], "ens", 2 * z) for z in others]
        last1, *to_z = call(
            bind(slot_c_kernel, plan), (kept1, came_x, came_y, to_x),
            [block(2 * plan.rows, F32)] + [block(2 * plan.rows + 2 * plan.film) for _ in others],
        )
        came_z1 = [swap(to_z[z - 1], "ens", 2 * z) for z in others]
        weight_out, film_out = call(
            bind(finish_kernel, plan),
            (last1, last2, to_x, came_x, *came_z1, *came_z2),
            [((LAYERS, 4, width // ens_count, LANES), F32),
             ((LAYERS, 2 * NOISE_FREQ, 2 * width // mesh_count), F32)],
        )
    else:
        film_rows = film_pieces((cond1, cond2), noise_level, mesh_count)
        for bit in bits_of(mesh_count):
            film_rows = film_mesh_step(film_rows, bit)
        for bit in bits_of(ens_count):
            film_rows = film_ens_step(film_rows, bit)
        film_out = film_end(film_rows)
        total = jnp.stack([weights1[0], weights2[0]]).astype(BF16)
        total = lax.psum_scatter(total, "ens", scatter_dimension=2, tiled=True)
        weight_out = lax.psum_scatter(total, "mesh", scatter_dimension=3, tiled=True).astype(F32)
    return (grad_input[None], weight_out, film_out)


def solution(mesh):
    placed = (
        P("ens", "mesh", None),
        P("ens", "mesh", None),
        P("ens"),
        P("mesh", None),
        P("mesh", None),
        P(),
        P(),
    )
    return jax.shard_map(
        body,
        mesh=mesh,
        in_specs=placed,
        out_specs=(P("ens", "mesh", None), P(None, None, "ens", "mesh"), P(None, None, "mesh")),
        check_vma=False,
    )
```

time: 84 us -> 79.6 us (0.948)
  waiting for transfers between devices: 24.7 us -> 21.2 us
    ppermute x16 -> x19, waiting for transfers between devices: 24.7 us -> 21.2 us  [swap(): return lax.ppermute(block, axis, [(i, i ^ bit) for i in range(count)])]
    ppermute x16 -> x19, starting transfers between devices: 30.7 us -> 29.9 us  [swap(): return lax.ppermute(block, axis, [(i, i ^ bit) for i in range(count)])]
    pallas_call x13 -> x18, Pallas kernels: 23.1 us -> 22.9 us  [call(): pl.pallas_call(kernel, out_shape=[jax.ShapeDtypeStruct(shape, kind) for s...]
  transfers between devices with their start and end apart: 20 -> 23, of which waited for: 6 -> 5; matrix products, arithmetic and copies ran while one was open for 0% -> 0% of each run, Pallas kernels for 8% -> 23%
where the time goes in v3:
time: 79.6 us; the launch traced here: 79.4 us
  starting transfers between devices  32.7 us (41%)
  Pallas kernels  22.9 us (29%)
  waiting for transfers between devices  21.2 us (27%)
  between operations  1.5 us (2%)
  local copies, waits for them, and re-layouts  1.02 us (1%)
    ppermute x19, starting transfers between devices, swap(): return lax.ppermute(block, axis, [(i, i ^ bit) for i in range(count)])  29.9 us
    pallas_call x18, Pallas kernels, call(): pl.pallas_call(kernel, out_shape=[jax.ShapeDtypeStruct(shape, kind) for s...  22.9 us
    ppermute x19, waiting for transfers between devices, swap(): return lax.ppermute(block, axis, [(i, i ^ bit) for i in range(count)])  21.2 us
    ppermute x4, starting transfers between devices, exchange_other(): return lax.ppermute(to_other, 'mesh', route)  2.83 us
  transfers between devices with their start and end apart: 23, of which 5 were waited for; matrix products, arithmetic and copies ran while one was open for 0% of the time, Pallas kernels for 23%

profile of v3, /device:TPU:0, one launch (start us, length us, event | category | flops | bytes accessed | tf_op | source)
XLA Modules:
  0.0 79.4 jit_solution(3961025403849129990)
XLA Ops:
  0.6 1.0 %dynamic-slice_bitcast_fusion = (bf16[128,512]{1,0:T(8,128)(2,1)S(1)}, bf16[128,512]{1,0:T(8,128)(2,1)S(1)}) fusion(bf16[1,256,512]{2,1,0:T(8,128)(2,1)} %param.7, s32[]{:T(128)S(6)} %select_n.7, s32[]{:T(128)S(6)} %select_n.6), kind=kLoop, calls=%fused_computation | loop fusion | bytes 524296 | tf_op jit(solution)/shard_map/dynamic_slice | solution.py:678
  2.3 4.4 %collective-permute-start.1 = (bf16[128,512]{1,0:T(8,128)(2,1)S(1)}, bf16[128,512]{1,0:T(8,128)(2,1)S(1)}, u32[]{:S(2)}, u32[]{:S(2)}) collective-permute-start(bf16[128,512]{1,0:T(8,128)(2,1)S(1)} %get-tuple-element.181.x_p_ref.x_ref), channel_id=1, source_target_pairs={{0,1},{1,0},{2,3},{3,2},{4,5},{5,4},{6,7},{7,6},{8,9},{9,8},{10,11... | collective-permute-start | bytes 393224 | tf_op jit(solution)/shard_map/ppermute | solution.py:592
  7.4 4.1 %shard_map.94 = (f32[2,1024]{1,0:T(2,128)S(1)}, f32[128,384]{1,0:T(8,128)S(1)}, f32[128,384]{1,0:T(8,128)S(1)}, bf16[256,512]{1,0:T(8,128)(2,1)S(1)}, bf16[256,5...) custom-call(bf16[128,512]{1,0:T(8,128)(2,1)S(1)} %get-tuple-element., ...), custom_call_target="tpu_custom_call" | custom-call | flops 402653184 | bytes 10428420 | tf_op jit(solution)/shard_map/pallas_call | solution.py:579
  11.5 1.2 %shard_map.95 = (bf16[128,512]{1,0:T(8,128)(2,1)S(1)}, bf16[128,512]{1,0:T(8,128)(2,1)S(1)}, bf16[128,512]{1,0:T(8,128)(2,1)S(1)}, bf16[128,512]{1,0:T(8,128)(2,...) custom-call(bf16[128,512]{1,0:T(8,128)(2,1)S(1)} %get-tuple-element.182.x_o, ...), custom_call_target="tpu_custom_call" | custom-call | flops 268435456 | bytes 6496256 | tf_op jit(solution)/shard_map/pallas_call | solution.py:579
  13.4 1.2 %shard_map.96 = (bf16[128,512]{1,0:T(8,128)(2,1)S(1)}, bf16[128,512]{1,0:T(8,128)(2,1)S(1)}, bf16[128,512]{1,0:T(8,128)(2,1)S(1)}, bf16[128,512]{1,0:T(8,128)(2,...) custom-call(bf16[128,512]{1,0:T(8,128)(2,1)S(1)} %get-tuple-element.181.x_p, ...), custom_call_target="tpu_custom_call" | custom-call | flops 268435456 | bytes 6496256 | tf_op jit(solution)/shard_map/pallas_call | solution.py:579
  14.6 1.3 %collective-permute-start.3 = (bf16[128,512]{1,0:T(8,128)(2,1)S(1)}, bf16[128,512]{1,0:T(8,128)(2,1)S(1)}, u32[]{:S(2)}, u32[]{:S(2)}) collective-permute-start(bf16[128,512]{1,0:T(8,128)(2,1)S(1)} %get-tuple-element.99.x_p_ref.next_ref), channel_id=1, source_target_pairs={{0,1},{1,0},{2,3},{3,2},{4,5},{5,4},{6,7},{7,6},{8,9},{9,8},{10,11... | collective-permute-start | bytes 393224 | tf_op jit(solution)/shard_map/ppermute | solution.py:592
  16.9 1.7 %shard_map.98 = (bf16[128,512]{1,0:T(8,128)(2,1)S(1)}, bf16[128,512]{1,0:T(8,128)(2,1)S(1)}, bf16[128,512]{1,0:T(8,128)(2,1)S(1)}, f32[256,512]{1,0:T(8,128)S(1)...) custom-call(bf16[128,512]{1,0:T(8,128)(2,1)S(1)} %collective-permute-done.3.halo_ref.halo_p_ref, ...), custom_call_target="tpu_custom_call" | custom-call | flops 536870912 | bytes 7282688 | tf_op jit(solution)/shard_map/pallas_call | solution.py:579
  18.6 2.0 %shard_map.99 = (bf16[128,512]{1,0:T(8,128)(2,1)S(1)}, bf16[128,512]{1,0:T(8,128)(2,1)S(1)}, bf16[128,512]{1,0:T(8,128)(2,1)S(1)}, bf16[256,512]{1,0:T(8,128)(2,...) custom-call(bf16[128,512]{1,0:T(8,128)(2,1)S(1)} %collective-permute, ...), custom_call_target="tpu_custom_call" | custom-call | flops 536870912 | bytes 7938048 | tf_op jit(solution)/shard_map/pallas_call | solution.py:579
  20.6 1.2 %shard_map.100 = (f32[256,512]{1,0:T(8,128)S(1)}, bf16[128,512]{1,0:T(8,128)(2,1)S(1)}, f32[1,1024]{1,0:T(1,128)S(1)}) custom-call(bf16[128,512]{1,0:T(8,128)(2,1)S(1)} %get-tuple-element.97.x_o_ref.next_ref, bf16[128,512]{1,0:T(8,128)(2,1)S(1)} %get-tuple-element.99.x_p_ref.next_ref, bf16[128,512]{1,0:T(8,128)(2,1)S(1)} %collective-permute-done.2.halo_ref.halo_o_ref, ...), custom_call_target="tpu_custom_call" | custom-call | flops 536870912 | bytes 6565888 | tf_op jit(solution)/shard_map/pallas_call | solution.py:579
  22.3 1.6 %shard_map.106 = (bf16[4096,128]{1,0:T(8,128)(2,1)S(1)}, f32[4096,128]{1,0:T(8,128)S(1)}) custom-call(bf16[256,512]{1,0:T(8,128)(2,1)S(1)} %get-tuple-element.149.refs_0_, bf16[128,512]{1,0:T(8,128)(2,1)S(1)} %get-tuple-element.150.refs_1_, bf16[128,512]{1,0:T(8,128)(2,1)S(1)} %get-tuple-element.151.refs_2_, ...), custom_call_target="tpu_custom_call" | custom-call | flops 805306368 | bytes 5505024 | tf_op jit(solution)/shard_map/pallas_call | solution.py:579
  24.8 1.4 %shard_map.101 = (bf16[128,512]{1,0:T(8,128)(2,1)S(1)}, bf16[128,512]{1,0:T(8,128)(2,1)S(1)}, f32[256,512]{1,0:T(8,128)S(1)}, f32[256,512]{1,0:T(8,128)S(1)}, bf...) custom-call(bf16[128,512]{1,0:T(8,128)(2,1)S(1)} %get-tuple-element.99.x_p_ref.next_ref, ...), custom_call_target="tpu_custom_call" | custom-call | flops 536870912 | bytes 8265728 | tf_op jit(solution)/shard_map/pallas_call | solution.py:579
  26.2 1.7 %shard_map.102 = (bf16[128,512]{1,0:T(8,128)(2,1)S(1)}, bf16[128,512]{1,0:T(8,128)(2,1)S(1)}, bf16[256,512]{1,0:T(8,128)(2,1)S(1)}, bf16[256,512]{1,0:T(8,128)(2...) custom-call(bf16[128,512]{1,0:T(8,128)(2,1)S(1)} %get-tuple-element.97.x_o_ref.nex, ...), custom_call_target="tpu_custom_call" | custom-call | flops 536870912 | bytes 8921088 | tf_op jit(solution)/shard_map/pallas_call | solution.py:579
  28.0 1.6 %shard_map.105 = (bf16[4096,128]{1,0:T(8,128)(2,1)S(1)}, f32[4096,128]{1,0:T(8,128)S(1)}) custom-call(bf16[256,512]{1,0:T(8,128)(2,1)S(1)} %get-tuple-element.138.refs_0_, bf16[128,512]{1,0:T(8,128)(2,1)S(1)} %get-tuple-element.139.refs_1_, bf16[128,512]{1,0:T(8,128)(2,1)S(1)} %get-tuple-element.140.refs_2_, ...), custom_call_target="tpu_custom_call" | custom-call | flops 805306368 | bytes 5505024 | tf_op jit(solution)/shard_map/pallas_call | solution.py:579
  29.5 4.5 %collective-permute-start.8 = (bf16[4096,128]{1,0:T(8,128)(2,1)S(1)}, bf16[4096,128]{1,0:T(8,128)(2,1)S(1)}, u32[]{:S(2)}, u32[]{:S(2)}) collective-permute-start(bf16[4096,128]{1,0:T(8,128)(2,1)S(1)} %get-tuple-element.147), channel_id=1, source_target_pairs={{0,1},{1,0},{2,3},{3,2},{4,5},{5,4},{6,7},{7,6},{8,9},{9,8},{10,11... | collective-permute-start | bytes 3145736 | tf_op jit(solution)/shard_map/ppermute | solution.py:592
  34.2 1.6 %collective-permute-start.11 = (bf16[1024,128]{1,0:T(8,128)(2,1)S(1)}, bf16[1024,128]{1,0:T(8,128)(2,1)S(1)}, u32[]{:S(2)}, u32[]{:S(2)}) collective-permute-start(bf16[1024,128]{1,0:T(8,128)(2,1)S(1)} %get-tuple-element.159), channel_id=1, source_target_pairs={{0,2},{1,3},{2,0},{3,1},{4,6},{5,7},{6,4},{7,5},{8,10},{9,11},{10,... | collective-permute-start | bytes 786440 | tf_op jit(solution)/shard_map/ppermute | solution.py:592
  35.8 1.5 %collective-permute-start.12 = (bf16[1024,128]{1,0:T(8,128)(2,1)S(1)}, bf16[1024,128]{1,0:T(8,128)(2,1)S(1)}, u32[]{:S(2)}, u32[]{:S(2)}) collective-permute-start(bf16[1024,128]{1,0:T(8,128)(2,1)S(1)} %get-tuple-element.160), channel_id=1, source_target_pairs={{0,4},{4,0},{8,12},{12,8},{16,20},{20,16},{24,28},{28,24},{1,5},{5... | collective-permute-start | bytes 786440 | tf_op jit(solution)/shard_map/ppermute | solution.py:592
  37.3 1.7 %shard_map.103 = (f32[256,512]{1,0:T(8,128)S(1)}, bf16[128,512]{1,0:T(8,128)(2,1)S(1)}, f32[1,1024]{1,0:T(1,128)}, f32[2,4,128]{2,1,0:T(4,128)S(1)}, bf16[32,128]{1,0:T(8,128)(2,1)S(1)}) custom-call(bf16[128,512]{1,0:T(8,128)(2,1)S(1)} %get-tuple-element.182.x_o_ref.x_ref, bf16[128,512]{1,0:T(8,128)(2,1)S(1)} %get-tuple-element.181.x_p_ref.x_ref, ...), custom_call_target="tpu_custom_call" | custom-call | flops 536870912 | bytes 6574080 | tf_op jit(solution)/shard_map/pallas_call | solution.py:579
  39.1 1.2 %collective-permute-done.9.film_came_ref = bf16[32,128]{1,0:T(8,128)(2,1)S(1)} collective-permute-done((bf16[32,128]{1,0:T(8,128)(2,1)S(1)}, bf16[32,128]{1,0:T(8,128)(2,1)S(1)}, u32[]{:S(2)}, u32[]{:S(2)}) %collective-permute-start.9) | collective-permute-done | bytes 8224 | tf_op jit(solution)/shard_map/ppermute | solution.py:592
  40.3 2.5 %collective-permute-done.11.y2_ref = bf16[1024,128]{1,0:T(8,128)(2,1)S(1)} collective-permute-done((bf16[1024,128]{1,0:T(8,128)(2,1)S(1)}, bf16[1024,128]{1,0:T(8,128)(2,1)S(1)}, u32[]{:S(2)}, u32[]{:S(2)}) %collective-permute-start.11) | collective-permute-done | bytes 262176 | tf_op jit(solution)/shard_map/ppermute | solution.py:592
  42.8 1.5 %collective-permute-done.12.x2_ref = bf16[1024,128]{1,0:T(8,128)(2,1)S(1)} collective-permute-done((bf16[1024,128]{1,0:T(8,128)(2,1)S(1)}, bf16[1024,128]{1,0:T(8,128)(2,1)S(1)}, u32[]{:S(2)}, u32[]{:S(2)}) %collective-permute-start.12) | collective-permute-done | bytes 262176 | tf_op jit(solution)/shard_map/ppermute | solution.py:592
  45.0 1.5 %collective-permute-start.14 = (bf16[1536,128]{1,0:T(8,128)(2,1)S(1)}, bf16[1536,128]{1,0:T(8,128)(2,1)S(1)}, u32[]{:S(2)}, u32[]{:S(2)}) collective-permute-start(bf16[1536,128]{1,0:T(8,128)(2,1)S(1)} %get-tuple-element.165), channel_id=1, source_target_pairs={{0,4},{4,0},{8,12},{12,8},{16,20},{20,16},{24,28},{28,24},{1,5},{5... | collective-permute-start | bytes 1179656 | tf_op jit(solution)/shard_map/ppermute | solution.py:592
  46.5 8.8 %collective-permute-done.14.x_ref = bf16[1536,128]{1,0:T(8,128)(2,1)S(1)} collective-permute-done((bf16[1536,128]{1,0:T(8,128)(2,1)S(1)}, bf16[1536,128]{1,0:T(8,128)(2,1)S(1)}, u32[]{:S(2)}, u32[]{:S(2)}) %collective-permute-start.14) | collective-permute-done | bytes 393248 | tf_op jit(solution)/shard_map/ppermute | solution.py:592
  55.5 1.6 %collective-permute-start.15 = (bf16[528,128]{1,0:T(8,128)(2,1)S(1)}, bf16[528,128]{1,0:T(8,128)(2,1)S(1)}, u32[]{:S(2)}, u32[]{:S(2)}) collective-permute-start(bf16[528,128]{1,0:T(8,128)(2,1)S(1)} %get-tuple-element.167.mine_ref), channel_id=1, source_target_pairs={{0,4},{4,0},{8,12},{12,8},{16,20},{20,16},{24,28},{28,24},{1,5},{5... | collective-permute-start | bytes 405512 | tf_op jit(solution)/shard_map/ppermute | solution.py:592
  57.0 1.5 %collective-permute-start.16 = (bf16[512,128]{1,0:T(8,128)(2,1)S(1)}, bf16[512,128]{1,0:T(8,128)(2,1)S(1)}, u32[]{:S(2)}, u32[]{:S(2)}) collective-permute-start(bf16[512,128]{1,0:T(8,128)(2,1)S(1)} %get-tuple-element.168), channel_id=1, source_target_pairs={{0,2},{1,3},{2,0},{3,1},{4,6},{5,7},{6,4},{7,5},{8,10},{9,11},{10,... | collective-permute-start | bytes 393224 | tf_op jit(solution)/shard_map/ppermute | solution.py:592
  59.2 2.0 %collective-permute-start.7 = (bf16[128,512]{1,0:T(8,128)(2,1)S(1)}, bf16[128,512]{1,0:T(8,128)(2,1)S(1)}, u32[]{:S(2)}, u32[]{:S(2)}) collective-permute-start(bf16[128,512]{1,0:T(8,128)(2,1)S(1)} %get-tuple-element.137), channel_id=1, source_target_pairs={{0,1},{1,0},{2,3},{3,2},{4,5},{5,4},{6,7},{7,6},{8,9},{9,8},{10,11... | collective-permute-start | bytes 393224 | tf_op jit(solution)/shard_map/ppermute | solution.py:592
  61.1 1.6 %collective-permute-start.20 = (bf16[256,128]{1,0:T(8,128)(2,1)S(1)}, bf16[256,128]{1,0:T(8,128)(2,1)S(1)}, u32[]{:S(2)}, u32[]{:S(2)}) collective-permute-start(bf16[256,128]{1,0:T(8,128)(2,1)S(1)} %get-tuple-element.174), channel_id=1, source_target_pairs={{0,8},{4,12},{8,0},{12,4},{16,24},{20,28},{24,16},{28,20},{1,9},{5... | collective-permute-start | bytes 196616 | tf_op jit(solution)/shard_map/ppermute | solution.py:592
  63.7 2.6 %collective-permute-start.18 = (bf16[288,128]{1,0:T(8,128)(2,1)S(1)}, bf16[288,128]{1,0:T(8,128)(2,1)S(1)}, u32[]{:S(2)}, u32[]{:S(2)}) collective-permute-start(bf16[288,128]{1,0:T(8,128)(2,1)S(1)} %get-tuple-element.172), channel_id=1, source_target_pairs={{0,16},{4,20},{8,24},{12,28},{16,0},{20,4},{24,8},{28,12},{1,17},{... | collective-permute-start | bytes 221192 | tf_op jit(solution)/shard_map/ppermute | solution.py:592
  66.3 1.0 %collective-permute-start.19 = (bf16[288,128]{1,0:T(8,128)(2,1)S(1)}, bf16[288,128]{1,0:T(8,128)(2,1)S(1)}, u32[]{:S(2)}, u32[]{:S(2)}) collective-permute-start(bf16[288,128]{1,0:T(8,128)(2,1)S(1)} %get-tuple-element.173), channel_id=1, source_target_pairs={{0,24},{4,28},{8,16},{12,20},{16,8},{20,12},{24,0},{28,4},{1,25},{... | collective-permute-start | bytes 221192 | tf_op jit(solution)/shard_map/ppermute | solution.py:592
  67.2 1.7 %collective-permute-start.21 = (bf16[256,128]{1,0:T(8,128)(2,1)S(1)}, bf16[256,128]{1,0:T(8,128)(2,1)S(1)}, u32[]{:S(2)}, u32[]{:S(2)}) collective-permute-start(bf16[256,128]{1,0:T(8,128)(2,1)S(1)} %get-tuple-element.175), channel_id=1, source_target_pairs={{0,16},{4,20},{8,24},{12,28},{16,0},{20,4},{24,8},{28,12},{1,17},{... | collective-permute-start | bytes 196616 | tf_op jit(solution)/shard_map/ppermute | solution.py:592
  68.9 1.3 %collective-permute-start.22 = (bf16[256,128]{1,0:T(8,128)(2,1)S(1)}, bf16[256,128]{1,0:T(8,128)(2,1)S(1)}, u32[]{:S(2)}, u32[]{:S(2)}) collective-permute-start(bf16[256,128]{1,0:T(8,128)(2,1)S(1)} %get-tuple-element.176), channel_id=1, source_target_pairs={{0,24},{4,28},{8,16},{12,20},{16,8},{20,12},{24,0},{28,4},{1,25},{... | collective-permute-start | bytes 196616 | tf_op jit(solution)/shard_map/ppermute | solution.py:592
  70.2 1.1 %shard_map.104 = bf16[256,512]{1,0:T(8,128)(2,1)} custom-call(bf16[128,512]{1,0:T(8,128)(2,1)S(1)} %get-tuple-element.182.x_o_ref.x_ref, bf16[128,512]{1,0:T(8,128)(2,1)S(1)} %get-tuple-element.181.x_p_ref.x_ref, bf16[128,512]{1,0:T(8,128)(2,1)S(1)} %get-tuple-element.126.up_o_ref.refs_5_, bf16[128,512]{1,0:T(8,128)(2,1)S(1)} %get-tuple-element.127.up_p_ref.refs_6_, ...), custom_call_target="tpu_custom_call" | custom-call | bytes 1581056 | tf_op jit(solution)/shard_map/pallas_call | solution.py:579
  71.3 7.2 %collective-permute-done.21.refs_4_ = bf16[256,128]{1,0:T(8,128)(2,1)S(1)} collective-permute-done((bf16[256,128]{1,0:T(8,128)(2,1)S(1)}, bf16[256,128]{1,0:T(8,128)(2,1)S(1)}, u32[]{:S(2)}, u32[]{:S(2)}) %collective-permute-start.21) | collective-permute-done | bytes 65568 | tf_op jit(solution)/shard_map/ppermute | solution.py:592
  (36 shorter events, 7.5 us)
Async XLA Ops:
  1.6 9.9 %collective-permute-start = (bf16[128,512]{1,0:T(8,128)(2,1)S(1)}, bf16[128,512]{1,0:T(8,128)(2,1)S(1)}, u32[]{:S(2)}, u32[]{:S(2)}) collective-permute-start(bf16[128,512]{1,0:T(8,128)(2,1)S(1)} %get-tuple-element.182.x_o_ref.x_ref), channel_id=1, source_target_pairs={{1,2},{2,1},{5,6},{6,5},{9,10},{10,9},{13,14},{14,13},{17,18},{18,... | collective-permute-start | bytes 393224 | tf_op jit(solution)/shard_map/ppermute | solution.py:600
  2.3 11.1 %collective-permute-start.1 = (bf16[128,512]{1,0:T(8,128)(2,1)S(1)}, bf16[128,512]{1,0:T(8,128)(2,1)S(1)}, u32[]{:S(2)}, u32[]{:S(2)}) collective-permute-start(bf16[128,512]{1,0:T(8,128)(2,1)S(1)} %get-tuple-element.181.x_p_ref.x_ref), channel_id=1, source_target_pairs={{0,1},{1,0},{2,3},{3,2},{4,5},{5,4},{6,7},{7,6},{8,9},{9,8},{10,11... | collective-permute-start | bytes 393224 | tf_op jit(solution)/shard_map/ppermute | solution.py:592
  11.5 4.4 %copy-start = (bf16[1,256,512]{2,1,0:T(8,128)(2,1)S(1)}, bf16[1,256,512]{2,1,0:T(8,128)(2,1)}, u32[]{:S(2)}) copy-start(bf16[1,256,512]{2,1,0:T(8,128)(2,1)} %param.8) | copy-start | bytes 786436
  12.7 5.8 %collective-permute-start.2 = (bf16[128,512]{1,0:T(8,128)(2,1)S(1)}, bf16[128,512]{1,0:T(8,128)(2,1)S(1)}, u32[]{:S(2)}, u32[]{:S(2)}) collective-permute-start(bf16[128,512]{1,0:T(8,128)(2,1)S(1)} %get-tuple-element.97.x_o_ref.next_ref), channel_id=1, source_target_pairs={{1,2},{2,1},{5,6},{6,5},{9,10},{10,9},{13,14},{14,13},{17,18},{18,... | collective-permute-start | bytes 393224 | tf_op jit(solution)/shard_map/ppermute | solution.py:600
  14.6 2.3 %collective-permute-start.3 = (bf16[128,512]{1,0:T(8,128)(2,1)S(1)}, bf16[128,512]{1,0:T(8,128)(2,1)S(1)}, u32[]{:S(2)}, u32[]{:S(2)}) collective-permute-start(bf16[128,512]{1,0:T(8,128)(2,1)S(1)} %get-tuple-element.99.x_p_ref.next_ref), channel_id=1, source_target_pairs={{0,1},{1,0},{2,3},{3,2},{4,5},{5,4},{6,7},{7,6},{8,9},{9,8},{10,11... | collective-permute-start | bytes 393224 | tf_op jit(solution)/shard_map/ppermute | solution.py:592
  21.8 3.1 %collective-permute-start.5 = (bf16[128,512]{1,0:T(8,128)(2,1)S(1)}, bf16[128,512]{1,0:T(8,128)(2,1)S(1)}, u32[]{:S(2)}, u32[]{:S(2)}) collective-permute-start(bf16[128,512]{1,0:T(8,128)(2,1)S(1)} %get-tuple-element.119), channel_id=1, source_target_pairs={{0,1},{1,0},{2,3},{3,2},{4,5},{5,4},{6,7},{7,6},{8,9},{9,8},{10,11... | collective-permute-start | bytes 393224 | tf_op jit(solution)/shard_map/ppermute | solution.py:592
  23.8 10.2 %collective-permute-start.10 = (bf16[4096,128]{1,0:T(8,128)(2,1)S(1)}, bf16[4096,128]{1,0:T(8,128)(2,1)S(1)}, u32[]{:S(2)}, u32[]{:S(2)}) collective-permute-start(bf16[4096,128]{1,0:T(8,128)(2,1)S(1)} %get-tuple-element.157), channel_id=1, source_target_pairs={{0,1},{1,0},{2,3},{3,2},{4,5},{5,4},{6,7},{7,6},{8,9},{9,8},{10,11... | collective-permute-start | bytes 3145736 | tf_op jit(solution)/shard_map/ppermute | solution.py:592
  24.0 2.3 %collective-permute-start.4 = (bf16[128,512]{1,0:T(8,128)(2,1)S(1)}, bf16[128,512]{1,0:T(8,128)(2,1)S(1)}, u32[]{:S(2)}, u32[]{:S(2)}) collective-permute-start(bf16[128,512]{1,0:T(8,128)(2,1)S(1)} %get-tuple-element.113.to_other_ref), channel_id=1, source_target_pairs={{1,2},{2,1},{5,6},{6,5},{9,10},{10,9},{13,14},{14,13},{17,18},{18,... | collective-permute-start | bytes 393224 | tf_op jit(solution)/shard_map/ppermute | solution.py:600
  29.5 10.7 %collective-permute-start.8 = (bf16[4096,128]{1,0:T(8,128)(2,1)S(1)}, bf16[4096,128]{1,0:T(8,128)(2,1)S(1)}, u32[]{:S(2)}, u32[]{:S(2)}) collective-permute-start(bf16[4096,128]{1,0:T(8,128)(2,1)S(1)} %get-tuple-element.147), channel_id=1, source_target_pairs={{0,1},{1,0},{2,3},{3,2},{4,5},{5,4},{6,7},{7,6},{8,9},{9,8},{10,11... | collective-permute-start | bytes 3145736 | tf_op jit(solution)/shard_map/ppermute | solution.py:592
  34.2 8.6 %collective-permute-start.11 = (bf16[1024,128]{1,0:T(8,128)(2,1)S(1)}, bf16[1024,128]{1,0:T(8,128)(2,1)S(1)}, u32[]{:S(2)}, u32[]{:S(2)}) collective-permute-start(bf16[1024,128]{1,0:T(8,128)(2,1)S(1)} %get-tuple-element.159), channel_id=1, source_target_pairs={{0,2},{1,3},{2,0},{3,1},{4,6},{5,7},{6,4},{7,5},{8,10},{9,11},{10,... | collective-permute-start | bytes 786440 | tf_op jit(solution)/shard_map/ppermute | solution.py:592
  35.8 8.4 %collective-permute-start.12 = (bf16[1024,128]{1,0:T(8,128)(2,1)S(1)}, bf16[1024,128]{1,0:T(8,128)(2,1)S(1)}, u32[]{:S(2)}, u32[]{:S(2)}) collective-permute-start(bf16[1024,128]{1,0:T(8,128)(2,1)S(1)} %get-tuple-element.160), channel_id=1, source_target_pairs={{0,4},{4,0},{8,12},{12,8},{16,20},{20,16},{24,28},{28,24},{1,5},{5... | collective-permute-start | bytes 786440 | tf_op jit(solution)/shard_map/ppermute | solution.py:592
  39.1 1.2 %collective-permute-start.9 = (bf16[32,128]{1,0:T(8,128)(2,1)S(1)}, bf16[32,128]{1,0:T(8,128)(2,1)S(1)}, u32[]{:S(2)}, u32[]{:S(2)}) collective-permute-start(bf16[32,128]{1,0:T(8,128)(2,1)S(1)} %get-tuple-element.148), channel_id=1, source_target_pairs={{0,1},{1,0},{2,3},{3,2},{4,5},{5,4},{6,7},{7,6},{8,9},{9,8},{10,11... | collective-permute-start | bytes 24584 | tf_op jit(solution)/shard_map/ppermute | solution.py:592
  44.6 10.7 %collective-permute-start.13 = (bf16[1552,128]{1,0:T(8,128)(2,1)S(1)}, bf16[1552,128]{1,0:T(8,128)(2,1)S(1)}, u32[]{:S(2)}, u32[]{:S(2)}) collective-permute-start(bf16[1552,128]{1,0:T(8,128)(2,1)S(1)} %get-tuple-element.164), channel_id=1, source_target_pairs={{0,2},{1,3},{2,0},{3,1},{4,6},{5,7},{6,4},{7,5},{8,10},{9,11},{10,... | collective-permute-start | bytes 1191944 | tf_op jit(solution)/shard_map/ppermute | solution.py:592
  45.0 10.3 %collective-permute-start.14 = (bf16[1536,128]{1,0:T(8,128)(2,1)S(1)}, bf16[1536,128]{1,0:T(8,128)(2,1)S(1)}, u32[]{:S(2)}, u32[]{:S(2)}) collective-permute-start(bf16[1536,128]{1,0:T(8,128)(2,1)S(1)} %get-tuple-element.165), channel_id=1, source_target_pairs={{0,4},{4,0},{8,12},{12,8},{16,20},{20,16},{24,28},{28,24},{1,5},{5... | collective-permute-start | bytes 1179656 | tf_op jit(solution)/shard_map/ppermute | solution.py:592
  55.5 7.3 %collective-permute-start.15 = (bf16[528,128]{1,0:T(8,128)(2,1)S(1)}, bf16[528,128]{1,0:T(8,128)(2,1)S(1)}, u32[]{:S(2)}, u32[]{:S(2)}) collective-permute-start(bf16[528,128]{1,0:T(8,128)(2,1)S(1)} %get-tuple-element.167.mine_ref), channel_id=1, source_target_pairs={{0,4},{4,0},{8,12},{12,8},{16,20},{20,16},{24,28},{28,24},{1,5},{5... | collective-permute-start | bytes 405512 | tf_op jit(solution)/shard_map/ppermute | solution.py:592
  57.0 5.7 %collective-permute-start.16 = (bf16[512,128]{1,0:T(8,128)(2,1)S(1)}, bf16[512,128]{1,0:T(8,128)(2,1)S(1)}, u32[]{:S(2)}, u32[]{:S(2)}) collective-permute-start(bf16[512,128]{1,0:T(8,128)(2,1)S(1)} %get-tuple-element.168), channel_id=1, source_target_pairs={{0,2},{1,3},{2,0},{3,1},{4,6},{5,7},{6,4},{7,5},{8,10},{9,11},{10,... | collective-permute-start | bytes 393224 | tf_op jit(solution)/shard_map/ppermute | solution.py:592
  58.5 7.8 %collective-permute-start.6 = (bf16[128,512]{1,0:T(8,128)(2,1)S(1)}, bf16[128,512]{1,0:T(8,128)(2,1)S(1)}, u32[]{:S(2)}, u32[]{:S(2)}) collective-permute-start(bf16[128,512]{1,0:T(8,128)(2,1)S(1)} %get-tuple-element.134.to_other_ref), channel_id=1, source_target_pairs={{1,2},{2,1},{5,6},{6,5},{9,10},{10,9},{13,14},{14,13},{17,18},{18,... | collective-permute-start | bytes 393224 | tf_op jit(solution)/shard_map/ppermute | solution.py:600
  59.2 8.1 %collective-permute-start.7 = (bf16[128,512]{1,0:T(8,128)(2,1)S(1)}, bf16[128,512]{1,0:T(8,128)(2,1)S(1)}, u32[]{:S(2)}, u32[]{:S(2)}) collective-permute-start(bf16[128,512]{1,0:T(8,128)(2,1)S(1)} %get-tuple-element.137), channel_id=1, source_target_pairs={{0,1},{1,0},{2,3},{3,2},{4,5},{5,4},{6,7},{7,6},{8,9},{9,8},{10,11... | collective-permute-start | bytes 393224 | tf_op jit(solution)/shard_map/ppermute | solution.py:592
  61.1 7.8 %collective-permute-start.20 = (bf16[256,128]{1,0:T(8,128)(2,1)S(1)}, bf16[256,128]{1,0:T(8,128)(2,1)S(1)}, u32[]{:S(2)}, u32[]{:S(2)}) collective-permute-start(bf16[256,128]{1,0:T(8,128)(2,1)S(1)} %get-tuple-element.174), channel_id=1, source_target_pairs={{0,8},{4,12},{8,0},{12,4},{16,24},{20,28},{24,16},{28,20},{1,9},{5... | collective-permute-start | bytes 196616 | tf_op jit(solution)/shard_map/ppermute | solution.py:592
  62.8 15.7 %collective-permute-start.17 = (bf16[288,128]{1,0:T(8,128)(2,1)S(1)}, bf16[288,128]{1,0:T(8,128)(2,1)S(1)}, u32[]{:S(2)}, u32[]{:S(2)}) collective-permute-start(bf16[288,128]{1,0:T(8,128)(2,1)S(1)} %get-tuple-element.171), channel_id=1, source_target_pairs={{0,8},{4,12},{8,0},{12,4},{16,24},{20,28},{24,16},{28,20},{1,9},{5... | collective-permute-start | bytes 221192 | tf_op jit(solution)/shard_map/ppermute | solution.py:592
  63.7 14.8 %collective-permute-start.18 = (bf16[288,128]{1,0:T(8,128)(2,1)S(1)}, bf16[288,128]{1,0:T(8,128)(2,1)S(1)}, u32[]{:S(2)}, u32[]{:S(2)}) collective-permute-start(bf16[288,128]{1,0:T(8,128)(2,1)S(1)} %get-tuple-element.172), channel_id=1, source_target_pairs={{0,16},{4,20},{8,24},{12,28},{16,0},{20,4},{24,8},{28,12},{1,17},{... | collective-permute-start | bytes 221192 | tf_op jit(solution)/shard_map/ppermute | solution.py:592
  66.3 12.2 %collective-permute-start.19 = (bf16[288,128]{1,0:T(8,128)(2,1)S(1)}, bf16[288,128]{1,0:T(8,128)(2,1)S(1)}, u32[]{:S(2)}, u32[]{:S(2)}) collective-permute-start(bf16[288,128]{1,0:T(8,128)(2,1)S(1)} %get-tuple-element.173), channel_id=1, source_target_pairs={{0,24},{4,28},{8,16},{12,20},{16,8},{20,12},{24,0},{28,4},{1,25},{... | collective-permute-start | bytes 221192 | tf_op jit(solution)/shard_map/ppermute | solution.py:592
  67.2 11.3 %collective-permute-start.21 = (bf16[256,128]{1,0:T(8,128)(2,1)S(1)}, bf16[256,128]{1,0:T(8,128)(2,1)S(1)}, u32[]{:S(2)}, u32[]{:S(2)}) collective-permute-start(bf16[256,128]{1,0:T(8,128)(2,1)S(1)} %get-tuple-element.175), channel_id=1, source_target_pairs={{0,16},{4,20},{8,24},{12,28},{16,0},{20,4},{24,8},{28,12},{1,17},{... | collective-permute-start | bytes 196616 | tf_op jit(solution)/shard_map/ppermute | solution.py:592
  68.9 9.6 %collective-permute-start.22 = (bf16[256,128]{1,0:T(8,128)(2,1)S(1)}, bf16[256,128]{1,0:T(8,128)(2,1)S(1)}, u32[]{:S(2)}, u32[]{:S(2)}) collective-permute-start(bf16[256,128]{1,0:T(8,128)(2,1)S(1)} %get-tuple-element.176), channel_id=1, source_target_pairs={{0,24},{4,28},{8,16},{12,20},{16,8},{20,12},{24,0},{28,4},{1,25},{... | collective-permute-start | bytes 196616 | tf_op jit(solution)/shard_map/ppermute | solution.py:592

commit v4 on v3

--- a/solution.py
+++ b/solution.py
@@ -15,6 +15,8 @@
 LANES = 128
 
 epsilon = 1e-05
+
+ENS, MESH = "ens", "mesh"
 F32 = jnp.float32
 BF16 = jnp.bfloat16
 ABSENT = -1e30
@@ -52,8 +54,8 @@
     return (unit * (1.0 + scale) + shift).astype(BF16)
 
 
-def embedding_of(noise):
-    row = lax.broadcasted_iota(jnp.int32, noise.shape, 0)
+def embedding_of(noise, axis):
+    row = lax.broadcasted_iota(jnp.int32, noise.shape, axis)
     wave = row - jnp.where(row >= NOISE_FREQ, NOISE_FREQ, 0) + 1
     angle = jnp.log(noise) * wave.astype(F32)
     return jnp.where(row < NOISE_FREQ, jnp.sin(angle), jnp.cos(angle))
@@ -81,67 +83,82 @@
     return pl.ds(pl.multiple_of(halves(parity, rim)[half], rim), rim)
 
 
+def load_kernel(
+    x_hbm, near_hbm, live_hbm, film_w_hbm, noise_ref,
+    x_o_ref, x_p_ref, near_ref, live_ref, film_w_ref, row_ref, sems,
+):
+    parity = lax.rem(lax.axis_index(MESH), 2)
+    copies = [
+        pltpu.make_async_copy(x_hbm.at[half_rows(x_hbm, parity, 0), :], x_o_ref, sems.at[0]),
+        pltpu.make_async_copy(x_hbm.at[half_rows(x_hbm, parity, 1), :], x_p_ref, sems.at[1]),
+        pltpu.make_async_copy(near_hbm, near_ref, sems.at[2]),
+        pltpu.make_async_copy(live_hbm, live_ref, sems.at[3]),
+        pltpu.make_async_copy(film_w_hbm, film_w_ref, sems.at[4]),
+    ]
+    for copy in copies:
+        copy.start()
+    row_ref[...] = embedding_of(jnp.full(row_ref.shape, noise_ref[0], F32), 1)
+    for copy in copies:
+        copy.wait()
+
+
 def start_kernel(
-    x_o_ref, x_p_ref, near_hbm, live_hbm, noise_ref, film_w_hbm, w_hbm,
+    x_o_ref, x_p_ref, near_ref, live_ref, row_ref, film_w_ref, w_hbm,
     film_ref, bias_o_ref, bias_p_ref, normed_ref, q_ref, k_ref, v_ref, w_ref,
-    near_ref, live_ref, film_w_ref, near_t_ref, sems,
+    near_t_ref, sems,
 ):
     copies = [
-        pltpu.make_async_copy(near_hbm, near_ref, sems.at[0]),
-        pltpu.make_async_copy(live_hbm, live_ref, sems.at[1]),
-        pltpu.make_async_copy(film_w_hbm, film_w_ref, sems.at[2]),
-        pltpu.make_async_copy(w_hbm.at[0], w_ref.at[0], sems.at[3]),
-        pltpu.make_async_copy(w_hbm.at[1:], w_ref.at[1:], sems.at[4]),
+        pltpu.make_async_copy(w_hbm.at[0], w_ref.at[0], sems.at[0]),
+        pltpu.make_async_copy(w_hbm.at[1:], w_ref.at[1:], sems.at[1]),
     ]
     for copy in copies:
         copy.start()
     slots, node_count = near_ref.shape
     rim = node_count // 2
-    place = lax.axis_index("mesh")
+    place = lax.axis_index(MESH)
     parity = lax.rem(place, 2)
-    embedding = embedding_of(jnp.full((2 * NOISE_FREQ, 1), noise_ref[0], F32))
-    copies[2].wait()
+    embedding = row_ref[...].T[: 2 * NOISE_FREQ, :1]
     for layer in range(LAYERS):
         film_ref[layer : layer + 1, :] = jnp.sum(
             embedding * film_w_ref[layer], axis=0, keepdims=True
         )
     normed_ref[:rim, :] = normed_of(x_o_ref[...], film_ref, 0)
     normed_ref[rim:, :] = normed_of(x_p_ref[...], film_ref, 0)
-    copies[0].wait()
-    copies[1].wait()
-    near_ref[...] = jnp.where(
-        live_ref[...] > 0, near_ref[...] - place * node_count, -(1 << 24)
-    )
+    kind = BF16 if rim + rim <= 256 else F32
+    near = near_ref[...] - (place * node_count + rim)
+    near = jnp.where(live_ref[...] > 0, near, -4 * node_count).astype(F32)
     column = lax.broadcasted_iota(jnp.int32, (1, 3 * rim), 1)
     side_o, side_p = halves(parity, rim)
     own = jnp.where(column < rim, column + side_o, column - rim + side_p)
     halo_o = column - 2 * rim + jnp.where(parity == 0, -rim, node_count)
     halo_p = column - 2 * rim + jnp.where(parity == 0, node_count, -rim)
-    ids_o = jnp.where(column < node_count, own, halo_o)
-    ids_p = jnp.where(column < node_count, own, halo_p)
     step = 32
-    for side, ids, out_ref in ((side_o, ids_o, bias_o_ref), (side_p, ids_p, bias_p_ref)):
-        near_t_ref[...] = near_ref[:, pl.ds(pl.multiple_of(side, rim), rim)].T
-
-        def rows(index, carry, ids=ids, out_ref=out_ref):
+    near_t_ref[...] = near.T
+    for side, halo, out_ref in ((side_o, halo_o, bias_o_ref), (side_p, halo_p, bias_p_ref)):
+        ids = (jnp.where(column < node_count, own, halo) - rim).astype(F32)
+        ids = jnp.broadcast_to(ids, (step, 3 * rim)).astype(kind)
+
+        def rows(index, carry, side=side, ids=ids, out_ref=out_ref):
             start = pl.multiple_of(index * step, step)
-            near = near_t_ref[pl.ds(start, step), :]
-            bias = jnp.full((step, 3 * rim), ABSENT, F32)
+            near = near_t_ref[pl.ds(pl.multiple_of(side + start, step), step), :]
+            bias = jnp.full((step, 3 * rim), ABSENT, kind)
+            zero = jnp.zeros((step, 3 * rim), kind)
             for slot in range(slots):
-                bias = jnp.where(near[:, slot : slot + 1] == ids, 0.0, bias)
-            out_ref[pl.ds(start, step), :] = bias
+                wide = jnp.broadcast_to(near[:, slot : slot + 1], (step, rim)).astype(kind)
+                bias = jnp.where(jnp.concatenate([wide] * 3, axis=1) == ids, zero, bias)
+            out_ref[pl.ds(start, step), :] = bias.astype(F32)
             return carry
 
         lax.fori_loop(0, rim // step, rows, 0)
-    copies[3].wait()
+    copies[0].wait()
     put_all((q_ref, k_ref, v_ref), project_own(normed_ref[...], w_ref, 0))
-    copies[4].wait()
+    copies[1].wait()
 
 
 def own_kernel(
     x_o_ref, x_p_ref, cot_ref, film_ref, w_ref, normed_ref, q_ref, k_ref, v_ref, ga_ref, cot2_ref
 ):
-    parity = lax.rem(lax.axis_index("mesh"), 2)
+    parity = lax.rem(lax.axis_index(MESH), 2)
     cot = jnp.concatenate([cot_ref[half_rows(cot_ref, parity, half), :] for half in range(2)])
     normed = normed_of(stacked(x_o_ref, x_p_ref), film_ref, 1)
     projected = project_own(normed, w_ref, 1)
@@ -252,8 +269,7 @@
             )
         )
     results = joined(parts, before, outs[1].dtype)
-    if half == 0:
-        results += (halo_grads(w_ref, 1, *results[3:]).astype(BF16),)
+    results += (halo_grads(w_ref, 1, *results[3:]).astype(BF16),)
     put_all((normed_h_ref, attended_ref, *outs), (normed, side_by_side(attended), *results))
 
 
@@ -262,43 +278,29 @@
 
 
 def grads_kernel(
-    plan, layer, x_o_ref, x_p_ref, halo_o_ref, halo_p_ref, gq_o_ref, gq_p_ref, gk_ref, gv_ref,
-    gk_h_ref, gv_h_ref, to_other_ref, w_ref, cond2_ref, gn_ref, to_pair_ref, cond_ref, *film_refs,
-):
-    rim, width = x_o_ref.shape
-    grad_p = halo_grads(w_ref, layer, gk_h_ref[...], gv_h_ref[...])
-    grad_own = mm_cols(gk_ref[...], w_ref[layer, 1]) + mm_cols(gv_ref[...], w_ref[layer, 2])
-    grads = [to_other_ref[...].astype(F32), grad_p]
-    for half, gq_ref in enumerate((gq_o_ref, gq_p_ref)):
-        rows = slice(half * rim, (half + 1) * rim)
-        grads.append(mm_cols(gq_ref[...], w_ref[layer, 0]) + grad_own[rows])
+    layer, x_o_ref, x_p_ref, halo_o_ref, halo_p_ref, gq_o_ref, gq_p_ref, gk_ref, gv_ref,
+    to_other_ref, to_pair_ref, w_ref, *refs,
+):
+    *before, gn_ref, cond_ref = refs
+    _, width = x_o_ref.shape
+    own = (
+        mm_cols(stacked(gq_o_ref, gq_p_ref), w_ref[layer, 0])
+        + mm_cols(gk_ref[...], w_ref[layer, 1])
+        + mm_cols(gv_ref[...], w_ref[layer, 2])
+    )
+    grads = [to_other_ref[...].astype(F32), to_pair_ref[...].astype(F32), own]
+    units = [unit_of(halo_o_ref[...])[0], unit_of(halo_p_ref[...])[0]]
+    units.append(unit_of(stacked(x_o_ref, x_p_ref))[0])
     scaled = jnp.zeros((1, width), F32)
     plain = jnp.zeros((1, width), F32)
-    for grad, ref in zip(grads, (halo_o_ref, halo_p_ref, x_o_ref, x_p_ref)):
-        scaled += jnp.sum(grad * unit_of(ref[...])[0], axis=0, keepdims=True)
+    for grad, unit in zip(grads, units, strict=True):
+        scaled += jnp.sum(grad * unit, axis=0, keepdims=True)
         plain += jnp.sum(grad, axis=0, keepdims=True)
-    to_pair_ref[...] = grad_p.astype(BF16)
-    gn_ref[:rim, :], gn_ref[rim:, :] = grads[2:]
-    cond_ref[:, :width] = scaled
-    cond_ref[:, width:] = plain
-    if not film_refs:
-        return
-    keep_ref, send_ref, scratch_ref = film_refs
-    part_rows = plan.film_rows // LAYERS
-    mesh = lax.axis_index("mesh")
-    for core in range(2):
-        for y in range(2):
-            col = lax.bitwise_xor(mesh, y * 2 + core) * (part_rows * LANES)
-            for layer_index, ref in enumerate((cond_ref, cond2_ref)):
-                for part in range(part_rows):
-                    start = pl.multiple_of(col + part * LANES, LANES)
-                    row = layer_index * part_rows + part
-                    out_ref = scratch_ref if core else keep_ref
-                    out_ref[y, row : row + 1, :] = ref[:, pl.ds(start, LANES)]
-    for y in range(2):
-        put_pair(
-            scratch_ref[y], send_ref.at[y * plan.film : y * plan.film + 2 * plan.film_rows, :]
-        )
+    gn_ref[...] = own
+    cond_ref[:1, :width] = scaled
+    cond_ref[:1, width:] = plain
+    for row, ref in enumerate(before, 1):
+        cond_ref[row : row + 1, :] = ref[...]
 
 
 def upstream_of(states, up, grad, film_ref, layer):
@@ -339,15 +341,14 @@
             )
         )
     results = joined(parts, before, outs[1].dtype)
-    if half == 0:
-        results += (halo_grads(w_ref, 0, *results[3:]).astype(BF16),)
+    results += (halo_grads(w_ref, 0, *results[3:]).astype(BF16),)
     put_all((up_ref, *outs), (up, *results))
 
 
 def end_kernel(
     x_o_ref, x_p_ref, up_o_ref, up_p_ref, gn_ref, back_o_ref, back_p_ref, film_ref, out_ref
 ):
-    parity = lax.rem(lax.axis_index("mesh"), 2)
+    parity = lax.rem(lax.axis_index(MESH), 2)
     rim = x_o_ref.shape[0]
     total = gn_ref[...] + stacked(back_o_ref, back_p_ref).astype(F32)
     grad = upstream_of(stacked(x_o_ref, x_p_ref), stacked(up_o_ref, up_p_ref), total, film_ref, 0)
@@ -411,7 +412,7 @@
 
     weight_products(*ins, put)
     rows = plan.rows // 2
-    ens, mesh = lax.axis_index("ens"), lax.axis_index("mesh")
+    ens, mesh = lax.axis_index(ENS), lax.axis_index(MESH)
     for slot in range(4):
         group, inner = slot // 2, slot % 2
         for core in range(2):
@@ -444,101 +445,126 @@
         ).astype(BF16)
 
 
-def stage_two(plan, kept_ref, y_ref, x_ref, y_base, x_base, to_x_ref, to_y_ref, next_ref):
+def stage_two(plan, kept_ref, y_ref, x_ref, to_x_ref, to_y_ref, next_ref):
     size = plan.weights // 8
-    for group, in_ref, base, out_ref in ((0, y_ref, y_base, to_x_ref), (1, x_ref, x_base, to_y_ref)):
+    for group, in_ref, out_ref in ((0, y_ref, to_x_ref), (1, x_ref, to_y_ref)):
         start = 2 * group * size
         next_ref[group * size : (group + 1) * size, :] = kept_ref[
             start : start + size, :
-        ] + in_ref[base : base + size, :].astype(F32)
+        ] + in_ref[:size, :].astype(F32)
         out_ref[...] = (
-            kept_ref[start + size : start + 2 * size, :]
-            + in_ref[base + size : base + 2 * size, :].astype(F32)
+            kept_ref[start + size : start + 2 * size, :] + in_ref[size : 2 * size, :].astype(F32)
         ).astype(BF16)
 
 
-def stage_three(plan, kept_ref, x_ref, y_ref, x_base, y_base, z_refs, last_ref):
+def stage_three(plan, kept_ref, x_ref, y_ref, z_refs, last_ref):
     rows = plan.rows
-    for group, in_ref, base in ((0, x_ref, x_base), (1, y_ref, y_base)):
+    for group, in_ref in enumerate((x_ref, y_ref)):
         for z in range(plan.deep):
             start = (group * plan.deep + z) * rows
-            value = kept_ref[start : start + rows, :] + in_ref[
-                base + z * rows : base + (z + 1) * rows, :
-            ].astype(F32)
+            value = kept_ref[start : start + rows, :] + in_ref[z * rows : (z + 1) * rows, :].astype(
+                F32
+            )
             if z:
                 z_refs[z - 1][group * rows : (group + 1) * rows, :] = value.astype(BF16)
             else:
                 last_ref[group * rows : (group + 1) * rows, :] = value
 
 
+def stage_across(plan, kept_ref, y_ref, x_ref, z_refs, last_ref):
+    rows = plan.rows
+    for group, in_ref in enumerate((y_ref, x_ref)):
+        for second in range(2):
+            for z in range(plan.deep):
+                start, inner = plan.at(0, group, second, z), plan.at(0, 0, second, z)
+                value = kept_ref[start : start + rows, :] + in_ref[inner : inner + rows, :].astype(F32)
+                spot = slice((group * 2 + second) * rows, (group * 2 + second + 1) * rows)
+                if z:
+                    z_refs[z - 1][spot, :] = value.astype(BF16)
+                else:
+                    last_ref[spot, :] = value
+
+
 def start_scatter_kernel(plan, keep_ref, came_ref, y_ref, x_ref, kept_ref):
     stage_one(plan, keep_ref, came_ref, y_ref, x_ref, kept_ref)
 
 
 def slot_a_kernel(
-    plan, keep1_ref, film1_ref, came1_ref, film_came_ref, kept2_ref, y2_ref, x2_ref,
-    y_ref, x_ref, kept1_ref, next2_ref, film_ref,
+    plan, keep1_ref, came1_ref, conds_ref, conds_came_ref, y_ref, x_ref, kept1_ref, film_ref,
+    total_ref, rows_ref,
+):
+    size = plan.weights // 4
+    stage_one(plan, keep1_ref, came1_ref, y_ref, x_ref, kept1_ref)
+    total_ref[...] = conds_ref[...] + conds_came_ref[...]
+    mesh = lax.axis_index(MESH)
+    part_rows = plan.film_rows // LAYERS
+    for y, out_ref in enumerate((film_ref, rows_ref)):
+        col = lax.bitwise_xor(mesh, y * 2) * (part_rows * LANES)
+        for layer in range(LAYERS):
+            for part in range(part_rows):
+                start = pl.multiple_of(col + part * LANES, LANES)
+                row = layer * part_rows + part
+                out_ref[row : row + 1, :] = total_ref[layer : layer + 1, pl.ds(start, LANES)]
+    put_pair(rows_ref[...], y_ref.at[size : size + 2 * plan.film_rows, :])
+
+
+def across_kernel(plan, kept2_ref, y2_ref, x2_ref, last2_ref, *z_refs):
+    stage_across(plan, kept2_ref, y2_ref, x2_ref, z_refs, last2_ref)
+
+
+def slot_b_kernel(
+    plan, kept1_ref, film_ref, y_ref, x_ref, embedding_ref, to_x_ref, to_y_ref, next1_ref
 ):
     size, small = plan.weights // 4, plan.weights // 8
-    stage_one(plan, keep1_ref, came1_ref, y_ref, x_ref, kept1_ref)
-    stage_two(
-        plan, kept2_ref, y2_ref, x2_ref, 0, 0,
-        x_ref.at[size : size + small, :], y_ref.at[size : size + small, :], next2_ref,
-    )
+    stage_two(plan, kept1_ref, y_ref, x_ref, to_x_ref.at[:small, :], to_y_ref, next1_ref)
     end = 2 * plan.film_rows
-    film_ref[...] = film1_ref[0] + get_pair(film_came_ref.at[:end, :])
-    put_pair(
-        film1_ref[1] + get_pair(film_came_ref.at[plan.film : plan.film + end, :]),
-        y_ref.at[size + small : size + small + end, :],
-    )
-
-
-def slot_b_kernel(
-    plan, kept1_ref, kept2_ref, film_ref, y_ref, x_ref, noise_ref, *outs,
-):
-    to_x_ref, to_y_ref, next1_ref, last2_ref, *z_refs = outs
-    size, small = plan.weights // 4, plan.weights // 8
-    stage_two(
-        plan, kept1_ref, y_ref, x_ref, 0, 0, to_x_ref.at[:small, :], to_y_ref.at[:small, :], next1_ref
-    )
-    stage_three(plan, kept2_ref, x_ref, y_ref, size, size, z_refs, last2_ref)
-    end = 2 * plan.film_rows
-    start = size + small
-    total = film_ref[...] + get_pair(y_ref.at[start : start + end, :])
+    total = film_ref[...] + get_pair(y_ref.at[size : size + end, :])
     put_pair(total, to_x_ref.at[small : small + end, :])
-    put_noise(jnp.full((1, LANES), noise_ref[0], F32), to_x_ref, small + end)
+    put_noise(embedding_ref[:1, :], to_x_ref, small + end)
 
 
 def slot_c_kernel(plan, kept1_ref, x_ref, y_ref, mine_ref, *outs):
     last1_ref, *z_refs = outs
-    stage_three(plan, kept1_ref, x_ref, y_ref, 0, 0, z_refs, last1_ref)
+    stage_three(plan, kept1_ref, x_ref, y_ref, z_refs, last1_ref)
     small, end = plan.weights // 8, 2 * plan.rows
     for z_ref in z_refs:
         z_ref[end : end + plan.film, :] = mine_ref[small : small + plan.film, :]
         z_ref[end + plan.film :, :] = x_ref[small : small + plan.film, :]
 
 
-def finish_kernel(plan, last1_ref, last2_ref, mine_ref, x_ref, *refs):
-    count = plan.deep - 1
-    z1_refs, z2_refs, (out_ref, film_ref) = refs[:count], refs[count : 2 * count], refs[2 * count :]
-    for layer, (last_ref, z_refs) in enumerate(((last1_ref, z1_refs), (last2_ref, z2_refs))):
-        rows = plan.rows // 2
-        for slot in range(4):
-            at = slice(slot * rows, (slot + 1) * rows)
-            total = last_ref[at, :]
+def late_kernel(plan, last2_ref, *refs):
+    *z_refs, to_x_ref, to_y_ref, kept_ref = refs
+    rows = plan.rows
+    for group, out_ref in enumerate((to_x_ref, to_y_ref)):
+        for second in range(2):
+            spot = slice((group * 2 + second) * rows, (group * 2 + second + 1) * rows)
+            total = last2_ref[spot, :]
             for z_ref in z_refs:
-                total = total + z_ref[at, :].astype(F32)
-            out_ref[layer, slot] = total
+                total = total + z_ref[spot, :].astype(F32)
+            if second:
+                out_ref[...] = total.astype(BF16)
+            else:
+                kept_ref[group * rows : (group + 1) * rows, :] = total
+
+
+def finish_kernel(plan, last1_ref, kept2_ref, late_x_ref, late_y_ref, mine_ref, x_ref, *refs):
+    *z_refs, out_ref, film_ref = refs
+    rows = plan.rows // 2
+    for slot in range(4):
+        at = slice(slot * rows, (slot + 1) * rows)
+        total = last1_ref[at, :]
+        for z_ref in z_refs:
+            total = total + z_ref[at, :].astype(F32)
+        out_ref[0, slot] = total
+        late_ref = late_y_ref if slot // 2 else late_x_ref
+        inner = slice(slot % 2 * rows, (slot % 2 + 1) * rows)
+        out_ref[1, slot] = kept2_ref[at, :] + late_ref[inner, :].astype(F32)
     small, end = plan.weights // 8, 2 * plan.rows
     packs = [ref.at[small : small + plan.film, :] for ref in (mine_ref, x_ref)]
-    for z_ref in z1_refs:
+    for z_ref in z_refs:
         packs += [z_ref.at[end + i * plan.film : end + (i + 1) * plan.film, :] for i in range(2)]
-    lane = lax.broadcasted_iota(jnp.int32, (1, LANES), 1)
-    noise = jnp.ones((1, LANES), F32)
     pair = 2 * plan.film_rows
-    for member, pack in enumerate(packs):
-        noise = jnp.where(lane == member, get_noise(pack, pair), noise)
-    embedding = embedding_of(jnp.broadcast_to(noise, (2 * NOISE_FREQ, LANES)))
+    embedding = jnp.concatenate([get_noise(pack, pair) for pack in packs], axis=0).T
     members = [get_pair(pack.at[:pair, :]) for pack in packs]
     half = plan.film_rows // LAYERS
     for layer in range(LAYERS):
@@ -546,7 +572,8 @@
             row = layer * half + part
             total = jnp.zeros((2 * NOISE_FREQ, LANES), F32)
             for member, value in enumerate(members):
-                total += embedding[:, member : member + 1] * value[row : row + 1, :]
+                weight = embedding[: 2 * NOISE_FREQ, member : member + 1]
+                total += weight * value[row : row + 1, :]
             film_ref[layer, :, part * LANES : (part + 1) * LANES] = total
 
 
@@ -557,7 +584,7 @@
     noise = jnp.ones((1, LANES), F32)
     for member in range(members):
         noise = jnp.where(lane == member, rows[member, LAYERS:, :1], noise)
-    embedding = embedding_of(jnp.broadcast_to(noise, (2 * NOISE_FREQ, LANES)))
+    embedding = embedding_of(jnp.broadcast_to(noise, (2 * NOISE_FREQ, LANES)), 0)
     for layer in range(LAYERS):
         total = jnp.zeros((2 * NOISE_FREQ, columns), F32)
         for member in range(members):
@@ -593,16 +620,16 @@
 
 
 def exchange_other(to_other):
-    count = lax.axis_size("mesh")
+    count = lax.axis_size(MESH)
     route = []
     for i in range(1, count - 1, 2):
         route += [(i, i + 1), (i + 1, i)]
-    return lax.ppermute(to_other, "mesh", route)
+    return lax.ppermute(to_other, MESH, route)
 
 
 def exchange(to_pair, to_other):
     other = exchange_other(to_other)
-    return swap(to_pair, "mesh", 1), other
+    return swap(to_pair, MESH, 1), other
 
 
 class Plan:
@@ -617,9 +644,8 @@
         return (((group * 2 + first) * 2 + second) * self.deep + z) * self.rows
 
 
-def film_pieces(conds, noise_level, mesh_count):
-    mesh = lax.axis_index("mesh")
-    rows = jnp.concatenate(conds, axis=0)
+def film_pieces(rows, noise_level, mesh_count):
+    mesh = lax.axis_index(MESH)
     width = rows.shape[1] // mesh_count
     pieces = rows.reshape(LAYERS, mesh_count, width).transpose(1, 0, 2)
     pieces = jnp.take(pieces, lax.bitwise_xor(jnp.arange(mesh_count), mesh), axis=0)
@@ -630,11 +656,11 @@
 
 def film_mesh_step(pieces, bit):
     pieces = pieces.reshape(-1, 2, *pieces.shape[1:])
-    return pieces[:, 0] + swap(pieces[:, 1], "mesh", bit)
+    return pieces[:, 0] + swap(pieces[:, 1], MESH, bit)
 
 
 def film_ens_step(rows, bit):
-    return jnp.concatenate([rows, swap(rows, "ens", bit)])
+    return jnp.concatenate([rows, swap(rows, ENS, bit)])
 
 
 def film_end(rows):
@@ -654,8 +680,8 @@
     states, cot = inputs[0], cotangent[0]
     nodes, width = states.shape
     rim = nodes // 2
-    mesh_count, ens_count = lax.axis_size("mesh"), lax.axis_size("ens")
-    side_o, side_p = halves(lax.rem(lax.axis_index("mesh"), 2), rim)
+    mesh_count, ens_count = lax.axis_size(MESH), lax.axis_size(ENS)
+    side_o, side_p = halves(lax.rem(lax.axis_index(MESH), 2), rim)
     square = 2 * nodes * width * width
     split = mesh_count == 4 and width % (mesh_count * LANES) == 0 and ens_count % 2 == 0
     plan = Plan(width, ens_count, mesh_count) if split else None
@@ -674,20 +700,22 @@
 
     smem = pl.BlockSpec(memory_space=pltpu.SMEM)
     cond_shape = ((1, 2 * width), F32)
-    x_o = lax.dynamic_slice_in_dim(states, side_o, rim)
-    x_p = lax.dynamic_slice_in_dim(states, side_p, rim)
+    slots = neighbours.shape[1]
+    table = ((slots, nodes), jnp.int32)
+    x_o, x_p, near, live, film_w, emb_row = call(
+        load_kernel,
+        (hbm(states), hbm(neighbours.T), hbm(live_slots.T), hbm(film_weights), noise_level),
+        [part(), part(), table, table, (film_weights.shape, F32), ((8, LANES), F32)],
+        sems=[pltpu.SemaphoreType.DMA((5,))], specs=[apart()] * 4 + [smem],
+    )
     halo_p, halo_o = exchange(x_p, x_o)
-    slots = neighbours.shape[1]
     film, bias_o, bias_p, normed1, q1, k1, v1, projections = call(
-        start_kernel,
-        (x_o, x_p, hbm(neighbours.T), hbm(live_slots.T), noise_level, hbm(film_weights),
-         hbm(projections)),
+        start_kernel, (x_o, x_p, near, live, emb_row, film_w, hbm(projections)),
         [((LAYERS, 2 * width), F32)] + [((rim, 3 * rim), F32)] * 2 + [full()] * 4
         + [(projections.shape, BF16)],
-        scratch=[((slots, nodes), jnp.int32), ((slots, nodes), jnp.int32),
-                 (film_weights.shape, F32), ((rim, slots), jnp.int32)],
-        sems=[pltpu.SemaphoreType.DMA((5,))], flops=3 * square,
-        specs=[whole()] * 2 + [apart()] * 2 + [smem] + [apart()] * 2,
+        scratch=[((nodes, slots), F32)],
+        sems=[pltpu.SemaphoreType.DMA((2,))], flops=3 * square,
+        specs=[whole()] * 6 + [apart()],
     )
     probs_shapes = [((HEADS, rim, nodes), BF16), ((HEADS, rim, rim), BF16)]
 
@@ -700,7 +728,7 @@
     next_o, normed1_o, k1_o, v1_o, own_o, over_o, attended1_o = forward(0, x_o, halo_o, bias_o)
     halo2_o = exchange_other(next_o)
     next_p, normed1_p, k1_p, v1_p, own_p, over_p, attended1_p = forward(1, x_p, halo_p, bias_p)
-    halo2_p = swap(next_p, "mesh", 1)
+    halo2_p = swap(next_p, MESH, 1)
     normed2, q2, k2, v2, ga2, cot2 = call(
         own_kernel, (next_o, next_p, cot, film, projections), [full()] * 6, flops=4 * square
     )
@@ -710,22 +738,21 @@
         return call(
             bind(last_layer_kernel, half),
             (halo, film, q2, k2, v2, ga2, bias, projections, *parts),
-            [part()] * 2 + grads + [part()] * (2 if half else 3),
+            [part()] * 2 + grads + [part()] * 3,
             flops=4 * square,
         )
 
-    normed2_p, attended2_p, gq2_p, *parts, gk2_p, gv2_p = last(1, halo2_p, bias_p, ())
+    normed2_p, attended2_p, gq2_p, *parts, gk2_p, gv2_p, to_pair = last(1, halo2_p, bias_p, ())
+    back_p = swap(to_pair, MESH, 1)
     normed2_o, attended2_o, gq2_o, gk2, gv2, gk2_o, gv2_o, to_other = last(
         0, halo2_o, bias_o, parts
     )
     back_o = exchange_other(to_other)
-    gn2, to_pair, cond2 = call(
-        bind(grads_kernel, None, 1),
-        (next_o, next_p, halo2_o, halo2_p, gq2_o, gq2_p, gk2, gv2, gk2_p, gv2_p, to_other,
-         projections, film),
-        [full(F32), part(), cond_shape], flops=4 * square,
-    )
-    back_p = swap(to_pair, "mesh", 1)
+    gn2, cond2 = call(
+        bind(grads_kernel, 1),
+        (next_o, next_p, halo2_o, halo2_p, gq2_o, gq2_p, gk2, gv2, to_other, to_pair, projections),
+        [full(F32), cond_shape], flops=4 * square,
+    )
 
     def weight_grads(*args):
         if not split:
@@ -742,23 +769,25 @@
     )
     if split:
         sums = plan.weights
-        came = swap(weights2[0], "mesh", 1)
+        came = swap(weights2[0], MESH, 1)
         to_y, to_x, kept2 = call(
             bind(start_scatter_kernel, plan), (weights2[1], came),
             [block(sums // 4)] * 2 + [block(sums // 2, F32)],
         )
-        y2, x2 = swap(to_y, "mesh", 2), swap(to_x, "ens", 1)
+        y2, x2 = swap(to_y, MESH, 2), swap(to_x, ENS, 1)
 
     def first(half, nxt, back, k_h, v_h, own, over, parts):
         grads = [part(), full(F32), full(F32)] if half else [part(), full(), full()]
         return call(
             bind(first_layer_kernel, half),
             (nxt, cot2, gn2, back, film, q1, k1, v1, k_h, v_h, own, over, projections, *parts),
-            [part()] + grads + [part()] * (2 if half else 3),
+            [part()] + grads + [part()] * 3,
             flops=4 * square,
         )
 
-    up_p, gq1_p, *parts, gk1_p, gv1_p = first(1, next_p, back_p, k1_p, v1_p, own_p, over_p, ())
+    up_p, gq1_p, *parts, gk1_p, gv1_p, to_pair = first(
+        1, next_p, back_p, k1_p, v1_p, own_p, over_p, ()
+    )
     up_o, gq1_o, gk1, gv1, gk1_o, gv1_o, to_other = first(
         0, next_o, back_o, k1_o, v1_o, own_o, over_o, parts
     )
@@ -766,70 +795,72 @@
         normed1, normed1_o, normed1_p, attended1_o, attended1_p, up_o, up_p,
         gq1_o, gq1_p, gk1, gk1_o, gk1_p, gv1, gv1_o, gv1_p,
     )
-    film_shapes = []
     if split:
-        came = swap(weights1[0], "mesh", 1)
-        film_shapes = [((2, plan.film_rows, LANES), F32), block(2 * plan.film)]
+        came = swap(weights1[0], MESH, 1)
     back_o = exchange_other(to_other)
-    gn1, to_pair, cond1, *film_parts = call(
-        bind(grads_kernel, plan, 0),
-        (x_o, x_p, halo_o, halo_p, gq1_o, gq1_p, gk1, gv1, gk1_p, gv1_p, to_other,
-         projections, cond2),
-        [full(F32), part(), cond_shape] + film_shapes,
-        scratch=film_shapes[:1], flops=4 * square,
-    )
-    back_p = swap(to_pair, "mesh", 1)
+    back_p = swap(to_pair, MESH, 1)
+    gn1, conds = call(
+        bind(grads_kernel, 0),
+        (x_o, x_p, halo_o, halo_p, gq1_o, gq1_p, gk1, gv1, to_other, to_pair, projections, cond2),
+        [full(F32), ((LAYERS, 2 * width), F32)], flops=4 * square,
+    )
     grad_input = call(end_kernel, (x_o, x_p, up_o, up_p, gn1, back_o, back_p, film), [full()])[0]
     if split:
-        film_came = swap(film_parts[1], "mesh", 1)
-        to_y, to_x, kept1, kept2, film_mine = call(
-            bind(slot_a_kernel, plan),
-            (weights1[1], film_parts[0], came, film_came, kept2, y2, x2),
-            [block(sums // 4 + sums // 8 + plan.film), block(sums // 4 + sums // 8),
-             block(sums // 2, F32), block(sums // 4, F32), block(plan.film_rows, F32)],
-        )
-        came_y, came_x = swap(to_y, "mesh", 2), swap(to_x, "ens", 1)
+        conds_came = swap(conds, MESH, 1)
         others = range(1, plan.deep)
-        to_x, to_y, kept1, last2, *to_z = call(
-            bind(slot_b_kernel, plan),
-            (kept1, kept2, film_mine, came_y, came_x, noise_level),
-            [block(sums // 8 + plan.film), block(sums // 8), block(sums // 4, F32),
-             block(2 * plan.rows, F32)] + [block(2 * plan.rows) for _ in others],
-            specs=[whole()] * 5 + [smem],
-        )
-        came_x, came_y = swap(to_x, "ens", 1), swap(to_y, "mesh", 2)
-        came_z2 = [swap(to_z[z - 1], "ens", 2 * z) for z in others]
+        to_y, to_x, kept1, film_mine = call(
+            bind(slot_a_kernel, plan), (weights1[1], came, conds, conds_came),
+            [block(sums // 4 + plan.film), block(sums // 4), block(sums // 2, F32),
+             block(plan.film_rows, F32)],
+            scratch=[(conds.shape, F32), block(plan.film_rows, F32)],
+        )
+        came_y, came_x = swap(to_y, MESH, 2), swap(to_x, ENS, 1)
+        last2, *to_z = call(
+            bind(across_kernel, plan), (kept2, y2, x2),
+            [block(4 * plan.rows, F32)] + [block(4 * plan.rows) for _ in others],
+        )
+        came_z2 = [swap(to_z[z - 1], ENS, 2 * z) for z in others]
+        to_x, to_y, kept1 = call(
+            bind(slot_b_kernel, plan), (kept1, film_mine, came_y, came_x, emb_row),
+            [block(sums // 8 + plan.film), block(sums // 8), block(sums // 4, F32)],
+        )
+        came_x, came_y = swap(to_x, ENS, 1), swap(to_y, MESH, 2)
         last1, *to_z = call(
             bind(slot_c_kernel, plan), (kept1, came_x, came_y, to_x),
             [block(2 * plan.rows, F32)] + [block(2 * plan.rows + 2 * plan.film) for _ in others],
         )
-        came_z1 = [swap(to_z[z - 1], "ens", 2 * z) for z in others]
+        came_z1 = [swap(to_z[z - 1], ENS, 2 * z) for z in others]
+        late_x, late_y, kept2 = call(
+            bind(late_kernel, plan), (last2, *came_z2),
+            [block(plan.rows)] * 2 + [block(2 * plan.rows, F32)],
+        )
+        late_x, late_y = swap(late_x, ENS, 1), swap(late_y, MESH, 2)
         weight_out, film_out = call(
             bind(finish_kernel, plan),
-            (last1, last2, to_x, came_x, *came_z1, *came_z2),
+            (last1, kept2, late_x, late_y, to_x, came_x, *came_z1),
             [((LAYERS, 4, width // ens_count, LANES), F32),
              ((LAYERS, 2 * NOISE_FREQ, 2 * width // mesh_count), F32)],
         )
     else:
-        film_rows = film_pieces((cond1, cond2), noise_level, mesh_count)
+        film_rows = film_pieces(conds, noise_level, mesh_count)
         for bit in bits_of(mesh_count):
             film_rows = film_mesh_step(film_rows, bit)
         for bit in bits_of(ens_count):
             film_rows = film_ens_step(film_rows, bit)
         film_out = film_end(film_rows)
         total = jnp.stack([weights1[0], weights2[0]]).astype(BF16)
-        total = lax.psum_scatter(total, "ens", scatter_dimension=2, tiled=True)
-        weight_out = lax.psum_scatter(total, "mesh", scatter_dimension=3, tiled=True).astype(F32)
+        total = lax.psum_scatter(total, ENS, scatter_dimension=2, tiled=True)
+        weight_out = lax.psum_scatter(total, MESH, scatter_dimension=3, tiled=True).astype(F32)
     return (grad_input[None], weight_out, film_out)
 
 
 def solution(mesh):
     placed = (
-        P("ens", "mesh", None),
-        P("ens", "mesh", None),
-        P("ens"),
-        P("mesh", None),
-        P("mesh", None),
+        P(ENS, MESH, None),
+        P(ENS, MESH, None),
+        P(ENS),
+        P(MESH, None),
+        P(MESH, None),
         P(),
         P(),
     )
@@ -837,6 +868,6 @@
         body,
         mesh=mesh,
         in_specs=placed,
-        out_specs=(P("ens", "mesh", None), P(None, None, "ens", "mesh"), P(None, None, "mesh")),
+        out_specs=(P(ENS, MESH, None), P(None, None, ENS, MESH), P(None, None, MESH)),
         check_vma=False,
     )

time: 79.6 us -> 75 us (0.942)
  the two profiles are of different devices: /device:TPU:0 before, /device:TPU:8 now
where the time goes in v4:
time: 75 us; the launch traced here: 74.8 us
  starting transfers between devices  35.6 us (47%)
  Pallas kernels  21.7 us (29%)
  waiting for transfers between devices  15.8 us (21%)
  between operations  1.51 us (2%)
    ppermute x21, starting transfers between devices, swap(): return lax.ppermute(block, axis, [(i, i ^ bit) for i in range(count)])  32.8 us
    pallas_call x21, Pallas kernels, call(): pl.pallas_call(kernel, out_shape=[jax.ShapeDtypeStruct(shape, kind) for s...  21.7 us
    ppermute x21, waiting for transfers between devices, swap(): return lax.ppermute(block, axis, [(i, i ^ bit) for i in range(count)])  15.8 us
    ppermute x4, starting transfers between devices, exchange_other(): return lax.ppermute(to_other, MESH, route)  2.85 us
  transfers between devices with their start and end apart: 25, of which 8 were waited for; matrix products, arithmetic and copies ran while one was open for 0% of the time, Pallas kernels for 22%

profile of v4, /device:TPU:8, one launch (start us, length us, event | category | flops | bytes accessed | tf_op | source)
XLA Modules:
  0.0 74.8 jit_solution(7167454422507117789)
XLA Ops:
  1.3 1.2 %shard_map.94 = (bf16[128,512]{1,0:T(8,128)(2,1)S(1)}, bf16[128,512]{1,0:T(8,128)(2,1)S(1)}, s32[32,256]{1,0:T(8,128)S(1)}, s32[32,256]{1,0:T(8,128)S(1)}, f32[2...) custom-call(bf16[256,512]{1,0:T(8,128)(2,1)} %bitcast.6, s32[32,256]{1,0:T(8,128)} %bitcast.8, s32[32,256]{1,0:T(8,128)} %bitcast.9, ...), custom_call_target="tpu_custom_call" | custom-call | bytes 1183748 | tf_op jit(solution)/shard_map/pallas_call | solution.py:606
  3.2 2.5 %shard_map.95 = (f32[2,1024]{1,0:T(2,128)S(1)}, f32[128,384]{1,0:T(8,128)S(1)}, f32[128,384]{1,0:T(8,128)S(1)}, bf16[256,512]{1,0:T(8,128)(2,1)S(1)}, bf16[256,5...) custom-call(bf16[128,512]{1,0:T(8,128)(2,1)S(1)} %get-tuple-element., ...), custom_call_target="tpu_custom_call" | custom-call | flops 402653184 | bytes 10432512 | tf_op jit(solution)/shard_map/pallas_call | solution.py:606
  5.7 1.2 %shard_map.97 = (bf16[128,512]{1,0:T(8,128)(2,1)S(1)}, bf16[128,512]{1,0:T(8,128)(2,1)S(1)}, bf16[128,512]{1,0:T(8,128)(2,1)S(1)}, bf16[128,512]{1,0:T(8,128)(2,...) custom-call(bf16[128,512]{1,0:T(8,128)(2,1)S(1)} %get-tuple-element.99.x_p_, ...), custom_call_target="tpu_custom_call" | custom-call | flops 268435456 | bytes 6496256 | tf_op jit(solution)/shard_map/pallas_call | solution.py:606
  6.9 2.9 %collective-permute-start.3 = (bf16[128,512]{1,0:T(8,128)(2,1)S(1)}, bf16[128,512]{1,0:T(8,128)(2,1)S(1)}, u32[]{:S(2)}, u32[]{:S(2)}) collective-permute-start(bf16[128,512]{1,0:T(8,128)(2,1)S(1)} %get-tuple-element.112.x_p_ref.next_ref), channel_id=1, source_target_pairs={{0,1},{1,0},{2,3},{3,2},{4,5},{5,4},{6,7},{7,6},{8,9},{9,8},{10,11... | collective-permute-start | bytes 393224 | tf_op jit(solution)/shard_map/ppermute | solution.py:619
  9.9 1.2 %shard_map.96 = (bf16[128,512]{1,0:T(8,128)(2,1)S(1)}, bf16[128,512]{1,0:T(8,128)(2,1)S(1)}, bf16[128,512]{1,0:T(8,128)(2,1)S(1)}, bf16[128,512]{1,0:T(8,128)(2,...) custom-call(bf16[128,512]{1,0:T(8,128)(2,1)S(1)} %get-tuple-element.98.x_o_, ...), custom_call_target="tpu_custom_call" | custom-call | flops 268435456 | bytes 6496256 | tf_op jit(solution)/shard_map/pallas_call | solution.py:606
  11.7 0.9 %shard_map.98 = (bf16[256,512]{1,0:T(8,128)(2,1)S(1)}, bf16[256,512]{1,0:T(8,128)(2,1)S(1)}, bf16[256,512]{1,0:T(8,128)(2,1)S(1)}, bf16[256,512]{1,0:T(8,128)(2,...) custom-call(bf16[128,512]{1,0:T(8,128)(2,1)S(1)} %get-tuple-element.110.x_o_ref.next_ref, ...), custom_call_target="tpu_custom_call" | custom-call | flops 536870912 | bytes 6299648 | tf_op jit(solution)/shard_map/pallas_call | solution.py:606
  12.7 2.0 %shard_map.99 = (bf16[128,512]{1,0:T(8,128)(2,1)S(1)}, bf16[128,512]{1,0:T(8,128)(2,1)S(1)}, bf16[128,512]{1,0:T(8,128)(2,1)S(1)}, f32[256,512]{1,0:T(8,128)S(1)...) custom-call(bf16[128,512]{1,0:T(8,128)(2,1)S(1)} %collective-permute, ...), custom_call_target="tpu_custom_call" | custom-call | flops 536870912 | bytes 7413760 | tf_op jit(solution)/shard_map/pallas_call | solution.py:606
  14.7 1.9 %collective-permute-start.5 = (bf16[128,512]{1,0:T(8,128)(2,1)S(1)}, bf16[128,512]{1,0:T(8,128)(2,1)S(1)}, u32[]{:S(2)}, u32[]{:S(2)}) collective-permute-start(bf16[128,512]{1,0:T(8,128)(2,1)S(1)} %get-tuple-element.125.to_pair_ref), channel_id=1, source_target_pairs={{0,1},{1,0},{2,3},{3,2},{4,5},{5,4},{6,7},{7,6},{8,9},{9,8},{10,11... | collective-permute-start | bytes 393224 | tf_op jit(solution)/shard_map/ppermute | solution.py:619
  16.6 2.0 %shard_map.100 = (bf16[128,512]{1,0:T(8,128)(2,1)S(1)}, bf16[128,512]{1,0:T(8,128)(2,1)S(1)}, bf16[128,512]{1,0:T(8,128)(2,1)S(1)}, bf16[256,512]{1,0:T(8,128)(2...) custom-call(bf16[128,512]{1,0:T(8,128)(2,1)S(1)} %collective-permute, ...), custom_call_target="tpu_custom_call" | custom-call | flops 536870912 | bytes 7938048 | tf_op jit(solution)/shard_map/pallas_call | solution.py:606
  20.2 1.7 %shard_map.102 = (bf16[128,512]{1,0:T(8,128)(2,1)S(1)}, bf16[128,512]{1,0:T(8,128)(2,1)S(1)}, f32[256,512]{1,0:T(8,128)S(1)}, f32[256,512]{1,0:T(8,128)S(1)}, bf...) custom-call(bf16[128,512]{1,0:T(8,128)(2,1)S(1)} %get-tuple-element.112.x_p_ref.next_ref, ...), custom_call_target="tpu_custom_call" | custom-call | flops 536870912 | bytes 8396800 | tf_op jit(solution)/shard_map/pallas_call | solution.py:606
  21.9 1.7 %shard_map.103 = (bf16[128,512]{1,0:T(8,128)(2,1)S(1)}, bf16[128,512]{1,0:T(8,128)(2,1)S(1)}, bf16[256,512]{1,0:T(8,128)(2,1)S(1)}, bf16[256,512]{1,0:T(8,128)(2...) custom-call(bf16[128,512]{1,0:T(8,128)(2,1)S(1)} %get-tuple-element.110.x_o_ref.ne, ...), custom_call_target="tpu_custom_call" | custom-call | flops 536870912 | bytes 8921088 | tf_op jit(solution)/shard_map/pallas_call | solution.py:606
  23.7 1.6 %shard_map.106 = (bf16[4096,128]{1,0:T(8,128)(2,1)S(1)}, f32[4096,128]{1,0:T(8,128)S(1)}) custom-call(bf16[256,512]{1,0:T(8,128)(2,1)S(1)} %get-tuple-element.147.refs_0_, bf16[128,512]{1,0:T(8,128)(2,1)S(1)} %get-tuple-element.148.refs_1_, bf16[128,512]{1,0:T(8,128)(2,1)S(1)} %get-tuple-element.149.refs_2_, ...), custom_call_target="tpu_custom_call" | custom-call | flops 805306368 | bytes 5505024 | tf_op jit(solution)/shard_map/pallas_call | solution.py:606
  25.2 3.8 %collective-permute-start.8 = (bf16[4096,128]{1,0:T(8,128)(2,1)S(1)}, bf16[4096,128]{1,0:T(8,128)(2,1)S(1)}, u32[]{:S(2)}, u32[]{:S(2)}) collective-permute-start(bf16[4096,128]{1,0:T(8,128)(2,1)S(1)} %get-tuple-element.157), channel_id=1, source_target_pairs={{0,1},{1,0},{2,3},{3,2},{4,5},{5,4},{6,7},{7,6},{8,9},{9,8},{10,11... | collective-permute-start | bytes 3145736 | tf_op jit(solution)/shard_map/ppermute | solution.py:619
  29.1 1.6 %shard_map.110 = (bf16[4096,128]{1,0:T(8,128)(2,1)S(1)}, f32[4096,128]{1,0:T(8,128)S(1)}) custom-call(bf16[256,512]{1,0:T(8,128)(2,1)S(1)} %get-tuple-element.167.refs_0_, bf16[128,512]{1,0:T(8,128)(2,1)S(1)} %get-tuple-element.168.refs_1_, bf16[128,512]{1,0:T(8,128)(2,1)S(1)} %get-tuple-element.169.refs_2_, ...), custom_call_target="tpu_custom_call" | custom-call | flops 805306368 | bytes 5505024 | tf_op jit(solution)/shard_map/pallas_call | solution.py:606
  32.0 1.4 %collective-permute-done.9.conds_came_ref = f32[2,1024]{1,0:T(2,128)S(1)} collective-permute-done((f32[2,1024]{1,0:T(2,128)S(1)}, f32[2,1024]{1,0:T(2,128)S(1)}, u32[]{:S(2)}, u32[]{:S(2)}) %collective-permute-start.9) | collective-permute-done | bytes 8224 | tf_op jit(solution)/shard_map/ppermute | solution.py:619
  34.4 1.5 %collective-permute-start.11 = (bf16[1024,128]{1,0:T(8,128)(2,1)S(1)}, bf16[1024,128]{1,0:T(8,128)(2,1)S(1)}, u32[]{:S(2)}, u32[]{:S(2)}) collective-permute-start(bf16[1024,128]{1,0:T(8,128)(2,1)S(1)} %get-tuple-element.162), channel_id=1, source_target_pairs={{0,4},{4,0},{8,12},{12,8},{16,20},{20,16},{24,28},{28,24},{1,5},{5... | collective-permute-start | bytes 786440 | tf_op jit(solution)/shard_map/ppermute | solution.py:619
  36.0 1.5 %collective-permute-start.15 = (bf16[1024,128]{1,0:T(8,128)(2,1)S(1)}, bf16[1024,128]{1,0:T(8,128)(2,1)S(1)}, u32[]{:S(2)}, u32[]{:S(2)}) collective-permute-start(bf16[1024,128]{1,0:T(8,128)(2,1)S(1)} %get-tuple-element.179), channel_id=1, source_target_pairs={{0,2},{1,3},{2,0},{3,1},{4,6},{5,7},{6,4},{7,5},{8,10},{9,11},{10,... | collective-permute-start | bytes 786440 | tf_op jit(solution)/shard_map/ppermute | solution.py:619
  38.1 5.5 %collective-permute-done.11.x_ref = bf16[1024,128]{1,0:T(8,128)(2,1)S(1)} collective-permute-done((bf16[1024,128]{1,0:T(8,128)(2,1)S(1)}, bf16[1024,128]{1,0:T(8,128)(2,1)S(1)}, u32[]{:S(2)}, u32[]{:S(2)}) %collective-permute-start.11) | collective-permute-done | bytes 262176 | tf_op jit(solution)/shard_map/ppermute | solution.py:619
  43.7 1.6 %collective-permute-start.12 = (bf16[528,128]{1,0:T(8,128)(2,1)S(1)}, bf16[528,128]{1,0:T(8,128)(2,1)S(1)}, u32[]{:S(2)}, u32[]{:S(2)}) collective-permute-start(bf16[528,128]{1,0:T(8,128)(2,1)S(1)} %get-tuple-element.164.mine_ref), channel_id=1, source_target_pairs={{0,4},{4,0},{8,12},{12,8},{16,20},{20,16},{24,28},{28,24},{1,5},{5... | collective-permute-start | bytes 405512 | tf_op jit(solution)/shard_map/ppermute | solution.py:619
  45.2 1.4 %collective-permute-start.13 = (bf16[512,128]{1,0:T(8,128)(2,1)S(1)}, bf16[512,128]{1,0:T(8,128)(2,1)S(1)}, u32[]{:S(2)}, u32[]{:S(2)}) collective-permute-start(bf16[512,128]{1,0:T(8,128)(2,1)S(1)} %get-tuple-element.165), channel_id=1, source_target_pairs={{0,2},{1,3},{2,0},{3,1},{4,6},{5,7},{6,4},{7,5},{8,10},{9,11},{10,... | collective-permute-start | bytes 393224 | tf_op jit(solution)/shard_map/ppermute | solution.py:619
  46.6 2.0 %collective-permute-done.15.y2_ref = bf16[1024,128]{1,0:T(8,128)(2,1)S(1)} collective-permute-done((bf16[1024,128]{1,0:T(8,128)(2,1)S(1)}, bf16[1024,128]{1,0:T(8,128)(2,1)S(1)}, u32[]{:S(2)}, u32[]{:S(2)}) %collective-permute-start.15) | collective-permute-done | bytes 262176 | tf_op jit(solution)/shard_map/ppermute | solution.py:619
  49.7 2.6 %collective-permute-start.18 = (bf16[512,128]{1,0:T(8,128)(2,1)S(1)}, bf16[512,128]{1,0:T(8,128)(2,1)S(1)}, u32[]{:S(2)}, u32[]{:S(2)}) collective-permute-start(bf16[512,128]{1,0:T(8,128)(2,1)S(1)} %get-tuple-element.183), channel_id=1, source_target_pairs={{0,16},{4,20},{8,24},{12,28},{16,0},{20,4},{24,8},{28,12},{1,17},{... | collective-permute-start | bytes 393224 | tf_op jit(solution)/shard_map/ppermute | solution.py:619
  53.5 2.8 %collective-permute-start.7 = (bf16[128,512]{1,0:T(8,128)(2,1)S(1)}, bf16[128,512]{1,0:T(8,128)(2,1)S(1)}, u32[]{:S(2)}, u32[]{:S(2)}) collective-permute-start(bf16[128,512]{1,0:T(8,128)(2,1)S(1)} %get-tuple-element.144.to_pair_ref), channel_id=1, source_target_pairs={{0,1},{1,0},{2,3},{3,2},{4,5},{5,4},{6,7},{7,6},{8,9},{9,8},{10,11... | collective-permute-start | bytes 393224 | tf_op jit(solution)/shard_map/ppermute | solution.py:619
  56.4 1.4 %collective-permute-start.22 = (bf16[288,128]{1,0:T(8,128)(2,1)S(1)}, bf16[288,128]{1,0:T(8,128)(2,1)S(1)}, u32[]{:S(2)}, u32[]{:S(2)}) collective-permute-start(bf16[288,128]{1,0:T(8,128)(2,1)S(1)} %get-tuple-element.188), channel_id=1, source_target_pairs={{0,8},{4,12},{8,0},{12,4},{16,24},{20,28},{24,16},{28,20},{1,9},{5... | collective-permute-start | bytes 221192 | tf_op jit(solution)/shard_map/ppermute | solution.py:619
  57.8 2.9 %collective-permute-done.18.refs_1_ = bf16[512,128]{1,0:T(8,128)(2,1)S(1)} collective-permute-done((bf16[512,128]{1,0:T(8,128)(2,1)S(1)}, bf16[512,128]{1,0:T(8,128)(2,1)S(1)}, u32[]{:S(2)}, u32[]{:S(2)}) %collective-permute-start.18) | collective-permute-done | bytes 131104 | tf_op jit(solution)/shard_map/ppermute | solution.py:619
  60.7 3.5 %collective-permute-start.23 = (bf16[288,128]{1,0:T(8,128)(2,1)S(1)}, bf16[288,128]{1,0:T(8,128)(2,1)S(1)}, u32[]{:S(2)}, u32[]{:S(2)}) collective-permute-start(bf16[288,128]{1,0:T(8,128)(2,1)S(1)} %get-tuple-element.189), channel_id=1, source_target_pairs={{0,16},{4,20},{8,24},{12,28},{16,0},{20,4},{24,8},{28,12},{1,17},{... | collective-permute-start | bytes 221192 | tf_op jit(solution)/shard_map/ppermute | solution.py:619
  64.2 1.6 %collective-permute-done.19.refs_2_ = bf16[512,128]{1,0:T(8,128)(2,1)S(1)} collective-permute-done((bf16[512,128]{1,0:T(8,128)(2,1)S(1)}, bf16[512,128]{1,0:T(8,128)(2,1)S(1)}, u32[]{:S(2)}, u32[]{:S(2)}) %collective-permute-start.19) | collective-permute-done | bytes 131104 | tf_op jit(solution)/shard_map/ppermute | solution.py:619
  65.8 2.5 %collective-permute-start.24 = (bf16[288,128]{1,0:T(8,128)(2,1)S(1)}, bf16[288,128]{1,0:T(8,128)(2,1)S(1)}, u32[]{:S(2)}, u32[]{:S(2)}) collective-permute-start(bf16[288,128]{1,0:T(8,128)(2,1)S(1)} %get-tuple-element.190), channel_id=1, source_target_pairs={{0,24},{4,28},{8,16},{12,20},{16,8},{20,12},{24,0},{28,4},{1,25},{... | collective-permute-start | bytes 221192 | tf_op jit(solution)/shard_map/ppermute | solution.py:619
  68.3 1.6 %collective-permute-start.20 = (bf16[128,128]{1,0:T(8,128)(2,1)S(1)}, bf16[128,128]{1,0:T(8,128)(2,1)S(1)}, u32[]{:S(2)}, u32[]{:S(2)}) collective-permute-start(bf16[128,128]{1,0:T(8,128)(2,1)S(1)} %get-tuple-element.186), channel_id=1, source_target_pairs={{0,4},{4,0},{8,12},{12,8},{16,20},{20,16},{24,28},{28,24},{1,5},{5... | collective-permute-start | bytes 98312 | tf_op jit(solution)/shard_map/ppermute | solution.py:619
  69.9 0.9 %collective-permute-start.21 = (bf16[128,128]{1,0:T(8,128)(2,1)S(1)}, bf16[128,128]{1,0:T(8,128)(2,1)S(1)}, u32[]{:S(2)}, u32[]{:S(2)}) collective-permute-start(bf16[128,128]{1,0:T(8,128)(2,1)S(1)} %get-tuple-element.187), channel_id=1, source_target_pairs={{0,2},{1,3},{2,0},{3,1},{4,6},{5,7},{6,4},{7,5},{8,10},{9,11},{10,... | collective-permute-start | bytes 98312 | tf_op jit(solution)/shard_map/ppermute | solution.py:619
  70.8 1.1 %shard_map.105 = bf16[256,512]{1,0:T(8,128)(2,1)} custom-call(bf16[128,512]{1,0:T(8,128)(2,1)S(1)} %get-tuple-element.98.x_o_ref.x_ref, bf16[128,512]{1,0:T(8,128)(2,1)S(1)} %get-tuple-element.99.x_p_ref.x_ref, bf16[128,512]{1,0:T(8,128)(2,1)S(1)} %get-tuple-element.137.up_o_ref.refs_5_, bf16[128,512]{1,0:T(8,128)(2,1)S(1)} %get-tuple-element.138.up_p_ref.refs_6_, ...), custom_call_target="tpu_custom_call" | custom-call | bytes 1581056 | tf_op jit(solution)/shard_map/pallas_call | solution.py:606
  72.3 1.5 %collective-permute-done.21.late_y_ref = bf16[128,128]{1,0:T(8,128)(2,1)S(1)} collective-permute-done((bf16[128,128]{1,0:T(8,128)(2,1)S(1)}, bf16[128,128]{1,0:T(8,128)(2,1)S(1)}, u32[]{:S(2)}, u32[]{:S(2)}) %collective-permute-start.21) | collective-permute-done | bytes 32800 | tf_op jit(solution)/shard_map/ppermute | solution.py:619
  (42 shorter events, 9.8 us)
Async XLA Ops:
  2.5 3.3 %collective-permute-start.1 = (bf16[128,512]{1,0:T(8,128)(2,1)S(1)}, bf16[128,512]{1,0:T(8,128)(2,1)S(1)}, u32[]{:S(2)}, u32[]{:S(2)}) collective-permute-start(bf16[128,512]{1,0:T(8,128)(2,1)S(1)} %get-tuple-element.99.x_p_ref.x_ref), channel_id=1, source_target_pairs={{0,1},{1,0},{2,3},{3,2},{4,5},{5,4},{6,7},{7,6},{8,9},{9,8},{10,11... | collective-permute-start | bytes 393224 | tf_op jit(solution)/shard_map/ppermute | solution.py:619
  2.5 7.3 %collective-permute-start = (bf16[128,512]{1,0:T(8,128)(2,1)S(1)}, bf16[128,512]{1,0:T(8,128)(2,1)S(1)}, u32[]{:S(2)}, u32[]{:S(2)}) collective-permute-start(bf16[128,512]{1,0:T(8,128)(2,1)S(1)} %get-tuple-element.98.x_o_ref.x_ref), channel_id=1, source_target_pairs={{1,2},{2,1},{5,6},{6,5},{9,10},{10,9},{13,14},{14,13},{17,18},{18,... | collective-permute-start | bytes 393224 | tf_op jit(solution)/shard_map/ppermute | solution.py:627
  5.7 6.0 %copy-start = (bf16[1,256,512]{2,1,0:T(8,128)(2,1)S(1)}, bf16[1,256,512]{2,1,0:T(8,128)(2,1)}, u32[]{:S(2)}) copy-start(bf16[1,256,512]{2,1,0:T(8,128)(2,1)} %param.8) | copy-start | bytes 786436
  6.9 5.7 %collective-permute-start.3 = (bf16[128,512]{1,0:T(8,128)(2,1)S(1)}, bf16[128,512]{1,0:T(8,128)(2,1)S(1)}, u32[]{:S(2)}, u32[]{:S(2)}) collective-permute-start(bf16[128,512]{1,0:T(8,128)(2,1)S(1)} %get-tuple-element.112.x_p_ref.next_ref), channel_id=1, source_target_pairs={{0,1},{1,0},{2,3},{3,2},{4,5},{5,4},{6,7},{7,6},{8,9},{9,8},{10,11... | collective-permute-start | bytes 393224 | tf_op jit(solution)/shard_map/ppermute | solution.py:619
  11.1 5.5 %collective-permute-start.2 = (bf16[128,512]{1,0:T(8,128)(2,1)S(1)}, bf16[128,512]{1,0:T(8,128)(2,1)S(1)}, u32[]{:S(2)}, u32[]{:S(2)}) collective-permute-start(bf16[128,512]{1,0:T(8,128)(2,1)S(1)} %get-tuple-element.110.x_o_ref.next_ref), channel_id=1, source_target_pairs={{1,2},{2,1},{5,6},{6,5},{9,10},{10,9},{13,14},{14,13},{17,18},{18,... | collective-permute-start | bytes 393224 | tf_op jit(solution)/shard_map/ppermute | solution.py:627
  14.7 5.5 %collective-permute-start.5 = (bf16[128,512]{1,0:T(8,128)(2,1)S(1)}, bf16[128,512]{1,0:T(8,128)(2,1)S(1)}, u32[]{:S(2)}, u32[]{:S(2)}) collective-permute-start(bf16[128,512]{1,0:T(8,128)(2,1)S(1)} %get-tuple-element.125.to_pair_ref), channel_id=1, source_target_pairs={{0,1},{1,0},{2,3},{3,2},{4,5},{5,4},{6,7},{7,6},{8,9},{9,8},{10,11... | collective-permute-start | bytes 393224 | tf_op jit(solution)/shard_map/ppermute | solution.py:619
  18.6 3.3 %collective-permute-start.4 = (bf16[128,512]{1,0:T(8,128)(2,1)S(1)}, bf16[128,512]{1,0:T(8,128)(2,1)S(1)}, u32[]{:S(2)}, u32[]{:S(2)}) collective-permute-start(bf16[128,512]{1,0:T(8,128)(2,1)S(1)} %get-tuple-element.124.to_other_ref), channel_id=1, source_target_pairs={{1,2},{2,1},{5,6},{6,5},{9,10},{10,9},{13,14},{14,13},{17,18},{18,... | collective-permute-start | bytes 393224 | tf_op jit(solution)/shard_map/ppermute | solution.py:627
  25.2 8.2 %collective-permute-start.8 = (bf16[4096,128]{1,0:T(8,128)(2,1)S(1)}, bf16[4096,128]{1,0:T(8,128)(2,1)S(1)}, u32[]{:S(2)}, u32[]{:S(2)}) collective-permute-start(bf16[4096,128]{1,0:T(8,128)(2,1)S(1)} %get-tuple-element.157), channel_id=1, source_target_pairs={{0,1},{1,0},{2,3},{3,2},{4,5},{5,4},{6,7},{7,6},{8,9},{9,8},{10,11... | collective-permute-start | bytes 3145736 | tf_op jit(solution)/shard_map/ppermute | solution.py:619
  30.6 5.2 %collective-permute-start.14 = (bf16[4096,128]{1,0:T(8,128)(2,1)S(1)}, bf16[4096,128]{1,0:T(8,128)(2,1)S(1)}, u32[]{:S(2)}, u32[]{:S(2)}) collective-permute-start(bf16[4096,128]{1,0:T(8,128)(2,1)S(1)} %get-tuple-element.177), channel_id=1, source_target_pairs={{0,1},{1,0},{2,3},{3,2},{4,5},{5,4},{6,7},{7,6},{8,9},{9,8},{10,11... | collective-permute-start | bytes 3145736 | tf_op jit(solution)/shard_map/ppermute | solution.py:619
  31.4 2.0 %collective-permute-start.9 = (f32[2,1024]{1,0:T(2,128)S(1)}, f32[2,1024]{1,0:T(2,128)S(1)}, u32[]{:S(2)}, u32[]{:S(2)}) collective-permute-start(f32[2,1024]{1,0:T(2,128)S(1)} %get-tuple-element.158.conds_ref), channel_id=1, source_target_pairs={{0,1},{1,0},{2,3},{3,2},{4,5},{5,4},{6,7},{7,6},{8,9},{9,8},{10,11... | collective-permute-start | bytes 24584 | tf_op jit(solution)/shard_map/ppermute | solution.py:619
  33.7 9.8 %collective-permute-start.10 = (bf16[1040,128]{1,0:T(8,128)(2,1)S(1)}, bf16[1040,128]{1,0:T(8,128)(2,1)S(1)}, u32[]{:S(2)}, u32[]{:S(2)}) collective-permute-start(bf16[1040,128]{1,0:T(8,128)(2,1)S(1)} %get-tuple-element.161), channel_id=1, source_target_pairs={{0,2},{1,3},{2,0},{3,1},{4,6},{5,7},{6,4},{7,5},{8,10},{9,11},{10,... | collective-permute-start | bytes 798728 | tf_op jit(solution)/shard_map/ppermute | solution.py:619
  34.4 9.2 %collective-permute-start.11 = (bf16[1024,128]{1,0:T(8,128)(2,1)S(1)}, bf16[1024,128]{1,0:T(8,128)(2,1)S(1)}, u32[]{:S(2)}, u32[]{:S(2)}) collective-permute-start(bf16[1024,128]{1,0:T(8,128)(2,1)S(1)} %get-tuple-element.162), channel_id=1, source_target_pairs={{0,4},{4,0},{8,12},{12,8},{16,20},{20,16},{24,28},{28,24},{1,5},{5... | collective-permute-start | bytes 786440 | tf_op jit(solution)/shard_map/ppermute | solution.py:619
  36.0 12.6 %collective-permute-start.15 = (bf16[1024,128]{1,0:T(8,128)(2,1)S(1)}, bf16[1024,128]{1,0:T(8,128)(2,1)S(1)}, u32[]{:S(2)}, u32[]{:S(2)}) collective-permute-start(bf16[1024,128]{1,0:T(8,128)(2,1)S(1)} %get-tuple-element.179), channel_id=1, source_target_pairs={{0,2},{1,3},{2,0},{3,1},{4,6},{5,7},{6,4},{7,5},{8,10},{9,11},{10,... | collective-permute-start | bytes 786440 | tf_op jit(solution)/shard_map/ppermute | solution.py:619
  37.5 11.6 %collective-permute-start.16 = (bf16[1024,128]{1,0:T(8,128)(2,1)S(1)}, bf16[1024,128]{1,0:T(8,128)(2,1)S(1)}, u32[]{:S(2)}, u32[]{:S(2)}) collective-permute-start(bf16[1024,128]{1,0:T(8,128)(2,1)S(1)} %get-tuple-element.180), channel_id=1, source_target_pairs={{0,4},{4,0},{8,12},{12,8},{16,20},{20,16},{24,28},{28,24},{1,5},{5... | collective-permute-start | bytes 786440 | tf_op jit(solution)/shard_map/ppermute | solution.py:619
  43.7 9.8 %collective-permute-start.12 = (bf16[528,128]{1,0:T(8,128)(2,1)S(1)}, bf16[528,128]{1,0:T(8,128)(2,1)S(1)}, u32[]{:S(2)}, u32[]{:S(2)}) collective-permute-start(bf16[528,128]{1,0:T(8,128)(2,1)S(1)} %get-tuple-element.164.mine_ref), channel_id=1, source_target_pairs={{0,4},{4,0},{8,12},{12,8},{16,20},{20,16},{24,28},{28,24},{1,5},{5... | collective-permute-start | bytes 405512 | tf_op jit(solution)/shard_map/ppermute | solution.py:619
  45.2 7.6 %collective-permute-start.13 = (bf16[512,128]{1,0:T(8,128)(2,1)S(1)}, bf16[512,128]{1,0:T(8,128)(2,1)S(1)}, u32[]{:S(2)}, u32[]{:S(2)}) collective-permute-start(bf16[512,128]{1,0:T(8,128)(2,1)S(1)} %get-tuple-element.165), channel_id=1, source_target_pairs={{0,2},{1,3},{2,0},{3,1},{4,6},{5,7},{6,4},{7,5},{8,10},{9,11},{10,... | collective-permute-start | bytes 393224 | tf_op jit(solution)/shard_map/ppermute | solution.py:619
  49.3 7.1 %collective-permute-start.17 = (bf16[512,128]{1,0:T(8,128)(2,1)S(1)}, bf16[512,128]{1,0:T(8,128)(2,1)S(1)}, u32[]{:S(2)}, u32[]{:S(2)}) collective-permute-start(bf16[512,128]{1,0:T(8,128)(2,1)S(1)} %get-tuple-element.182), channel_id=1, source_target_pairs={{0,8},{4,12},{8,0},{12,4},{16,24},{20,28},{24,16},{28,20},{1,9},{5... | collective-permute-start | bytes 393224 | tf_op jit(solution)/shard_map/ppermute | solution.py:619
  49.7 11.0 %collective-permute-start.18 = (bf16[512,128]{1,0:T(8,128)(2,1)S(1)}, bf16[512,128]{1,0:T(8,128)(2,1)S(1)}, u32[]{:S(2)}, u32[]{:S(2)}) collective-permute-start(bf16[512,128]{1,0:T(8,128)(2,1)S(1)} %get-tuple-element.183), channel_id=1, source_target_pairs={{0,16},{4,20},{8,24},{12,28},{16,0},{20,4},{24,8},{28,12},{1,17},{... | collective-permute-start | bytes 393224 | tf_op jit(solution)/shard_map/ppermute | solution.py:619
  52.4 13.4 %collective-permute-start.19 = (bf16[512,128]{1,0:T(8,128)(2,1)S(1)}, bf16[512,128]{1,0:T(8,128)(2,1)S(1)}, u32[]{:S(2)}, u32[]{:S(2)}) collective-permute-start(bf16[512,128]{1,0:T(8,128)(2,1)S(1)} %get-tuple-element.184), channel_id=1, source_target_pairs={{0,24},{4,28},{8,16},{12,20},{16,8},{20,12},{24,0},{28,4},{1,25},{... | collective-permute-start | bytes 393224 | tf_op jit(solution)/shard_map/ppermute | solution.py:619
  52.8 15.5 %collective-permute-start.6 = (bf16[128,512]{1,0:T(8,128)(2,1)S(1)}, bf16[128,512]{1,0:T(8,128)(2,1)S(1)}, u32[]{:S(2)}, u32[]{:S(2)}) collective-permute-start(bf16[128,512]{1,0:T(8,128)(2,1)S(1)} %get-tuple-element.143.to_other_ref), channel_id=1, source_target_pairs={{1,2},{2,1},{5,6},{6,5},{9,10},{10,9},{13,14},{14,13},{17,18},{18,... | collective-permute-start | bytes 393224 | tf_op jit(solution)/shard_map/ppermute | solution.py:627
  53.5 16.4 %collective-permute-start.7 = (bf16[128,512]{1,0:T(8,128)(2,1)S(1)}, bf16[128,512]{1,0:T(8,128)(2,1)S(1)}, u32[]{:S(2)}, u32[]{:S(2)}) collective-permute-start(bf16[128,512]{1,0:T(8,128)(2,1)S(1)} %get-tuple-element.144.to_pair_ref), channel_id=1, source_target_pairs={{0,1},{1,0},{2,3},{3,2},{4,5},{5,4},{6,7},{7,6},{8,9},{9,8},{10,11... | collective-permute-start | bytes 393224 | tf_op jit(solution)/shard_map/ppermute | solution.py:619
  56.4 17.4 %collective-permute-start.22 = (bf16[288,128]{1,0:T(8,128)(2,1)S(1)}, bf16[288,128]{1,0:T(8,128)(2,1)S(1)}, u32[]{:S(2)}, u32[]{:S(2)}) collective-permute-start(bf16[288,128]{1,0:T(8,128)(2,1)S(1)} %get-tuple-element.188), channel_id=1, source_target_pairs={{0,8},{4,12},{8,0},{12,4},{16,24},{20,28},{24,16},{28,20},{1,9},{5... | collective-permute-start | bytes 221192 | tf_op jit(solution)/shard_map/ppermute | solution.py:619
  60.7 13.1 %collective-permute-start.23 = (bf16[288,128]{1,0:T(8,128)(2,1)S(1)}, bf16[288,128]{1,0:T(8,128)(2,1)S(1)}, u32[]{:S(2)}, u32[]{:S(2)}) collective-permute-start(bf16[288,128]{1,0:T(8,128)(2,1)S(1)} %get-tuple-element.189), channel_id=1, source_target_pairs={{0,16},{4,20},{8,24},{12,28},{16,0},{20,4},{24,8},{28,12},{1,17},{... | collective-permute-start | bytes 221192 | tf_op jit(solution)/shard_map/ppermute | solution.py:619
  65.8 8.0 %collective-permute-start.24 = (bf16[288,128]{1,0:T(8,128)(2,1)S(1)}, bf16[288,128]{1,0:T(8,128)(2,1)S(1)}, u32[]{:S(2)}, u32[]{:S(2)}) collective-permute-start(bf16[288,128]{1,0:T(8,128)(2,1)S(1)} %get-tuple-element.190), channel_id=1, source_target_pairs={{0,24},{4,28},{8,16},{12,20},{16,8},{20,12},{24,0},{28,4},{1,25},{... | collective-permute-start | bytes 221192 | tf_op jit(solution)/shard_map/ppermute | solution.py:619
  68.3 4.0 %collective-permute-start.20 = (bf16[128,128]{1,0:T(8,128)(2,1)S(1)}, bf16[128,128]{1,0:T(8,128)(2,1)S(1)}, u32[]{:S(2)}, u32[]{:S(2)}) collective-permute-start(bf16[128,128]{1,0:T(8,128)(2,1)S(1)} %get-tuple-element.186), channel_id=1, source_target_pairs={{0,4},{4,0},{8,12},{12,8},{16,20},{20,16},{24,28},{28,24},{1,5},{5... | collective-permute-start | bytes 98312 | tf_op jit(solution)/shard_map/ppermute | solution.py:619
  69.9 3.9 %collective-permute-start.21 = (bf16[128,128]{1,0:T(8,128)(2,1)S(1)}, bf16[128,128]{1,0:T(8,128)(2,1)S(1)}, u32[]{:S(2)}, u32[]{:S(2)}) collective-permute-start(bf16[128,128]{1,0:T(8,128)(2,1)S(1)} %get-tuple-element.187), channel_id=1, source_target_pairs={{0,2},{1,3},{2,0},{3,1},{4,6},{5,7},{6,4},{7,5},{8,10},{9,11},{10,... | collective-permute-start | bytes 98312 | tf_op jit(solution)/shard_map/ppermute | solution.py:619

commit v5 on v4

--- a/solution.py
+++ b/solution.py
@@ -405,31 +405,40 @@
 
 
 def split_weight_kernel(plan, *refs):
-    *ins, send_ref, keep_ref, total_ref = refs
-
-    def put(slot, value):
-        total_ref[slot] = value
-
-    weight_products(*ins, put)
+    (
+        normed_ref, normed_o_ref, normed_p_ref, attended_o_ref, attended_p_ref, up_o_ref, up_p_ref,
+        gq_o_ref, gq_p_ref, gk_ref, gk_o_ref, gk_p_ref, gv_ref, gv_o_ref, gv_p_ref,
+        send_ref, keep_ref,
+    ) = refs
+    normed = stacked(normed_ref, normed_o_ref, normed_p_ref).T
+    attended = stacked(attended_o_ref, attended_p_ref).T
+    products = (
+        (3, attended, (up_o_ref, up_p_ref)),
+        (0, normed[:, : normed_ref.shape[0]], (gq_o_ref, gq_p_ref)),
+        (1, normed, (gk_ref, gk_o_ref, gk_p_ref)),
+        (2, normed, (gv_ref, gv_o_ref, gv_p_ref)),
+    )
     rows = plan.rows // 2
     ens, mesh = lax.axis_index(ENS), lax.axis_index(MESH)
-    for slot in range(4):
+    for slot, left, rights in products:
         group, inner = slot // 2, slot % 2
-        for core in range(2):
+        for core, out_ref in ((1, send_ref), (0, keep_ref)):
+            right = []
             for y in range(2):
-                col = lax.bitwise_xor(mesh, y * 2 + core)
-                cols = pl.ds(pl.multiple_of(col * LANES, LANES), LANES)
-                for x in range(2):
-                    for z in range(plan.deep):
-                        row = lax.bitwise_xor(ens, z * 2 + x)
-                        at = pl.ds(pl.multiple_of(row * rows, rows), rows)
-                        piece = total_ref[slot, at, cols]
-                        first, second = (y, x) if group == 0 else (x, y)
-                        start = plan.at(group, first, second, z) + inner * rows
-                        if core:
-                            send_ref[start : start + rows, :] = piece.astype(BF16)
-                        else:
-                            keep_ref[start : start + rows, :] = piece
+                col = pl.multiple_of(lax.bitwise_xor(mesh, y * 2 + core) * LANES, LANES)
+                right.append(
+                    jnp.concatenate([ref[:, pl.ds(col, LANES)] for ref in rights], axis=0)
+                )
+            value = mm(left, side_by_side(right)).astype(out_ref.dtype)
+            for row in range(2 * plan.deep):
+                place = lax.bitwise_xor(ens, row)
+                x, z = lax.bitwise_and(place, 1), lax.shift_right_logical(place, 1)
+                for y in range(2):
+                    first, second = (y, x) if group == 0 else (x, y)
+                    start = pl.multiple_of(plan.at(group, first, second, z) + inner * rows, rows)
+                    out_ref[pl.ds(start, rows), :] = value[
+                        row * rows : (row + 1) * rows, y * LANES : (y + 1) * LANES
+                    ]
 
 
 def stage_one(plan, keep_ref, came_ref, y_ref, x_ref, kept_ref):
@@ -759,8 +768,7 @@
             return call(plain_weight_kernel, args, [((4, width, width), F32)], flops=6 * square)
         return call(
             bind(split_weight_kernel, plan), args,
-            [block(plan.weights), block(plan.weights, F32)],
-            scratch=[((4, width, width), F32)], flops=6 * square,
+            [block(plan.weights), block(plan.weights, F32)], flops=6 * square,
         )
 
     weights2 = weight_grads(

time: 75 us -> 74 us (0.987)
  the two profiles are of different devices: /device:TPU:8 before, /device:TPU:0 now
where the time goes in v5:
time: 74 us; the launch traced here: 73.2 us
  starting transfers between devices  35.7 us (48%)
  Pallas kernels  20.7 us (28%)
  waiting for transfers between devices  15.2 us (21%)
  between operations  1.51 us (2%)
    ppermute x21, starting transfers between devices, swap(): return lax.ppermute(block, axis, [(i, i ^ bit) for i in range(count)])  32.9 us
    pallas_call x21, Pallas kernels, call(): pl.pallas_call(kernel, out_shape=[jax.ShapeDtypeStruct(shape, kind) for s...  20.7 us
    ppermute x21, waiting for transfers between devices, swap(): return lax.ppermute(block, axis, [(i, i ^ bit) for i in range(count)])  15.2 us
    ppermute x4, starting transfers between devices, exchange_other(): return lax.ppermute(to_other, MESH, route)  2.83 us
  transfers between devices with their start and end apart: 25, of which 6 were waited for; matrix products, arithmetic and copies ran while one was open for 0% of the time, Pallas kernels for 22%

profile of v5, /device:TPU:0, one launch (start us, length us, event | category | flops | bytes accessed | tf_op | source)
XLA Modules:
  0.0 73.2 jit_solution(4166564263841027403)
XLA Ops:
  1.3 1.2 %shard_map.94 = (bf16[128,512]{1,0:T(8,128)(2,1)S(1)}, bf16[128,512]{1,0:T(8,128)(2,1)S(1)}, s32[32,256]{1,0:T(8,128)S(1)}, s32[32,256]{1,0:T(8,128)S(1)}, f32[2...) custom-call(bf16[256,512]{1,0:T(8,128)(2,1)} %bitcast.6, s32[32,256]{1,0:T(8,128)} %bitcast.8, s32[32,256]{1,0:T(8,128)} %bitcast.9, ...), custom_call_target="tpu_custom_call" | custom-call | bytes 1183748 | tf_op jit(solution)/shard_map/pallas_call | solution.py:615
  3.7 2.5 %shard_map.95 = (f32[2,1024]{1,0:T(2,128)S(1)}, f32[128,384]{1,0:T(8,128)S(1)}, f32[128,384]{1,0:T(8,128)S(1)}, bf16[256,512]{1,0:T(8,128)(2,1)S(1)}, bf16[256,5...) custom-call(bf16[128,512]{1,0:T(8,128)(2,1)S(1)} %get-tuple-element., ...), custom_call_target="tpu_custom_call" | custom-call | flops 402653184 | bytes 10432512 | tf_op jit(solution)/shard_map/pallas_call | solution.py:615
  6.2 1.2 %shard_map.97 = (bf16[128,512]{1,0:T(8,128)(2,1)S(1)}, bf16[128,512]{1,0:T(8,128)(2,1)S(1)}, bf16[128,512]{1,0:T(8,128)(2,1)S(1)}, bf16[128,512]{1,0:T(8,128)(2,...) custom-call(bf16[128,512]{1,0:T(8,128)(2,1)S(1)} %get-tuple-element.99.x_p_, ...), custom_call_target="tpu_custom_call" | custom-call | flops 268435456 | bytes 6496256 | tf_op jit(solution)/shard_map/pallas_call | solution.py:615
  7.4 4.0 %collective-permute-start.3 = (bf16[128,512]{1,0:T(8,128)(2,1)S(1)}, bf16[128,512]{1,0:T(8,128)(2,1)S(1)}, u32[]{:S(2)}, u32[]{:S(2)}) collective-permute-start(bf16[128,512]{1,0:T(8,128)(2,1)S(1)} %get-tuple-element.112.x_p_ref.next_ref), channel_id=1, source_target_pairs={{0,1},{1,0},{2,3},{3,2},{4,5},{5,4},{6,7},{7,6},{8,9},{9,8},{10,11... | collective-permute-start | bytes 393224 | tf_op jit(solution)/shard_map/ppermute | solution.py:628
  11.3 1.2 %shard_map.96 = (bf16[128,512]{1,0:T(8,128)(2,1)S(1)}, bf16[128,512]{1,0:T(8,128)(2,1)S(1)}, bf16[128,512]{1,0:T(8,128)(2,1)S(1)}, bf16[128,512]{1,0:T(8,128)(2,...) custom-call(bf16[128,512]{1,0:T(8,128)(2,1)S(1)} %get-tuple-element.98.x_o_, ...), custom_call_target="tpu_custom_call" | custom-call | flops 268435456 | bytes 6496256 | tf_op jit(solution)/shard_map/pallas_call | solution.py:615
  13.2 0.9 %shard_map.98 = (bf16[256,512]{1,0:T(8,128)(2,1)S(1)}, bf16[256,512]{1,0:T(8,128)(2,1)S(1)}, bf16[256,512]{1,0:T(8,128)(2,1)S(1)}, bf16[256,512]{1,0:T(8,128)(2,...) custom-call(bf16[128,512]{1,0:T(8,128)(2,1)S(1)} %get-tuple-element.110.x_o_ref.next_ref, ...), custom_call_target="tpu_custom_call" | custom-call | flops 536870912 | bytes 6299648 | tf_op jit(solution)/shard_map/pallas_call | solution.py:615
  14.2 2.0 %shard_map.99 = (bf16[128,512]{1,0:T(8,128)(2,1)S(1)}, bf16[128,512]{1,0:T(8,128)(2,1)S(1)}, bf16[128,512]{1,0:T(8,128)(2,1)S(1)}, f32[256,512]{1,0:T(8,128)S(1)...) custom-call(bf16[128,512]{1,0:T(8,128)(2,1)S(1)} %collective-permute, ...), custom_call_target="tpu_custom_call" | custom-call | flops 536870912 | bytes 7413760 | tf_op jit(solution)/shard_map/pallas_call | solution.py:615
  16.1 1.9 %collective-permute-start.5 = (bf16[128,512]{1,0:T(8,128)(2,1)S(1)}, bf16[128,512]{1,0:T(8,128)(2,1)S(1)}, u32[]{:S(2)}, u32[]{:S(2)}) collective-permute-start(bf16[128,512]{1,0:T(8,128)(2,1)S(1)} %get-tuple-element.125.to_pair_ref), channel_id=1, source_target_pairs={{0,1},{1,0},{2,3},{3,2},{4,5},{5,4},{6,7},{7,6},{8,9},{9,8},{10,11... | collective-permute-start | bytes 393224 | tf_op jit(solution)/shard_map/ppermute | solution.py:628
  18.0 2.0 %shard_map.100 = (bf16[128,512]{1,0:T(8,128)(2,1)S(1)}, bf16[128,512]{1,0:T(8,128)(2,1)S(1)}, bf16[128,512]{1,0:T(8,128)(2,1)S(1)}, bf16[256,512]{1,0:T(8,128)(2...) custom-call(bf16[128,512]{1,0:T(8,128)(2,1)S(1)} %collective-permute, ...), custom_call_target="tpu_custom_call" | custom-call | flops 536870912 | bytes 7938048 | tf_op jit(solution)/shard_map/pallas_call | solution.py:615
  20.1 0.8 %collective-permute-start.4 = (bf16[128,512]{1,0:T(8,128)(2,1)S(1)}, bf16[128,512]{1,0:T(8,128)(2,1)S(1)}, u32[]{:S(2)}, u32[]{:S(2)}) collective-permute-start(bf16[128,512]{1,0:T(8,128)(2,1)S(1)} %get-tuple-element.124.to_other_ref), channel_id=1, source_target_pairs={{1,2},{2,1},{5,6},{6,5},{9,10},{10,9},{13,14},{14,13},{17,18},{18,... | collective-permute-start | bytes 393224 | tf_op jit(solution)/shard_map/ppermute | solution.py:636
  21.6 1.7 %shard_map.102 = (bf16[128,512]{1,0:T(8,128)(2,1)S(1)}, bf16[128,512]{1,0:T(8,128)(2,1)S(1)}, f32[256,512]{1,0:T(8,128)S(1)}, f32[256,512]{1,0:T(8,128)S(1)}, bf...) custom-call(bf16[128,512]{1,0:T(8,128)(2,1)S(1)} %get-tuple-element.112.x_p_ref.next_ref, ...), custom_call_target="tpu_custom_call" | custom-call | flops 536870912 | bytes 8396800 | tf_op jit(solution)/shard_map/pallas_call | solution.py:615
  23.4 1.7 %shard_map.103 = (bf16[128,512]{1,0:T(8,128)(2,1)S(1)}, bf16[128,512]{1,0:T(8,128)(2,1)S(1)}, bf16[256,512]{1,0:T(8,128)(2,1)S(1)}, bf16[256,512]{1,0:T(8,128)(2...) custom-call(bf16[128,512]{1,0:T(8,128)(2,1)S(1)} %get-tuple-element.110.x_o_ref.ne, ...), custom_call_target="tpu_custom_call" | custom-call | flops 536870912 | bytes 8921088 | tf_op jit(solution)/shard_map/pallas_call | solution.py:615
  25.1 1.0 %shard_map.106 = (bf16[4096,128]{1,0:T(8,128)(2,1)S(1)}, f32[4096,128]{1,0:T(8,128)S(1)}) custom-call(bf16[256,512]{1,0:T(8,128)(2,1)S(1)} %get-tuple-element.147.refs_0_, bf16[128,512]{1,0:T(8,128)(2,1)S(1)} %get-tuple-element.148.refs_1_, bf16[128,512]{1,0:T(8,128)(2,1)S(1)} %get-tuple-element.149.refs_2_, ...), custom_call_target="tpu_custom_call" | custom-call | flops 805306368 | bytes 5505024 | tf_op jit(solution)/shard_map/pallas_call | solution.py:615
  26.2 3.9 %collective-permute-start.8 = (bf16[4096,128]{1,0:T(8,128)(2,1)S(1)}, bf16[4096,128]{1,0:T(8,128)(2,1)S(1)}, u32[]{:S(2)}, u32[]{:S(2)}) collective-permute-start(bf16[4096,128]{1,0:T(8,128)(2,1)S(1)} %get-tuple-element.157), channel_id=1, source_target_pairs={{0,1},{1,0},{2,3},{3,2},{4,5},{5,4},{6,7},{7,6},{8,9},{9,8},{10,11... | collective-permute-start | bytes 3145736 | tf_op jit(solution)/shard_map/ppermute | solution.py:628
  30.0 1.0 %shard_map.110 = (bf16[4096,128]{1,0:T(8,128)(2,1)S(1)}, f32[4096,128]{1,0:T(8,128)S(1)}) custom-call(bf16[256,512]{1,0:T(8,128)(2,1)S(1)} %get-tuple-element.167.refs_0_, bf16[128,512]{1,0:T(8,128)(2,1)S(1)} %get-tuple-element.168.refs_1_, bf16[128,512]{1,0:T(8,128)(2,1)S(1)} %get-tuple-element.169.refs_2_, ...), custom_call_target="tpu_custom_call" | custom-call | flops 805306368 | bytes 5505024 | tf_op jit(solution)/shard_map/pallas_call | solution.py:615
  32.4 1.4 %collective-permute-done.9.conds_came_ref = f32[2,1024]{1,0:T(2,128)S(1)} collective-permute-done((f32[2,1024]{1,0:T(2,128)S(1)}, f32[2,1024]{1,0:T(2,128)S(1)}, u32[]{:S(2)}, u32[]{:S(2)}) %collective-permute-start.9) | collective-permute-done | bytes 8224 | tf_op jit(solution)/shard_map/ppermute | solution.py:628
  34.1 0.9 %collective-permute-start.10 = (bf16[1040,128]{1,0:T(8,128)(2,1)S(1)}, bf16[1040,128]{1,0:T(8,128)(2,1)S(1)}, u32[]{:S(2)}, u32[]{:S(2)}) collective-permute-start(bf16[1040,128]{1,0:T(8,128)(2,1)S(1)} %get-tuple-element.161), channel_id=1, source_target_pairs={{0,2},{1,3},{2,0},{3,1},{4,6},{5,7},{6,4},{7,5},{8,10},{9,11},{10,... | collective-permute-start | bytes 798728 | tf_op jit(solution)/shard_map/ppermute | solution.py:628
  35.0 1.5 %collective-permute-start.11 = (bf16[1024,128]{1,0:T(8,128)(2,1)S(1)}, bf16[1024,128]{1,0:T(8,128)(2,1)S(1)}, u32[]{:S(2)}, u32[]{:S(2)}) collective-permute-start(bf16[1024,128]{1,0:T(8,128)(2,1)S(1)} %get-tuple-element.162), channel_id=1, source_target_pairs={{0,4},{4,0},{8,12},{12,8},{16,20},{20,16},{24,28},{28,24},{1,5},{5... | collective-permute-start | bytes 786440 | tf_op jit(solution)/shard_map/ppermute | solution.py:628
  36.7 1.2 %collective-permute-start.15 = (bf16[1024,128]{1,0:T(8,128)(2,1)S(1)}, bf16[1024,128]{1,0:T(8,128)(2,1)S(1)}, u32[]{:S(2)}, u32[]{:S(2)}) collective-permute-start(bf16[1024,128]{1,0:T(8,128)(2,1)S(1)} %get-tuple-element.179), channel_id=1, source_target_pairs={{0,2},{1,3},{2,0},{3,1},{4,6},{5,7},{6,4},{7,5},{8,10},{9,11},{10,... | collective-permute-start | bytes 786440 | tf_op jit(solution)/shard_map/ppermute | solution.py:628
  38.5 5.7 %collective-permute-done.11.x_ref = bf16[1024,128]{1,0:T(8,128)(2,1)S(1)} collective-permute-done((bf16[1024,128]{1,0:T(8,128)(2,1)S(1)}, bf16[1024,128]{1,0:T(8,128)(2,1)S(1)}, u32[]{:S(2)}, u32[]{:S(2)}) %collective-permute-start.11) | collective-permute-done | bytes 262176 | tf_op jit(solution)/shard_map/ppermute | solution.py:628
  44.3 1.6 %collective-permute-start.12 = (bf16[528,128]{1,0:T(8,128)(2,1)S(1)}, bf16[528,128]{1,0:T(8,128)(2,1)S(1)}, u32[]{:S(2)}, u32[]{:S(2)}) collective-permute-start(bf16[528,128]{1,0:T(8,128)(2,1)S(1)} %get-tuple-element.164.mine_ref), channel_id=1, source_target_pairs={{0,4},{4,0},{8,12},{12,8},{16,20},{20,16},{24,28},{28,24},{1,5},{5... | collective-permute-start | bytes 405512 | tf_op jit(solution)/shard_map/ppermute | solution.py:628
  45.9 1.2 %collective-permute-start.13 = (bf16[512,128]{1,0:T(8,128)(2,1)S(1)}, bf16[512,128]{1,0:T(8,128)(2,1)S(1)}, u32[]{:S(2)}, u32[]{:S(2)}) collective-permute-start(bf16[512,128]{1,0:T(8,128)(2,1)S(1)} %get-tuple-element.165), channel_id=1, source_target_pairs={{0,2},{1,3},{2,0},{3,1},{4,6},{5,7},{6,4},{7,5},{8,10},{9,11},{10,... | collective-permute-start | bytes 393224 | tf_op jit(solution)/shard_map/ppermute | solution.py:628
  47.1 2.0 %collective-permute-done.15.y2_ref = bf16[1024,128]{1,0:T(8,128)(2,1)S(1)} collective-permute-done((bf16[1024,128]{1,0:T(8,128)(2,1)S(1)}, bf16[1024,128]{1,0:T(8,128)(2,1)S(1)}, u32[]{:S(2)}, u32[]{:S(2)}) %collective-permute-start.15) | collective-permute-done | bytes 262176 | tf_op jit(solution)/shard_map/ppermute | solution.py:628
  49.9 1.7 %collective-permute-start.17 = (bf16[512,128]{1,0:T(8,128)(2,1)S(1)}, bf16[512,128]{1,0:T(8,128)(2,1)S(1)}, u32[]{:S(2)}, u32[]{:S(2)}) collective-permute-start(bf16[512,128]{1,0:T(8,128)(2,1)S(1)} %get-tuple-element.182), channel_id=1, source_target_pairs={{0,8},{4,12},{8,0},{12,4},{16,24},{20,28},{24,16},{28,20},{1,9},{5... | collective-permute-start | bytes 393224 | tf_op jit(solution)/shard_map/ppermute | solution.py:628
  51.6 2.6 %collective-permute-start.18 = (bf16[512,128]{1,0:T(8,128)(2,1)S(1)}, bf16[512,128]{1,0:T(8,128)(2,1)S(1)}, u32[]{:S(2)}, u32[]{:S(2)}) collective-permute-start(bf16[512,128]{1,0:T(8,128)(2,1)S(1)} %get-tuple-element.183), channel_id=1, source_target_pairs={{0,16},{4,20},{8,24},{12,28},{16,0},{20,4},{24,8},{28,12},{1,17},{... | collective-permute-start | bytes 393224 | tf_op jit(solution)/shard_map/ppermute | solution.py:628
  55.0 2.6 %collective-permute-start.7 = (bf16[128,512]{1,0:T(8,128)(2,1)S(1)}, bf16[128,512]{1,0:T(8,128)(2,1)S(1)}, u32[]{:S(2)}, u32[]{:S(2)}) collective-permute-start(bf16[128,512]{1,0:T(8,128)(2,1)S(1)} %get-tuple-element.144.to_pair_ref), channel_id=1, source_target_pairs={{0,1},{1,0},{2,3},{3,2},{4,5},{5,4},{6,7},{7,6},{8,9},{9,8},{10,11... | collective-permute-start | bytes 393224 | tf_op jit(solution)/shard_map/ppermute | solution.py:628
  58.5 4.5 %collective-permute-done.18.refs_1_ = bf16[512,128]{1,0:T(8,128)(2,1)S(1)} collective-permute-done((bf16[512,128]{1,0:T(8,128)(2,1)S(1)}, bf16[512,128]{1,0:T(8,128)(2,1)S(1)}, u32[]{:S(2)}, u32[]{:S(2)}) %collective-permute-start.18) | collective-permute-done | bytes 131104 | tf_op jit(solution)/shard_map/ppermute | solution.py:628
  63.0 2.6 %collective-permute-start.24 = (bf16[288,128]{1,0:T(8,128)(2,1)S(1)}, bf16[288,128]{1,0:T(8,128)(2,1)S(1)}, u32[]{:S(2)}, u32[]{:S(2)}) collective-permute-start(bf16[288,128]{1,0:T(8,128)(2,1)S(1)} %get-tuple-element.190), channel_id=1, source_target_pairs={{0,24},{4,28},{8,16},{12,20},{16,8},{20,12},{24,0},{28,4},{1,25},{... | collective-permute-start | bytes 221192 | tf_op jit(solution)/shard_map/ppermute | solution.py:628
  65.7 1.6 %collective-permute-start.20 = (bf16[128,128]{1,0:T(8,128)(2,1)S(1)}, bf16[128,128]{1,0:T(8,128)(2,1)S(1)}, u32[]{:S(2)}, u32[]{:S(2)}) collective-permute-start(bf16[128,128]{1,0:T(8,128)(2,1)S(1)} %get-tuple-element.186), channel_id=1, source_target_pairs={{0,4},{4,0},{8,12},{12,8},{16,20},{20,16},{24,28},{28,24},{1,5},{5... | collective-permute-start | bytes 98312 | tf_op jit(solution)/shard_map/ppermute | solution.py:628
  67.2 3.1 %collective-permute-start.21 = (bf16[128,128]{1,0:T(8,128)(2,1)S(1)}, bf16[128,128]{1,0:T(8,128)(2,1)S(1)}, u32[]{:S(2)}, u32[]{:S(2)}) collective-permute-start(bf16[128,128]{1,0:T(8,128)(2,1)S(1)} %get-tuple-element.187), channel_id=1, source_target_pairs={{0,2},{1,3},{2,0},{3,1},{4,6},{5,7},{6,4},{7,5},{8,10},{9,11},{10,... | collective-permute-start | bytes 98312 | tf_op jit(solution)/shard_map/ppermute | solution.py:628
  70.3 1.1 %shard_map.105 = bf16[256,512]{1,0:T(8,128)(2,1)} custom-call(bf16[128,512]{1,0:T(8,128)(2,1)S(1)} %get-tuple-element.98.x_o_ref.x_ref, bf16[128,512]{1,0:T(8,128)(2,1)S(1)} %get-tuple-element.99.x_p_ref.x_ref, bf16[128,512]{1,0:T(8,128)(2,1)S(1)} %get-tuple-element.137.up_o_ref.refs_5_, bf16[128,512]{1,0:T(8,128)(2,1)S(1)} %get-tuple-element.138.up_p_ref.refs_6_, ...), custom_call_target="tpu_custom_call" | custom-call | bytes 1581056 | tf_op jit(solution)/shard_map/pallas_call | solution.py:615
  72.2 0.9 %shard_map.114 = (f32[2,4,64,128]{3,2,1,0:T(8,128)}, f32[2,32,256]{2,1,0:T(8,128)}) custom-call(f32[256,128]{1,0:T(8,128)S(1)} %get-tuple-element.166.last1_ref, f32[256,128]{1,0:T(8,128)S(1)} %get-tuple-element.185.kept2_ref, bf16[128,128]{1,0:T(8,128)(2,1)S(1)} %collective-permute-done.20.late_x_ref, ...), custom_call_target="tpu_custom_call" | custom-call | bytes 1146880 | tf_op jit(solution)/shard_map/pallas_call | solution.py:615
  (42 shorter events, 8.5 us)
Async XLA Ops:
  2.5 3.7 %collective-permute-start.1 = (bf16[128,512]{1,0:T(8,128)(2,1)S(1)}, bf16[128,512]{1,0:T(8,128)(2,1)S(1)}, u32[]{:S(2)}, u32[]{:S(2)}) collective-permute-start(bf16[128,512]{1,0:T(8,128)(2,1)S(1)} %get-tuple-element.99.x_p_ref.x_ref), channel_id=1, source_target_pairs={{0,1},{1,0},{2,3},{3,2},{4,5},{5,4},{6,7},{7,6},{8,9},{9,8},{10,11... | collective-permute-start | bytes 393224 | tf_op jit(solution)/shard_map/ppermute | solution.py:628
  3.0 8.3 %collective-permute-start = (bf16[128,512]{1,0:T(8,128)(2,1)S(1)}, bf16[128,512]{1,0:T(8,128)(2,1)S(1)}, u32[]{:S(2)}, u32[]{:S(2)}) collective-permute-start(bf16[128,512]{1,0:T(8,128)(2,1)S(1)} %get-tuple-element.98.x_o_ref.x_ref), channel_id=1, source_target_pairs={{1,2},{2,1},{5,6},{6,5},{9,10},{10,9},{13,14},{14,13},{17,18},{18,... | collective-permute-start | bytes 393224 | tf_op jit(solution)/shard_map/ppermute | solution.py:636
  6.2 7.0 %copy-start = (bf16[1,256,512]{2,1,0:T(8,128)(2,1)S(1)}, bf16[1,256,512]{2,1,0:T(8,128)(2,1)}, u32[]{:S(2)}) copy-start(bf16[1,256,512]{2,1,0:T(8,128)(2,1)} %param.8) | copy-start | bytes 786436
  7.4 6.8 %collective-permute-start.3 = (bf16[128,512]{1,0:T(8,128)(2,1)S(1)}, bf16[128,512]{1,0:T(8,128)(2,1)S(1)}, u32[]{:S(2)}, u32[]{:S(2)}) collective-permute-start(bf16[128,512]{1,0:T(8,128)(2,1)S(1)} %get-tuple-element.112.x_p_ref.next_ref), channel_id=1, source_target_pairs={{0,1},{1,0},{2,3},{3,2},{4,5},{5,4},{6,7},{7,6},{8,9},{9,8},{10,11... | collective-permute-start | bytes 393224 | tf_op jit(solution)/shard_map/ppermute | solution.py:628
  12.5 5.5 %collective-permute-start.2 = (bf16[128,512]{1,0:T(8,128)(2,1)S(1)}, bf16[128,512]{1,0:T(8,128)(2,1)S(1)}, u32[]{:S(2)}, u32[]{:S(2)}) collective-permute-start(bf16[128,512]{1,0:T(8,128)(2,1)S(1)} %get-tuple-element.110.x_o_ref.next_ref), channel_id=1, source_target_pairs={{1,2},{2,1},{5,6},{6,5},{9,10},{10,9},{13,14},{14,13},{17,18},{18,... | collective-permute-start | bytes 393224 | tf_op jit(solution)/shard_map/ppermute | solution.py:636
  16.1 5.5 %collective-permute-start.5 = (bf16[128,512]{1,0:T(8,128)(2,1)S(1)}, bf16[128,512]{1,0:T(8,128)(2,1)S(1)}, u32[]{:S(2)}, u32[]{:S(2)}) collective-permute-start(bf16[128,512]{1,0:T(8,128)(2,1)S(1)} %get-tuple-element.125.to_pair_ref), channel_id=1, source_target_pairs={{0,1},{1,0},{2,3},{3,2},{4,5},{5,4},{6,7},{7,6},{8,9},{9,8},{10,11... | collective-permute-start | bytes 393224 | tf_op jit(solution)/shard_map/ppermute | solution.py:628
  20.1 3.3 %collective-permute-start.4 = (bf16[128,512]{1,0:T(8,128)(2,1)S(1)}, bf16[128,512]{1,0:T(8,128)(2,1)S(1)}, u32[]{:S(2)}, u32[]{:S(2)}) collective-permute-start(bf16[128,512]{1,0:T(8,128)(2,1)S(1)} %get-tuple-element.124.to_other_ref), channel_id=1, source_target_pairs={{1,2},{2,1},{5,6},{6,5},{9,10},{10,9},{13,14},{14,13},{17,18},{18,... | collective-permute-start | bytes 393224 | tf_op jit(solution)/shard_map/ppermute | solution.py:636
  26.2 7.7 %collective-permute-start.8 = (bf16[4096,128]{1,0:T(8,128)(2,1)S(1)}, bf16[4096,128]{1,0:T(8,128)(2,1)S(1)}, u32[]{:S(2)}, u32[]{:S(2)}) collective-permute-start(bf16[4096,128]{1,0:T(8,128)(2,1)S(1)} %get-tuple-element.157), channel_id=1, source_target_pairs={{0,1},{1,0},{2,3},{3,2},{4,5},{5,4},{6,7},{7,6},{8,9},{9,8},{10,11... | collective-permute-start | bytes 3145736 | tf_op jit(solution)/shard_map/ppermute | solution.py:628
  31.1 5.5 %collective-permute-start.14 = (bf16[4096,128]{1,0:T(8,128)(2,1)S(1)}, bf16[4096,128]{1,0:T(8,128)(2,1)S(1)}, u32[]{:S(2)}, u32[]{:S(2)}) collective-permute-start(bf16[4096,128]{1,0:T(8,128)(2,1)S(1)} %get-tuple-element.177), channel_id=1, source_target_pairs={{0,1},{1,0},{2,3},{3,2},{4,5},{5,4},{6,7},{7,6},{8,9},{9,8},{10,11... | collective-permute-start | bytes 3145736 | tf_op jit(solution)/shard_map/ppermute | solution.py:628
  31.8 2.0 %collective-permute-start.9 = (f32[2,1024]{1,0:T(2,128)S(1)}, f32[2,1024]{1,0:T(2,128)S(1)}, u32[]{:S(2)}, u32[]{:S(2)}) collective-permute-start(f32[2,1024]{1,0:T(2,128)S(1)} %get-tuple-element.158.conds_ref), channel_id=1, source_target_pairs={{0,1},{1,0},{2,3},{3,2},{4,5},{5,4},{6,7},{7,6},{8,9},{9,8},{10,11... | collective-permute-start | bytes 24584 | tf_op jit(solution)/shard_map/ppermute | solution.py:628
  34.1 10.1 %collective-permute-start.10 = (bf16[1040,128]{1,0:T(8,128)(2,1)S(1)}, bf16[1040,128]{1,0:T(8,128)(2,1)S(1)}, u32[]{:S(2)}, u32[]{:S(2)}) collective-permute-start(bf16[1040,128]{1,0:T(8,128)(2,1)S(1)} %get-tuple-element.161), channel_id=1, source_target_pairs={{0,2},{1,3},{2,0},{3,1},{4,6},{5,7},{6,4},{7,5},{8,10},{9,11},{10,... | collective-permute-start | bytes 798728 | tf_op jit(solution)/shard_map/ppermute | solution.py:628
  35.0 9.2 %collective-permute-start.11 = (bf16[1024,128]{1,0:T(8,128)(2,1)S(1)}, bf16[1024,128]{1,0:T(8,128)(2,1)S(1)}, u32[]{:S(2)}, u32[]{:S(2)}) collective-permute-start(bf16[1024,128]{1,0:T(8,128)(2,1)S(1)} %get-tuple-element.162), channel_id=1, source_target_pairs={{0,4},{4,0},{8,12},{12,8},{16,20},{20,16},{24,28},{28,24},{1,5},{5... | collective-permute-start | bytes 786440 | tf_op jit(solution)/shard_map/ppermute | solution.py:628
  36.7 12.4 %collective-permute-start.15 = (bf16[1024,128]{1,0:T(8,128)(2,1)S(1)}, bf16[1024,128]{1,0:T(8,128)(2,1)S(1)}, u32[]{:S(2)}, u32[]{:S(2)}) collective-permute-start(bf16[1024,128]{1,0:T(8,128)(2,1)S(1)} %get-tuple-element.179), channel_id=1, source_target_pairs={{0,2},{1,3},{2,0},{3,1},{4,6},{5,7},{6,4},{7,5},{8,10},{9,11},{10,... | collective-permute-start | bytes 786440 | tf_op jit(solution)/shard_map/ppermute | solution.py:628
  37.9 11.9 %collective-permute-start.16 = (bf16[1024,128]{1,0:T(8,128)(2,1)S(1)}, bf16[1024,128]{1,0:T(8,128)(2,1)S(1)}, u32[]{:S(2)}, u32[]{:S(2)}) collective-permute-start(bf16[1024,128]{1,0:T(8,128)(2,1)S(1)} %get-tuple-element.180), channel_id=1, source_target_pairs={{0,4},{4,0},{8,12},{12,8},{16,20},{20,16},{24,28},{28,24},{1,5},{5... | collective-permute-start | bytes 786440 | tf_op jit(solution)/shard_map/ppermute | solution.py:628
  44.3 10.7 %collective-permute-start.12 = (bf16[528,128]{1,0:T(8,128)(2,1)S(1)}, bf16[528,128]{1,0:T(8,128)(2,1)S(1)}, u32[]{:S(2)}, u32[]{:S(2)}) collective-permute-start(bf16[528,128]{1,0:T(8,128)(2,1)S(1)} %get-tuple-element.164.mine_ref), channel_id=1, source_target_pairs={{0,4},{4,0},{8,12},{12,8},{16,20},{20,16},{24,28},{28,24},{1,5},{5... | collective-permute-start | bytes 405512 | tf_op jit(solution)/shard_map/ppermute | solution.py:628
  45.9 8.4 %collective-permute-start.13 = (bf16[512,128]{1,0:T(8,128)(2,1)S(1)}, bf16[512,128]{1,0:T(8,128)(2,1)S(1)}, u32[]{:S(2)}, u32[]{:S(2)}) collective-permute-start(bf16[512,128]{1,0:T(8,128)(2,1)S(1)} %get-tuple-element.165), channel_id=1, source_target_pairs={{0,2},{1,3},{2,0},{3,1},{4,6},{5,7},{6,4},{7,5},{8,10},{9,11},{10,... | collective-permute-start | bytes 393224 | tf_op jit(solution)/shard_map/ppermute | solution.py:628
  49.9 7.8 %collective-permute-start.17 = (bf16[512,128]{1,0:T(8,128)(2,1)S(1)}, bf16[512,128]{1,0:T(8,128)(2,1)S(1)}, u32[]{:S(2)}, u32[]{:S(2)}) collective-permute-start(bf16[512,128]{1,0:T(8,128)(2,1)S(1)} %get-tuple-element.182), channel_id=1, source_target_pairs={{0,8},{4,12},{8,0},{12,4},{16,24},{20,28},{24,16},{28,20},{1,9},{5... | collective-permute-start | bytes 393224 | tf_op jit(solution)/shard_map/ppermute | solution.py:628
  51.6 11.4 %collective-permute-start.18 = (bf16[512,128]{1,0:T(8,128)(2,1)S(1)}, bf16[512,128]{1,0:T(8,128)(2,1)S(1)}, u32[]{:S(2)}, u32[]{:S(2)}) collective-permute-start(bf16[512,128]{1,0:T(8,128)(2,1)S(1)} %get-tuple-element.183), channel_id=1, source_target_pairs={{0,16},{4,20},{8,24},{12,28},{16,0},{20,4},{24,8},{28,12},{1,17},{... | collective-permute-start | bytes 393224 | tf_op jit(solution)/shard_map/ppermute | solution.py:628
  54.2 8.9 %collective-permute-start.19 = (bf16[512,128]{1,0:T(8,128)(2,1)S(1)}, bf16[512,128]{1,0:T(8,128)(2,1)S(1)}, u32[]{:S(2)}, u32[]{:S(2)}) collective-permute-start(bf16[512,128]{1,0:T(8,128)(2,1)S(1)} %get-tuple-element.184), channel_id=1, source_target_pairs={{0,24},{4,28},{8,16},{12,20},{16,8},{20,12},{24,0},{28,4},{1,25},{... | collective-permute-start | bytes 393224 | tf_op jit(solution)/shard_map/ppermute | solution.py:628
  54.3 11.3 %collective-permute-start.6 = (bf16[128,512]{1,0:T(8,128)(2,1)S(1)}, bf16[128,512]{1,0:T(8,128)(2,1)S(1)}, u32[]{:S(2)}, u32[]{:S(2)}) collective-permute-start(bf16[128,512]{1,0:T(8,128)(2,1)S(1)} %get-tuple-element.143.to_other_ref), channel_id=1, source_target_pairs={{1,2},{2,1},{5,6},{6,5},{9,10},{10,9},{13,14},{14,13},{17,18},{18,... | collective-permute-start | bytes 393224 | tf_op jit(solution)/shard_map/ppermute | solution.py:636
  55.0 12.2 %collective-permute-start.7 = (bf16[128,512]{1,0:T(8,128)(2,1)S(1)}, bf16[128,512]{1,0:T(8,128)(2,1)S(1)}, u32[]{:S(2)}, u32[]{:S(2)}) collective-permute-start(bf16[128,512]{1,0:T(8,128)(2,1)S(1)} %get-tuple-element.144.to_pair_ref), channel_id=1, source_target_pairs={{0,1},{1,0},{2,3},{3,2},{4,5},{5,4},{6,7},{7,6},{8,9},{9,8},{10,11... | collective-permute-start | bytes 393224 | tf_op jit(solution)/shard_map/ppermute | solution.py:628
  57.7 14.5 %collective-permute-start.22 = (bf16[288,128]{1,0:T(8,128)(2,1)S(1)}, bf16[288,128]{1,0:T(8,128)(2,1)S(1)}, u32[]{:S(2)}, u32[]{:S(2)}) collective-permute-start(bf16[288,128]{1,0:T(8,128)(2,1)S(1)} %get-tuple-element.188), channel_id=1, source_target_pairs={{0,8},{4,12},{8,0},{12,4},{16,24},{20,28},{24,16},{28,20},{1,9},{5... | collective-permute-start | bytes 221192 | tf_op jit(solution)/shard_map/ppermute | solution.py:628
  63.0 9.2 %collective-permute-start.23 = (bf16[288,128]{1,0:T(8,128)(2,1)S(1)}, bf16[288,128]{1,0:T(8,128)(2,1)S(1)}, u32[]{:S(2)}, u32[]{:S(2)}) collective-permute-start(bf16[288,128]{1,0:T(8,128)(2,1)S(1)} %get-tuple-element.189), channel_id=1, source_target_pairs={{0,16},{4,20},{8,24},{12,28},{16,0},{20,4},{24,8},{28,12},{1,17},{... | collective-permute-start | bytes 221192 | tf_op jit(solution)/shard_map/ppermute | solution.py:628
  63.0 9.2 %collective-permute-start.24 = (bf16[288,128]{1,0:T(8,128)(2,1)S(1)}, bf16[288,128]{1,0:T(8,128)(2,1)S(1)}, u32[]{:S(2)}, u32[]{:S(2)}) collective-permute-start(bf16[288,128]{1,0:T(8,128)(2,1)S(1)} %get-tuple-element.190), channel_id=1, source_target_pairs={{0,24},{4,28},{8,16},{12,20},{16,8},{20,12},{24,0},{28,4},{1,25},{... | collective-permute-start | bytes 221192 | tf_op jit(solution)/shard_map/ppermute | solution.py:628
  65.7 5.8 %collective-permute-start.20 = (bf16[128,128]{1,0:T(8,128)(2,1)S(1)}, bf16[128,128]{1,0:T(8,128)(2,1)S(1)}, u32[]{:S(2)}, u32[]{:S(2)}) collective-permute-start(bf16[128,128]{1,0:T(8,128)(2,1)S(1)} %get-tuple-element.186), channel_id=1, source_target_pairs={{0,4},{4,0},{8,12},{12,8},{16,20},{20,16},{24,28},{28,24},{1,5},{5... | collective-permute-start | bytes 98312 | tf_op jit(solution)/shard_map/ppermute | solution.py:628
  67.2 5.0 %collective-permute-start.21 = (bf16[128,128]{1,0:T(8,128)(2,1)S(1)}, bf16[128,128]{1,0:T(8,128)(2,1)S(1)}, u32[]{:S(2)}, u32[]{:S(2)}) collective-permute-start(bf16[128,128]{1,0:T(8,128)(2,1)S(1)} %get-tuple-element.187), channel_id=1, source_target_pairs={{0,2},{1,3},{2,0},{3,1},{4,6},{5,7},{6,4},{7,5},{8,10},{9,11},{10,... | collective-permute-start | bytes 98312 | tf_op jit(solution)/shard_map/ppermute | solution.py:628

commit v6 on v5

--- a/solution.py
+++ b/solution.py
@@ -408,7 +408,7 @@
     (
         normed_ref, normed_o_ref, normed_p_ref, attended_o_ref, attended_p_ref, up_o_ref, up_p_ref,
         gq_o_ref, gq_p_ref, gk_ref, gk_o_ref, gk_p_ref, gv_ref, gv_o_ref, gv_p_ref,
-        send_ref, keep_ref,
+        *send_refs, keep_ref,
     ) = refs
     normed = stacked(normed_ref, normed_o_ref, normed_p_ref).T
     attended = stacked(attended_o_ref, attended_p_ref).T
@@ -422,7 +422,10 @@
     ens, mesh = lax.axis_index(ENS), lax.axis_index(MESH)
     for slot, left, rights in products:
         group, inner = slot // 2, slot % 2
-        for core, out_ref in ((1, send_ref), (0, keep_ref)):
+        send_ref, base = send_refs[0], 0
+        if len(send_refs) > 1:
+            send_ref, base = send_refs[group], group * (plan.weights // 2)
+        for core, out_ref, base in ((1, send_ref, base), (0, keep_ref, 0)):
             right = []
             for y in range(2):
                 col = pl.multiple_of(lax.bitwise_xor(mesh, y * 2 + core) * LANES, LANES)
@@ -435,49 +438,40 @@
                 x, z = lax.bitwise_and(place, 1), lax.shift_right_logical(place, 1)
                 for y in range(2):
                     first, second = (y, x) if group == 0 else (x, y)
-                    start = pl.multiple_of(plan.at(group, first, second, z) + inner * rows, rows)
+                    start = plan.at(group, first, second, z) + inner * rows - base
+                    start = pl.multiple_of(start, rows)
                     out_ref[pl.ds(start, rows), :] = value[
                         row * rows : (row + 1) * rows, y * LANES : (y + 1) * LANES
                     ]
 
 
-def stage_one(plan, keep_ref, came_ref, y_ref, x_ref, kept_ref):
+def stage_one(plan, group, keep_ref, came_ref, base, out_ref, kept_ref):
     size = plan.weights // 4
-    for group, out_ref in ((0, y_ref), (1, x_ref)):
-        start = 2 * group * size
-        kept_ref[group * size : (group + 1) * size, :] = keep_ref[
-            start : start + size, :
-        ] + came_ref[start : start + size, :].astype(F32)
-        start += size
-        out_ref[:size, :] = (
-            keep_ref[start : start + size, :] + came_ref[start : start + size, :].astype(F32)
-        ).astype(BF16)
-
-
-def stage_two(plan, kept_ref, y_ref, x_ref, to_x_ref, to_y_ref, next_ref):
+    start, inner = 2 * group * size, base
+    kept_ref[...] = keep_ref[start : start + size, :] + came_ref[inner : inner + size, :].astype(F32)
+    start, inner = start + size, inner + size
+    out_ref[...] = (
+        keep_ref[start : start + size, :] + came_ref[inner : inner + size, :].astype(F32)
+    ).astype(BF16)
+
+
+def stage_two(plan, kept_ref, in_ref, out_ref, next_ref):
     size = plan.weights // 8
-    for group, in_ref, out_ref in ((0, y_ref, to_x_ref), (1, x_ref, to_y_ref)):
-        start = 2 * group * size
-        next_ref[group * size : (group + 1) * size, :] = kept_ref[
-            start : start + size, :
-        ] + in_ref[:size, :].astype(F32)
-        out_ref[...] = (
-            kept_ref[start + size : start + 2 * size, :] + in_ref[size : 2 * size, :].astype(F32)
-        ).astype(BF16)
-
-
-def stage_three(plan, kept_ref, x_ref, y_ref, z_refs, last_ref):
+    next_ref[...] = kept_ref[:size, :] + in_ref[:size, :].astype(F32)
+    out_ref[...] = (kept_ref[size:, :] + in_ref[size : 2 * size, :].astype(F32)).astype(BF16)
+
+
+def stage_three(plan, kept_refs, in_refs, z_refs, last_ref):
     rows = plan.rows
-    for group, in_ref in enumerate((x_ref, y_ref)):
+    for group, (kept_ref, in_ref) in enumerate(zip(kept_refs, in_refs, strict=True)):
+        spot = slice(group * rows, (group + 1) * rows)
         for z in range(plan.deep):
-            start = (group * plan.deep + z) * rows
-            value = kept_ref[start : start + rows, :] + in_ref[z * rows : (z + 1) * rows, :].astype(
-                F32
-            )
+            at = slice(z * rows, (z + 1) * rows)
+            value = kept_ref[at, :] + in_ref[at, :].astype(F32)
             if z:
-                z_refs[z - 1][group * rows : (group + 1) * rows, :] = value.astype(BF16)
+                z_refs[z - 1][spot, :] = value.astype(BF16)
             else:
-                last_ref[group * rows : (group + 1) * rows, :] = value
+                last_ref[spot, :] = value
 
 
 def stage_across(plan, kept_ref, y_ref, x_ref, z_refs, last_ref):
@@ -495,15 +489,22 @@
 
 
 def start_scatter_kernel(plan, keep_ref, came_ref, y_ref, x_ref, kept_ref):
-    stage_one(plan, keep_ref, came_ref, y_ref, x_ref, kept_ref)
-
-
-def slot_a_kernel(
-    plan, keep1_ref, came1_ref, conds_ref, conds_came_ref, y_ref, x_ref, kept1_ref, film_ref,
+    size = plan.weights // 4
+    for group, out_ref in enumerate((y_ref, x_ref)):
+        kept = kept_ref.at[group * size : (group + 1) * size, :]
+        stage_one(plan, group, keep_ref, came_ref, 2 * group * size, out_ref, kept)
+
+
+def slot_ax_kernel(plan, keep1_ref, came1_ref, x_ref, kept1_ref):
+    stage_one(plan, 1, keep1_ref, came1_ref, 0, x_ref, kept1_ref)
+
+
+def slot_ay_kernel(
+    plan, keep1_ref, came1_ref, conds_ref, conds_came_ref, y_ref, kept1_ref, film_ref,
     total_ref, rows_ref,
 ):
     size = plan.weights // 4
-    stage_one(plan, keep1_ref, came1_ref, y_ref, x_ref, kept1_ref)
+    stage_one(plan, 0, keep1_ref, came1_ref, 0, y_ref.at[:size, :], kept1_ref)
     total_ref[...] = conds_ref[...] + conds_came_ref[...]
     mesh = lax.axis_index(MESH)
     part_rows = plan.film_rows // LAYERS
@@ -521,20 +522,22 @@
     stage_across(plan, kept2_ref, y2_ref, x2_ref, z_refs, last2_ref)
 
 
-def slot_b_kernel(
-    plan, kept1_ref, film_ref, y_ref, x_ref, embedding_ref, to_x_ref, to_y_ref, next1_ref
-):
+def slot_by_kernel(plan, kept1_ref, x_ref, to_y_ref, next1_ref):
+    stage_two(plan, kept1_ref, x_ref, to_y_ref, next1_ref)
+
+
+def slot_bx_kernel(plan, kept1_ref, film_ref, y_ref, embedding_ref, to_x_ref, next1_ref):
     size, small = plan.weights // 4, plan.weights // 8
-    stage_two(plan, kept1_ref, y_ref, x_ref, to_x_ref.at[:small, :], to_y_ref, next1_ref)
+    stage_two(plan, kept1_ref, y_ref, to_x_ref.at[:small, :], next1_ref)
     end = 2 * plan.film_rows
     total = film_ref[...] + get_pair(y_ref.at[size : size + end, :])
     put_pair(total, to_x_ref.at[small : small + end, :])
     put_noise(embedding_ref[:1, :], to_x_ref, small + end)
 
 
-def slot_c_kernel(plan, kept1_ref, x_ref, y_ref, mine_ref, *outs):
+def slot_c_kernel(plan, kept_x_ref, kept_y_ref, x_ref, y_ref, mine_ref, *outs):
     last1_ref, *z_refs = outs
-    stage_three(plan, kept1_ref, x_ref, y_ref, z_refs, last1_ref)
+    stage_three(plan, (kept_x_ref, kept_y_ref), (x_ref, y_ref), z_refs, last1_ref)
     small, end = plan.weights // 8, 2 * plan.rows
     for z_ref in z_refs:
         z_ref[end : end + plan.film, :] = mine_ref[small : small + plan.film, :]
@@ -763,16 +766,17 @@
         [full(F32), cond_shape], flops=4 * square,
     )
 
-    def weight_grads(*args):
+    def weight_grads(parts, *args):
         if not split:
             return call(plain_weight_kernel, args, [((4, width, width), F32)], flops=6 * square)
         return call(
             bind(split_weight_kernel, plan), args,
-            [block(plan.weights), block(plan.weights, F32)], flops=6 * square,
+            [block(plan.weights // parts)] * parts + [block(plan.weights, F32)],
+            flops=6 * square,
         )
 
     weights2 = weight_grads(
-        normed2, normed2_o, normed2_p, attended2_o, attended2_p, cot2[:rim], cot2[rim:],
+        1, normed2, normed2_o, normed2_p, attended2_o, attended2_p, cot2[:rim], cot2[rim:],
         gq2_o, gq2_p, gk2, gk2_o, gk2_p, gv2, gv2_o, gv2_p,
     )
     if split:
@@ -800,11 +804,11 @@
         0, next_o, back_o, k1_o, v1_o, own_o, over_o, parts
     )
     weights1 = weight_grads(
-        normed1, normed1_o, normed1_p, attended1_o, attended1_p, up_o, up_p,
+        2, normed1, normed1_o, normed1_p, attended1_o, attended1_p, up_o, up_p,
         gq1_o, gq1_p, gk1, gk1_o, gk1_p, gv1, gv1_o, gv1_p,
     )
     if split:
-        came = swap(weights1[0], MESH, 1)
+        core_x, core_y = swap(weights1[1], MESH, 1), swap(weights1[0], MESH, 1)
     back_o = exchange_other(to_other)
     back_p = swap(to_pair, MESH, 1)
     gn1, conds = call(
@@ -816,25 +820,34 @@
     if split:
         conds_came = swap(conds, MESH, 1)
         others = range(1, plan.deep)
-        to_y, to_x, kept1, film_mine = call(
-            bind(slot_a_kernel, plan), (weights1[1], came, conds, conds_came),
-            [block(sums // 4 + plan.film), block(sums // 4), block(sums // 2, F32),
-             block(plan.film_rows, F32)],
+        to_x, kept_x = call(
+            bind(slot_ax_kernel, plan), (weights1[2], core_x),
+            [block(sums // 4), block(sums // 4, F32)],
+        )
+        came_x = swap(to_x, ENS, 1)
+        to_y, kept_y, film_mine = call(
+            bind(slot_ay_kernel, plan), (weights1[2], core_y, conds, conds_came),
+            [block(sums // 4 + plan.film), block(sums // 4, F32), block(plan.film_rows, F32)],
             scratch=[(conds.shape, F32), block(plan.film_rows, F32)],
         )
-        came_y, came_x = swap(to_y, MESH, 2), swap(to_x, ENS, 1)
+        came_y = swap(to_y, MESH, 2)
         last2, *to_z = call(
             bind(across_kernel, plan), (kept2, y2, x2),
             [block(4 * plan.rows, F32)] + [block(4 * plan.rows) for _ in others],
         )
         came_z2 = [swap(to_z[z - 1], ENS, 2 * z) for z in others]
-        to_x, to_y, kept1 = call(
-            bind(slot_b_kernel, plan), (kept1, film_mine, came_y, came_x, emb_row),
-            [block(sums // 8 + plan.film), block(sums // 8), block(sums // 4, F32)],
-        )
-        came_x, came_y = swap(to_x, ENS, 1), swap(to_y, MESH, 2)
+        to_y, kept_y_next = call(
+            bind(slot_by_kernel, plan), (kept_x, came_x),
+            [block(sums // 8), block(sums // 8, F32)],
+        )
+        came_y2 = swap(to_y, MESH, 2)
+        to_x, kept_x_next = call(
+            bind(slot_bx_kernel, plan), (kept_y, film_mine, came_y, emb_row),
+            [block(sums // 8 + plan.film), block(sums // 8, F32)],
+        )
+        came_x = swap(to_x, ENS, 1)
         last1, *to_z = call(
-            bind(slot_c_kernel, plan), (kept1, came_x, came_y, to_x),
+            bind(slot_c_kernel, plan), (kept_x_next, kept_y_next, came_x, came_y2, to_x),
             [block(2 * plan.rows, F32)] + [block(2 * plan.rows + 2 * plan.film) for _ in others],
         )
         came_z1 = [swap(to_z[z - 1], ENS, 2 * z) for z in others]

time: 74 us -> 74.6 us (level)
  starting transfers between devices: 35.7 us -> 36.5 us
    ppermute x21 -> x22, starting transfers between devices: 32.9 us -> 33.7 us  [swap(): return lax.ppermute(block, axis, [(i, i ^ bit) for i in range(count)])]
    ppermute x21 -> x22, waiting for transfers between devices: 15.2 us -> 15.4 us  [swap(): return lax.ppermute(block, axis, [(i, i ^ bit) for i in range(count)])]
    pallas_call x21 -> x23, Pallas kernels: 20.7 us -> 20.5 us  [call(): pl.pallas_call(kernel, out_shape=[jax.ShapeDtypeStruct(shape, kind) for s...]
  transfers between devices with their start and end apart: 25 -> 26, of which waited for: 6 -> 7; matrix products, arithmetic and copies ran while one was open for 0% -> 0% of each run, Pallas kernels for 22% -> 21%
where the time goes in v6:
time: 74.6 us; the launch traced here: 73.9 us
  starting transfers between devices  36.5 us (49%)
  Pallas kernels  20.5 us (27%)
  waiting for transfers between devices  15.4 us (21%)
  between operations  1.52 us (2%)
    ppermute x22, starting transfers between devices, swap(): return lax.ppermute(block, axis, [(i, i ^ bit) for i in range(count)])  33.7 us
    pallas_call x23, Pallas kernels, call(): pl.pallas_call(kernel, out_shape=[jax.ShapeDtypeStruct(shape, kind) for s...  20.5 us
    ppermute x22, waiting for transfers between devices, swap(): return lax.ppermute(block, axis, [(i, i ^ bit) for i in range(count)])  15.4 us
    ppermute x4, starting transfers between devices, exchange_other(): return lax.ppermute(to_other, MESH, route)  2.83 us
  transfers between devices with their start and end apart: 26, of which 7 were waited for; matrix products, arithmetic and copies ran while one was open for 0% of the time, Pallas kernels for 21%

profile of v6, /device:TPU:0, one launch (start us, length us, event | category | flops | bytes accessed | tf_op | source)
XLA Modules:
  0.0 73.9 jit_solution(5937987114436406825)
XLA Ops:
  1.3 1.2 %shard_map.94 = (bf16[128,512]{1,0:T(8,128)(2,1)S(1)}, bf16[128,512]{1,0:T(8,128)(2,1)S(1)}, s32[32,256]{1,0:T(8,128)S(1)}, s32[32,256]{1,0:T(8,128)S(1)}, f32[2...) custom-call(bf16[256,512]{1,0:T(8,128)(2,1)} %bitcast.6, s32[32,256]{1,0:T(8,128)} %bitcast.8, s32[32,256]{1,0:T(8,128)} %bitcast.9, ...), custom_call_target="tpu_custom_call" | custom-call | bytes 1183748 | tf_op jit(solution)/shard_map/pallas_call | solution.py:618
  3.1 4.4 %collective-permute-start.1 = (bf16[128,512]{1,0:T(8,128)(2,1)S(1)}, bf16[128,512]{1,0:T(8,128)(2,1)S(1)}, u32[]{:S(2)}, u32[]{:S(2)}) collective-permute-start(bf16[128,512]{1,0:T(8,128)(2,1)S(1)} %get-tuple-element.102.x_p_ref.x_ref), channel_id=1, source_target_pairs={{0,1},{1,0},{2,3},{3,2},{4,5},{5,4},{6,7},{7,6},{8,9},{9,8},{10,11... | collective-permute-start | bytes 393224 | tf_op jit(solution)/shard_map/ppermute | solution.py:631
  7.5 2.5 %shard_map.95 = (f32[2,1024]{1,0:T(2,128)S(1)}, f32[128,384]{1,0:T(8,128)S(1)}, f32[128,384]{1,0:T(8,128)S(1)}, bf16[256,512]{1,0:T(8,128)(2,1)S(1)}, bf16[256,5...) custom-call(bf16[128,512]{1,0:T(8,128)(2,1)S(1)} %get-tuple-element., ...), custom_call_target="tpu_custom_call" | custom-call | flops 402653184 | bytes 10432512 | tf_op jit(solution)/shard_map/pallas_call | solution.py:618
  10.1 1.2 %shard_map.96 = (bf16[128,512]{1,0:T(8,128)(2,1)S(1)}, bf16[128,512]{1,0:T(8,128)(2,1)S(1)}, bf16[128,512]{1,0:T(8,128)(2,1)S(1)}, bf16[128,512]{1,0:T(8,128)(2,...) custom-call(bf16[128,512]{1,0:T(8,128)(2,1)S(1)} %get-tuple-element.101.x_o, ...), custom_call_target="tpu_custom_call" | custom-call | flops 268435456 | bytes 6496256 | tf_op jit(solution)/shard_map/pallas_call | solution.py:618
  11.9 1.2 %shard_map.97 = (bf16[128,512]{1,0:T(8,128)(2,1)S(1)}, bf16[128,512]{1,0:T(8,128)(2,1)S(1)}, bf16[128,512]{1,0:T(8,128)(2,1)S(1)}, bf16[128,512]{1,0:T(8,128)(2,...) custom-call(bf16[128,512]{1,0:T(8,128)(2,1)S(1)} %get-tuple-element.102.x_p, ...), custom_call_target="tpu_custom_call" | custom-call | flops 268435456 | bytes 6496256 | tf_op jit(solution)/shard_map/pallas_call | solution.py:618
  13.1 3.1 %collective-permute-start.3 = (bf16[128,512]{1,0:T(8,128)(2,1)S(1)}, bf16[128,512]{1,0:T(8,128)(2,1)S(1)}, u32[]{:S(2)}, u32[]{:S(2)}) collective-permute-start(bf16[128,512]{1,0:T(8,128)(2,1)S(1)} %get-tuple-element.115.x_p_ref.next_ref), channel_id=1, source_target_pairs={{0,1},{1,0},{2,3},{3,2},{4,5},{5,4},{6,7},{7,6},{8,9},{9,8},{10,11... | collective-permute-start | bytes 393224 | tf_op jit(solution)/shard_map/ppermute | solution.py:631
  16.2 0.9 %shard_map.98 = (bf16[256,512]{1,0:T(8,128)(2,1)S(1)}, bf16[256,512]{1,0:T(8,128)(2,1)S(1)}, bf16[256,512]{1,0:T(8,128)(2,1)S(1)}, bf16[256,512]{1,0:T(8,128)(2,...) custom-call(bf16[128,512]{1,0:T(8,128)(2,1)S(1)} %get-tuple-element.113.x_o_ref.next_ref, ...), custom_call_target="tpu_custom_call" | custom-call | flops 536870912 | bytes 6299648 | tf_op jit(solution)/shard_map/pallas_call | solution.py:618
  17.2 2.0 %shard_map.99 = (bf16[128,512]{1,0:T(8,128)(2,1)S(1)}, bf16[128,512]{1,0:T(8,128)(2,1)S(1)}, bf16[128,512]{1,0:T(8,128)(2,1)S(1)}, f32[256,512]{1,0:T(8,128)S(1)...) custom-call(bf16[128,512]{1,0:T(8,128)(2,1)S(1)} %collective-permute, ...), custom_call_target="tpu_custom_call" | custom-call | flops 536870912 | bytes 7413760 | tf_op jit(solution)/shard_map/pallas_call | solution.py:618
  19.2 2.0 %shard_map.100 = (bf16[128,512]{1,0:T(8,128)(2,1)S(1)}, bf16[128,512]{1,0:T(8,128)(2,1)S(1)}, bf16[128,512]{1,0:T(8,128)(2,1)S(1)}, bf16[256,512]{1,0:T(8,128)(2...) custom-call(bf16[128,512]{1,0:T(8,128)(2,1)S(1)} %collective-permute, ...), custom_call_target="tpu_custom_call" | custom-call | flops 536870912 | bytes 7938048 | tf_op jit(solution)/shard_map/pallas_call | solution.py:618
  21.2 1.0 %shard_map.112 = (bf16[4096,128]{1,0:T(8,128)(2,1)S(1)}, f32[4096,128]{1,0:T(8,128)S(1)}) custom-call(bf16[256,512]{1,0:T(8,128)(2,1)S(1)} %get-tuple-element.173.refs_0_, bf16[128,512]{1,0:T(8,128)(2,1)S(1)} %get-tuple-element.174.refs_1_, bf16[128,512]{1,0:T(8,128)(2,1)S(1)} %get-tuple-element.175.refs_2_, ...), custom_call_target="tpu_custom_call" | custom-call | flops 805306368 | bytes 5505024 | tf_op jit(solution)/shard_map/pallas_call | solution.py:618
  22.8 0.8 %collective-permute-start.4 = (bf16[128,512]{1,0:T(8,128)(2,1)S(1)}, bf16[128,512]{1,0:T(8,128)(2,1)S(1)}, u32[]{:S(2)}, u32[]{:S(2)}) collective-permute-start(bf16[128,512]{1,0:T(8,128)(2,1)S(1)} %get-tuple-element.127.to_other_ref), channel_id=1, source_target_pairs={{1,2},{2,1},{5,6},{6,5},{9,10},{10,9},{13,14},{14,13},{17,18},{18,... | collective-permute-start | bytes 393224 | tf_op jit(solution)/shard_map/ppermute | solution.py:639
  24.3 0.8 %collective-permute-done.5.back_ref = bf16[128,512]{1,0:T(8,128)(2,1)S(1)} collective-permute-done((bf16[128,512]{1,0:T(8,128)(2,1)S(1)}, bf16[128,512]{1,0:T(8,128)(2,1)S(1)}, u32[]{:S(2)}, u32[]{:S(2)}) %collective-permute-start.5) | collective-permute-done | bytes 131104 | tf_op jit(solution)/shard_map/ppermute | solution.py:631
  25.1 1.7 %shard_map.102 = (bf16[128,512]{1,0:T(8,128)(2,1)S(1)}, bf16[128,512]{1,0:T(8,128)(2,1)S(1)}, f32[256,512]{1,0:T(8,128)S(1)}, f32[256,512]{1,0:T(8,128)S(1)}, bf...) custom-call(bf16[128,512]{1,0:T(8,128)(2,1)S(1)} %get-tuple-element.115.x_p_ref.next_ref, ...), custom_call_target="tpu_custom_call" | custom-call | flops 536870912 | bytes 8396800 | tf_op jit(solution)/shard_map/pallas_call | solution.py:618
  26.8 1.7 %shard_map.103 = (bf16[128,512]{1,0:T(8,128)(2,1)S(1)}, bf16[128,512]{1,0:T(8,128)(2,1)S(1)}, bf16[256,512]{1,0:T(8,128)(2,1)S(1)}, bf16[256,512]{1,0:T(8,128)(2...) custom-call(bf16[128,512]{1,0:T(8,128)(2,1)S(1)} %get-tuple-element.113.x_o_ref.ne, ...), custom_call_target="tpu_custom_call" | custom-call | flops 536870912 | bytes 8921088 | tf_op jit(solution)/shard_map/pallas_call | solution.py:618
  28.6 1.0 %shard_map.106 = (bf16[2048,128]{1,0:T(8,128)(2,1)S(1)}, bf16[2048,128]{1,0:T(8,128)(2,1)S(1)}, f32[4096,128]{1,0:T(8,128)S(1)}) custom-call(bf16[256,512]{1,0:T(8,128)(2,1)S(1)} %get-tuple-element.150.refs_0_, bf16[128,512]{1,0:T(8,128)(2,1)S(1)} %get-tuple-element.151.refs_1_, bf16[128,512]{1,0:T(8,128)(2,1)S(1)} %get-tuple-element.152.refs_2_, ...), custom_call_target="tpu_custom_call" | custom-call | flops 805306368 | bytes 5505024 | tf_op jit(solution)/shard_map/pallas_call | solution.py:618
  29.6 2.7 %collective-permute-start.8 = (bf16[2048,128]{1,0:T(8,128)(2,1)S(1)}, bf16[2048,128]{1,0:T(8,128)(2,1)S(1)}, u32[]{:S(2)}, u32[]{:S(2)}) collective-permute-start(bf16[2048,128]{1,0:T(8,128)(2,1)S(1)} %get-tuple-element.160), channel_id=1, source_target_pairs={{0,1},{1,0},{2,3},{3,2},{4,5},{5,4},{6,7},{7,6},{8,9},{9,8},{10,11... | collective-permute-start | bytes 1572872 | tf_op jit(solution)/shard_map/ppermute | solution.py:631
  33.5 1.0 %collective-permute-done.9.conds_came_ref = f32[2,1024]{1,0:T(2,128)S(1)} collective-permute-done((f32[2,1024]{1,0:T(2,128)S(1)}, f32[2,1024]{1,0:T(2,128)S(1)}, u32[]{:S(2)}, u32[]{:S(2)}) %collective-permute-start.9) | collective-permute-done | bytes 8224 | tf_op jit(solution)/shard_map/ppermute | solution.py:631
  35.2 1.6 %collective-permute-start.12 = (bf16[1024,128]{1,0:T(8,128)(2,1)S(1)}, bf16[1024,128]{1,0:T(8,128)(2,1)S(1)}, u32[]{:S(2)}, u32[]{:S(2)}) collective-permute-start(bf16[1024,128]{1,0:T(8,128)(2,1)S(1)} %get-tuple-element.168), channel_id=1, source_target_pairs={{0,4},{4,0},{8,12},{12,8},{16,20},{20,16},{24,28},{28,24},{1,5},{5... | collective-permute-start | bytes 786440 | tf_op jit(solution)/shard_map/ppermute | solution.py:631
  36.9 1.8 %collective-permute-start.16 = (bf16[1024,128]{1,0:T(8,128)(2,1)S(1)}, bf16[1024,128]{1,0:T(8,128)(2,1)S(1)}, u32[]{:S(2)}, u32[]{:S(2)}) collective-permute-start(bf16[1024,128]{1,0:T(8,128)(2,1)S(1)} %get-tuple-element.185), channel_id=1, source_target_pairs={{0,2},{1,3},{2,0},{3,1},{4,6},{5,7},{6,4},{7,5},{8,10},{9,11},{10,... | collective-permute-start | bytes 786440 | tf_op jit(solution)/shard_map/ppermute | solution.py:631
  39.3 4.8 %collective-permute-done.10.y_ref = bf16[1040,128]{1,0:T(8,128)(2,1)S(1)} collective-permute-done((bf16[1040,128]{1,0:T(8,128)(2,1)S(1)}, bf16[1040,128]{1,0:T(8,128)(2,1)S(1)}, u32[]{:S(2)}, u32[]{:S(2)}) %collective-permute-start.10) | collective-permute-done | bytes 266272 | tf_op jit(solution)/shard_map/ppermute | solution.py:631
  44.1 1.6 %collective-permute-start.13 = (bf16[528,128]{1,0:T(8,128)(2,1)S(1)}, bf16[528,128]{1,0:T(8,128)(2,1)S(1)}, u32[]{:S(2)}, u32[]{:S(2)}) collective-permute-start(bf16[528,128]{1,0:T(8,128)(2,1)S(1)} %get-tuple-element.170.mine_ref), channel_id=1, source_target_pairs={{0,4},{4,0},{8,12},{12,8},{16,20},{20,16},{24,28},{28,24},{1,5},{5... | collective-permute-start | bytes 405512 | tf_op jit(solution)/shard_map/ppermute | solution.py:631
  46.3 3.4 %collective-permute-done.16.y2_ref = bf16[1024,128]{1,0:T(8,128)(2,1)S(1)} collective-permute-done((bf16[1024,128]{1,0:T(8,128)(2,1)S(1)}, bf16[1024,128]{1,0:T(8,128)(2,1)S(1)}, u32[]{:S(2)}, u32[]{:S(2)}) %collective-permute-start.16) | collective-permute-done | bytes 262176 | tf_op jit(solution)/shard_map/ppermute | solution.py:631
  50.1 1.6 %collective-permute-start.18 = (bf16[512,128]{1,0:T(8,128)(2,1)S(1)}, bf16[512,128]{1,0:T(8,128)(2,1)S(1)}, u32[]{:S(2)}, u32[]{:S(2)}) collective-permute-start(bf16[512,128]{1,0:T(8,128)(2,1)S(1)} %get-tuple-element.188), channel_id=1, source_target_pairs={{0,8},{4,12},{8,0},{12,4},{16,24},{20,28},{24,16},{28,20},{1,9},{5... | collective-permute-start | bytes 393224 | tf_op jit(solution)/shard_map/ppermute | solution.py:631
  51.8 2.6 %collective-permute-start.19 = (bf16[512,128]{1,0:T(8,128)(2,1)S(1)}, bf16[512,128]{1,0:T(8,128)(2,1)S(1)}, u32[]{:S(2)}, u32[]{:S(2)}) collective-permute-start(bf16[512,128]{1,0:T(8,128)(2,1)S(1)} %get-tuple-element.189), channel_id=1, source_target_pairs={{0,16},{4,20},{8,24},{12,28},{16,0},{20,4},{24,8},{28,12},{1,17},{... | collective-permute-start | bytes 393224 | tf_op jit(solution)/shard_map/ppermute | solution.py:631
  55.3 3.2 %collective-permute-start.7 = (bf16[128,512]{1,0:T(8,128)(2,1)S(1)}, bf16[128,512]{1,0:T(8,128)(2,1)S(1)}, u32[]{:S(2)}, u32[]{:S(2)}) collective-permute-start(bf16[128,512]{1,0:T(8,128)(2,1)S(1)} %get-tuple-element.147.to_pair_ref), channel_id=1, source_target_pairs={{0,1},{1,0},{2,3},{3,2},{4,5},{5,4},{6,7},{7,6},{8,9},{9,8},{10,11... | collective-permute-start | bytes 393224 | tf_op jit(solution)/shard_map/ppermute | solution.py:631
  59.3 4.2 %collective-permute-done.19.refs_1_ = bf16[512,128]{1,0:T(8,128)(2,1)S(1)} collective-permute-done((bf16[512,128]{1,0:T(8,128)(2,1)S(1)}, bf16[512,128]{1,0:T(8,128)(2,1)S(1)}, u32[]{:S(2)}, u32[]{:S(2)}) %collective-permute-start.19) | collective-permute-done | bytes 131104 | tf_op jit(solution)/shard_map/ppermute | solution.py:631
  63.4 2.7 %collective-permute-start.25 = (bf16[288,128]{1,0:T(8,128)(2,1)S(1)}, bf16[288,128]{1,0:T(8,128)(2,1)S(1)}, u32[]{:S(2)}, u32[]{:S(2)}) collective-permute-start(bf16[288,128]{1,0:T(8,128)(2,1)S(1)} %get-tuple-element.196), channel_id=1, source_target_pairs={{0,24},{4,28},{8,16},{12,20},{16,8},{20,12},{24,0},{28,4},{1,25},{... | collective-permute-start | bytes 221192 | tf_op jit(solution)/shard_map/ppermute | solution.py:631
  66.2 1.6 %collective-permute-start.21 = (bf16[128,128]{1,0:T(8,128)(2,1)S(1)}, bf16[128,128]{1,0:T(8,128)(2,1)S(1)}, u32[]{:S(2)}, u32[]{:S(2)}) collective-permute-start(bf16[128,128]{1,0:T(8,128)(2,1)S(1)} %get-tuple-element.192), channel_id=1, source_target_pairs={{0,4},{4,0},{8,12},{12,8},{16,20},{20,16},{24,28},{28,24},{1,5},{5... | collective-permute-start | bytes 98312 | tf_op jit(solution)/shard_map/ppermute | solution.py:631
  67.8 3.4 %collective-permute-start.22 = (bf16[128,128]{1,0:T(8,128)(2,1)S(1)}, bf16[128,128]{1,0:T(8,128)(2,1)S(1)}, u32[]{:S(2)}, u32[]{:S(2)}) collective-permute-start(bf16[128,128]{1,0:T(8,128)(2,1)S(1)} %get-tuple-element.193), channel_id=1, source_target_pairs={{0,2},{1,3},{2,0},{3,1},{4,6},{5,7},{6,4},{7,5},{8,10},{9,11},{10,... | collective-permute-start | bytes 98312 | tf_op jit(solution)/shard_map/ppermute | solution.py:631
  71.1 1.1 %shard_map.105 = bf16[256,512]{1,0:T(8,128)(2,1)} custom-call(bf16[128,512]{1,0:T(8,128)(2,1)S(1)} %get-tuple-element.101.x_o_ref.x_ref, bf16[128,512]{1,0:T(8,128)(2,1)S(1)} %get-tuple-element.102.x_p_ref.x_ref, bf16[128,512]{1,0:T(8,128)(2,1)S(1)} %get-tuple-element.140.up_o_ref.refs_5_, bf16[128,512]{1,0:T(8,128)(2,1)S(1)} %get-tuple-element.141.up_p_ref.refs_6_, ...), custom_call_target="tpu_custom_call" | custom-call | bytes 1581056 | tf_op jit(solution)/shard_map/pallas_call | solution.py:618
  72.3 0.8 %collective-permute-done.22.late_y_ref = bf16[128,128]{1,0:T(8,128)(2,1)S(1)} collective-permute-done((bf16[128,128]{1,0:T(8,128)(2,1)S(1)}, bf16[128,128]{1,0:T(8,128)(2,1)S(1)}, u32[]{:S(2)}, u32[]{:S(2)}) %collective-permute-start.22) | collective-permute-done | bytes 32800 | tf_op jit(solution)/shard_map/ppermute | solution.py:631
  73.0 0.9 %shard_map.116 = (f32[2,4,64,128]{3,2,1,0:T(8,128)}, f32[2,32,256]{2,1,0:T(8,128)}) custom-call(f32[256,128]{1,0:T(8,128)S(1)} %get-tuple-element.172.last1_ref, f32[256,128]{1,0:T(8,128)S(1)} %get-tuple-element.191.kept2_ref, bf16[128,128]{1,0:T(8,128)(2,1)S(1)} %collective-permute-done.21.late_x_ref, ...), custom_call_target="tpu_custom_call" | custom-call | bytes 1146880 | tf_op jit(solution)/shard_map/pallas_call | solution.py:618
  (46 shorter events, 8.2 us)
Async XLA Ops:
  2.5 7.6 %collective-permute-start = (bf16[128,512]{1,0:T(8,128)(2,1)S(1)}, bf16[128,512]{1,0:T(8,128)(2,1)S(1)}, u32[]{:S(2)}, u32[]{:S(2)}) collective-permute-start(bf16[128,512]{1,0:T(8,128)(2,1)S(1)} %get-tuple-element.101.x_o_ref.x_ref), channel_id=1, source_target_pairs={{1,2},{2,1},{5,6},{6,5},{9,10},{10,9},{13,14},{14,13},{17,18},{18,... | collective-permute-start | bytes 393224 | tf_op jit(solution)/shard_map/ppermute | solution.py:639
  3.1 8.8 %collective-permute-start.1 = (bf16[128,512]{1,0:T(8,128)(2,1)S(1)}, bf16[128,512]{1,0:T(8,128)(2,1)S(1)}, u32[]{:S(2)}, u32[]{:S(2)}) collective-permute-start(bf16[128,512]{1,0:T(8,128)(2,1)S(1)} %get-tuple-element.102.x_p_ref.x_ref), channel_id=1, source_target_pairs={{0,1},{1,0},{2,3},{3,2},{4,5},{5,4},{6,7},{7,6},{8,9},{9,8},{10,11... | collective-permute-start | bytes 393224 | tf_op jit(solution)/shard_map/ppermute | solution.py:631
  10.1 6.1 %copy-start = (bf16[1,256,512]{2,1,0:T(8,128)(2,1)S(1)}, bf16[1,256,512]{2,1,0:T(8,128)(2,1)}, u32[]{:S(2)}) copy-start(bf16[1,256,512]{2,1,0:T(8,128)(2,1)} %param.8) | copy-start | bytes 786436
  11.2 7.9 %collective-permute-start.2 = (bf16[128,512]{1,0:T(8,128)(2,1)S(1)}, bf16[128,512]{1,0:T(8,128)(2,1)S(1)}, u32[]{:S(2)}, u32[]{:S(2)}) collective-permute-start(bf16[128,512]{1,0:T(8,128)(2,1)S(1)} %get-tuple-element.113.x_o_ref.next_ref), channel_id=1, source_target_pairs={{1,2},{2,1},{5,6},{6,5},{9,10},{10,9},{13,14},{14,13},{17,18},{18,... | collective-permute-start | bytes 393224 | tf_op jit(solution)/shard_map/ppermute | solution.py:639
  13.1 4.1 %collective-permute-start.3 = (bf16[128,512]{1,0:T(8,128)(2,1)S(1)}, bf16[128,512]{1,0:T(8,128)(2,1)S(1)}, u32[]{:S(2)}, u32[]{:S(2)}) collective-permute-start(bf16[128,512]{1,0:T(8,128)(2,1)S(1)} %get-tuple-element.115.x_p_ref.next_ref), channel_id=1, source_target_pairs={{0,1},{1,0},{2,3},{3,2},{4,5},{5,4},{6,7},{7,6},{8,9},{9,8},{10,11... | collective-permute-start | bytes 393224 | tf_op jit(solution)/shard_map/ppermute | solution.py:631
  22.2 14.5 %collective-permute-start.15 = (bf16[4096,128]{1,0:T(8,128)(2,1)S(1)}, bf16[4096,128]{1,0:T(8,128)(2,1)S(1)}, u32[]{:S(2)}, u32[]{:S(2)}) collective-permute-start(bf16[4096,128]{1,0:T(8,128)(2,1)S(1)} %get-tuple-element.183), channel_id=1, source_target_pairs={{0,1},{1,0},{2,3},{3,2},{4,5},{5,4},{6,7},{7,6},{8,9},{9,8},{10,11... | collective-permute-start | bytes 3145736 | tf_op jit(solution)/shard_map/ppermute | solution.py:631
  22.6 2.5 %collective-permute-start.5 = (bf16[128,512]{1,0:T(8,128)(2,1)S(1)}, bf16[128,512]{1,0:T(8,128)(2,1)S(1)}, u32[]{:S(2)}, u32[]{:S(2)}) collective-permute-start(bf16[128,512]{1,0:T(8,128)(2,1)S(1)} %get-tuple-element.128.to_pair_ref), channel_id=1, source_target_pairs={{0,1},{1,0},{2,3},{3,2},{4,5},{5,4},{6,7},{7,6},{8,9},{9,8},{10,11... | collective-permute-start | bytes 393224 | tf_op jit(solution)/shard_map/ppermute | solution.py:631
  22.8 4.0 %collective-permute-start.4 = (bf16[128,512]{1,0:T(8,128)(2,1)S(1)}, bf16[128,512]{1,0:T(8,128)(2,1)S(1)}, u32[]{:S(2)}, u32[]{:S(2)}) collective-permute-start(bf16[128,512]{1,0:T(8,128)(2,1)S(1)} %get-tuple-element.127.to_other_ref), channel_id=1, source_target_pairs={{1,2},{2,1},{5,6},{6,5},{9,10},{10,9},{13,14},{14,13},{17,18},{18,... | collective-permute-start | bytes 393224 | tf_op jit(solution)/shard_map/ppermute | solution.py:639
  29.6 5.0 %collective-permute-start.8 = (bf16[2048,128]{1,0:T(8,128)(2,1)S(1)}, bf16[2048,128]{1,0:T(8,128)(2,1)S(1)}, u32[]{:S(2)}, u32[]{:S(2)}) collective-permute-start(bf16[2048,128]{1,0:T(8,128)(2,1)S(1)} %get-tuple-element.160), channel_id=1, source_target_pairs={{0,1},{1,0},{2,3},{3,2},{4,5},{5,4},{6,7},{7,6},{8,9},{9,8},{10,11... | collective-permute-start | bytes 1572872 | tf_op jit(solution)/shard_map/ppermute | solution.py:631
  32.2 2.8 %collective-permute-start.11 = (bf16[2048,128]{1,0:T(8,128)(2,1)S(1)}, bf16[2048,128]{1,0:T(8,128)(2,1)S(1)}, u32[]{:S(2)}, u32[]{:S(2)}) collective-permute-start(bf16[2048,128]{1,0:T(8,128)(2,1)S(1)} %get-tuple-element.166), channel_id=1, source_target_pairs={{0,1},{1,0},{2,3},{3,2},{4,5},{5,4},{6,7},{7,6},{8,9},{9,8},{10,11... | collective-permute-start | bytes 1572872 | tf_op jit(solution)/shard_map/ppermute | solution.py:631
  33.0 1.5 %collective-permute-start.9 = (f32[2,1024]{1,0:T(2,128)S(1)}, f32[2,1024]{1,0:T(2,128)S(1)}, u32[]{:S(2)}, u32[]{:S(2)}) collective-permute-start(f32[2,1024]{1,0:T(2,128)S(1)} %get-tuple-element.161.conds_ref), channel_id=1, source_target_pairs={{0,1},{1,0},{2,3},{3,2},{4,5},{5,4},{6,7},{7,6},{8,9},{9,8},{10,11... | collective-permute-start | bytes 24584 | tf_op jit(solution)/shard_map/ppermute | solution.py:631
  34.7 9.3 %collective-permute-start.10 = (bf16[1040,128]{1,0:T(8,128)(2,1)S(1)}, bf16[1040,128]{1,0:T(8,128)(2,1)S(1)}, u32[]{:S(2)}, u32[]{:S(2)}) collective-permute-start(bf16[1040,128]{1,0:T(8,128)(2,1)S(1)} %get-tuple-element.164), channel_id=1, source_target_pairs={{0,2},{1,3},{2,0},{3,1},{4,6},{5,7},{6,4},{7,5},{8,10},{9,11},{10,... | collective-permute-start | bytes 798728 | tf_op jit(solution)/shard_map/ppermute | solution.py:631
  35.2 10.5 %collective-permute-start.12 = (bf16[1024,128]{1,0:T(8,128)(2,1)S(1)}, bf16[1024,128]{1,0:T(8,128)(2,1)S(1)}, u32[]{:S(2)}, u32[]{:S(2)}) collective-permute-start(bf16[1024,128]{1,0:T(8,128)(2,1)S(1)} %get-tuple-element.168), channel_id=1, source_target_pairs={{0,4},{4,0},{8,12},{12,8},{16,20},{20,16},{24,28},{28,24},{1,5},{5... | collective-permute-start | bytes 786440 | tf_op jit(solution)/shard_map/ppermute | solution.py:631
  36.9 12.8 %collective-permute-start.16 = (bf16[1024,128]{1,0:T(8,128)(2,1)S(1)}, bf16[1024,128]{1,0:T(8,128)(2,1)S(1)}, u32[]{:S(2)}, u32[]{:S(2)}) collective-permute-start(bf16[1024,128]{1,0:T(8,128)(2,1)S(1)} %get-tuple-element.185), channel_id=1, source_target_pairs={{0,2},{1,3},{2,0},{3,1},{4,6},{5,7},{6,4},{7,5},{8,10},{9,11},{10,... | collective-permute-start | bytes 786440 | tf_op jit(solution)/shard_map/ppermute | solution.py:631
  38.7 11.3 %collective-permute-start.17 = (bf16[1024,128]{1,0:T(8,128)(2,1)S(1)}, bf16[1024,128]{1,0:T(8,128)(2,1)S(1)}, u32[]{:S(2)}, u32[]{:S(2)}) collective-permute-start(bf16[1024,128]{1,0:T(8,128)(2,1)S(1)} %get-tuple-element.186), channel_id=1, source_target_pairs={{0,4},{4,0},{8,12},{12,8},{16,20},{20,16},{24,28},{28,24},{1,5},{5... | collective-permute-start | bytes 786440 | tf_op jit(solution)/shard_map/ppermute | solution.py:631
  44.1 11.1 %collective-permute-start.13 = (bf16[528,128]{1,0:T(8,128)(2,1)S(1)}, bf16[528,128]{1,0:T(8,128)(2,1)S(1)}, u32[]{:S(2)}, u32[]{:S(2)}) collective-permute-start(bf16[528,128]{1,0:T(8,128)(2,1)S(1)} %get-tuple-element.170.mine_ref), channel_id=1, source_target_pairs={{0,4},{4,0},{8,12},{12,8},{16,20},{20,16},{24,28},{28,24},{1,5},{5... | collective-permute-start | bytes 405512 | tf_op jit(solution)/shard_map/ppermute | solution.py:631
  45.7 8.9 %collective-permute-start.14 = (bf16[512,128]{1,0:T(8,128)(2,1)S(1)}, bf16[512,128]{1,0:T(8,128)(2,1)S(1)}, u32[]{:S(2)}, u32[]{:S(2)}) collective-permute-start(bf16[512,128]{1,0:T(8,128)(2,1)S(1)} %get-tuple-element.171), channel_id=1, source_target_pairs={{0,2},{1,3},{2,0},{3,1},{4,6},{5,7},{6,4},{7,5},{8,10},{9,11},{10,... | collective-permute-start | bytes 393224 | tf_op jit(solution)/shard_map/ppermute | solution.py:631
  50.1 8.4 %collective-permute-start.18 = (bf16[512,128]{1,0:T(8,128)(2,1)S(1)}, bf16[512,128]{1,0:T(8,128)(2,1)S(1)}, u32[]{:S(2)}, u32[]{:S(2)}) collective-permute-start(bf16[512,128]{1,0:T(8,128)(2,1)S(1)} %get-tuple-element.188), channel_id=1, source_target_pairs={{0,8},{4,12},{8,0},{12,4},{16,24},{20,28},{24,16},{28,20},{1,9},{5... | collective-permute-start | bytes 393224 | tf_op jit(solution)/shard_map/ppermute | solution.py:631
  51.8 11.7 %collective-permute-start.19 = (bf16[512,128]{1,0:T(8,128)(2,1)S(1)}, bf16[512,128]{1,0:T(8,128)(2,1)S(1)}, u32[]{:S(2)}, u32[]{:S(2)}) collective-permute-start(bf16[512,128]{1,0:T(8,128)(2,1)S(1)} %get-tuple-element.189), channel_id=1, source_target_pairs={{0,16},{4,20},{8,24},{12,28},{16,0},{20,4},{24,8},{28,12},{1,17},{... | collective-permute-start | bytes 393224 | tf_op jit(solution)/shard_map/ppermute | solution.py:631
  54.4 9.1 %collective-permute-start.20 = (bf16[512,128]{1,0:T(8,128)(2,1)S(1)}, bf16[512,128]{1,0:T(8,128)(2,1)S(1)}, u32[]{:S(2)}, u32[]{:S(2)}) collective-permute-start(bf16[512,128]{1,0:T(8,128)(2,1)S(1)} %get-tuple-element.190), channel_id=1, source_target_pairs={{0,24},{4,28},{8,16},{12,20},{16,8},{20,12},{24,0},{28,4},{1,25},{... | collective-permute-start | bytes 393224 | tf_op jit(solution)/shard_map/ppermute | solution.py:631
  54.6 11.6 %collective-permute-start.6 = (bf16[128,512]{1,0:T(8,128)(2,1)S(1)}, bf16[128,512]{1,0:T(8,128)(2,1)S(1)}, u32[]{:S(2)}, u32[]{:S(2)}) collective-permute-start(bf16[128,512]{1,0:T(8,128)(2,1)S(1)} %get-tuple-element.146.to_other_ref), channel_id=1, source_target_pairs={{1,2},{2,1},{5,6},{6,5},{9,10},{10,9},{13,14},{14,13},{17,18},{18,... | collective-permute-start | bytes 393224 | tf_op jit(solution)/shard_map/ppermute | solution.py:639
  55.3 12.5 %collective-permute-start.7 = (bf16[128,512]{1,0:T(8,128)(2,1)S(1)}, bf16[128,512]{1,0:T(8,128)(2,1)S(1)}, u32[]{:S(2)}, u32[]{:S(2)}) collective-permute-start(bf16[128,512]{1,0:T(8,128)(2,1)S(1)} %get-tuple-element.147.to_pair_ref), channel_id=1, source_target_pairs={{0,1},{1,0},{2,3},{3,2},{4,5},{5,4},{6,7},{7,6},{8,9},{9,8},{10,11... | collective-permute-start | bytes 393224 | tf_op jit(solution)/shard_map/ppermute | solution.py:631
  58.5 13.7 %collective-permute-start.23 = (bf16[288,128]{1,0:T(8,128)(2,1)S(1)}, bf16[288,128]{1,0:T(8,128)(2,1)S(1)}, u32[]{:S(2)}, u32[]{:S(2)}) collective-permute-start(bf16[288,128]{1,0:T(8,128)(2,1)S(1)} %get-tuple-element.194), channel_id=1, source_target_pairs={{0,8},{4,12},{8,0},{12,4},{16,24},{20,28},{24,16},{28,20},{1,9},{5... | collective-permute-start | bytes 221192 | tf_op jit(solution)/shard_map/ppermute | solution.py:631
  63.4 8.8 %collective-permute-start.24 = (bf16[288,128]{1,0:T(8,128)(2,1)S(1)}, bf16[288,128]{1,0:T(8,128)(2,1)S(1)}, u32[]{:S(2)}, u32[]{:S(2)}) collective-permute-start(bf16[288,128]{1,0:T(8,128)(2,1)S(1)} %get-tuple-element.195), channel_id=1, source_target_pairs={{0,16},{4,20},{8,24},{12,28},{16,0},{20,4},{24,8},{28,12},{1,17},{... | collective-permute-start | bytes 221192 | tf_op jit(solution)/shard_map/ppermute | solution.py:631
  63.4 8.8 %collective-permute-start.25 = (bf16[288,128]{1,0:T(8,128)(2,1)S(1)}, bf16[288,128]{1,0:T(8,128)(2,1)S(1)}, u32[]{:S(2)}, u32[]{:S(2)}) collective-permute-start(bf16[288,128]{1,0:T(8,128)(2,1)S(1)} %get-tuple-element.196), channel_id=1, source_target_pairs={{0,24},{4,28},{8,16},{12,20},{16,8},{20,12},{24,0},{28,4},{1,25},{... | collective-permute-start | bytes 221192 | tf_op jit(solution)/shard_map/ppermute | solution.py:631
  66.2 6.1 %collective-permute-start.21 = (bf16[128,128]{1,0:T(8,128)(2,1)S(1)}, bf16[128,128]{1,0:T(8,128)(2,1)S(1)}, u32[]{:S(2)}, u32[]{:S(2)}) collective-permute-start(bf16[128,128]{1,0:T(8,128)(2,1)S(1)} %get-tuple-element.192), channel_id=1, source_target_pairs={{0,4},{4,0},{8,12},{12,8},{16,20},{20,16},{24,28},{28,24},{1,5},{5... | collective-permute-start | bytes 98312 | tf_op jit(solution)/shard_map/ppermute | solution.py:631
  67.8 5.3 %collective-permute-start.22 = (bf16[128,128]{1,0:T(8,128)(2,1)S(1)}, bf16[128,128]{1,0:T(8,128)(2,1)S(1)}, u32[]{:S(2)}, u32[]{:S(2)}) collective-permute-start(bf16[128,128]{1,0:T(8,128)(2,1)S(1)} %get-tuple-element.193), channel_id=1, source_target_pairs={{0,2},{1,3},{2,0},{3,1},{4,6},{5,7},{6,4},{7,5},{8,10},{9,11},{10,... | collective-permute-start | bytes 98312 | tf_op jit(solution)/shard_map/ppermute | solution.py:631
